TPU v7x, 256 devices: a whole 4x4x8 slice. The times are simulated.
256 devices in a mesh: ctx: 32 (over z, x), head: 8 (over y, core).
Axes of the slice: x: 4, y: 4, z: 8, core: 2. Of those that a mesh axis runs over, the one named last changes fastest.
Arguments:
- x_raw: bfloat16 [8192, 8192], P('ctx', 'head'), may hold values from -6 to 6
- bc_raw: bfloat16 [8192, 256], P('ctx'), may hold values from -6 to 6
- conv_x_w: bfloat16 [4, 8192], P(None, 'head'), may hold values from -3 to 3
- conv_bc_w: bfloat16 [4, 256], replicated, may hold values from -3 to 3
- dt_raw: float32 [128, 8192], P('head', 'ctx'), may hold values from -7 to 0
- a_log: float32 [128], P('head'), may hold values from -10 to 1
- d_skip: float32 [128], P('head'), may hold values from 0.5 to 1.5
- doc_starts: int32 [32], P('ctx'), may hold values from 0 to 256, as said below
- grad_y: bfloat16 [8192, 8192], P('ctx', 'head'), may hold values from -6 to 6
Outputs:
- y_out: bfloat16 [8192, 8192], P('ctx', 'head')
- grad_x_raw: bfloat16 [8192, 8192], P('ctx', 'head')
- grad_bc_raw: bfloat16 [8192, 256], P('ctx')
- grad_dt_raw: float32 [128, 8192], P('head', 'ctx')
Inputs may be any that keep to these rules, and one draw needn't show every extreme that they name: Block b holds a document start at row 256 * b + doc_starts[b] when doc_starts[b] < 256, and none when doc_starts[b] = 256; doc_starts[0] = 0.
All inputs are finite; a program needn't handle non-finite values.
Results may differ from a plain program's by a relative error of at most 0.013.
Values may be sent and summed in bfloat16 or wider, within the bound.
No kernel may reach another device: no remote copies, remote signals or barrier semaphores. Data moves between devices by JAX's collectives and lax.ppermute only.
A program may use at most 128 MiB of HBM per device.

v0:
```python
import jax
import jax.numpy as jnp
from jax import lax
from jax.sharding import PartitionSpec as P


def shifted(x, axis, by):
    size = lax.axis_size(axis)
    pairs = [(i, i + by) for i in range(size) if 0 <= i + by < size]
    return lax.ppermute(x, axis, pairs)


def entering_2(value, axis, join, neutral, backward):
    count, mine = (lax.axis_size(axis), lax.axis_index(axis))
    pieces = jax.tree.map(lambda part: lax.all_gather(part, axis), value)
    if backward:
        pieces = jax.tree.map(lambda part: part[::-1], pieces)
        mine = count - 1 - mine
    so_far = jax.tree.map(
        lambda part, zero: jnp.full_like(part, 0) + jnp.asarray(zero, part.dtype), value, neutral
    )

    def step(position, so_far):
        longer = join(so_far, jax.tree.map(lambda part: part[position], pieces))
        return jax.tree.map(lambda new, old: jnp.where(position < mine, new, old), longer, so_far)

    return lax.fori_loop(0, count - 1, step, so_far)


def contract(pattern, first_op, second_op):
    return jnp.einsum(pattern, first_op, second_op, preferred_element_type=jnp.float32)


def contract_exact(pattern, first_op, second_op):
    return jnp.einsum(
        pattern,
        first_op.astype(jnp.float32),
        second_op.astype(jnp.float32),
        precision=lax.Precision.HIGHEST,
    )


def silu_grad(values):
    sigmoid_v = jax.nn.sigmoid(values)
    return sigmoid_v * (1.0 + values * (1.0 - sigmoid_v))


def causal_conv(tok_rows, before, weight):
    row_count = tok_rows.shape[0]
    tap_count = weight.shape[0]
    padded = jnp.concatenate([before, tok_rows], axis=0).astype(jnp.float32)
    weight_f = weight.astype(jnp.float32)
    running = jnp.zeros(tok_rows.shape, jnp.float32)
    for offset in range(tap_count):
        running = running + weight_f[offset] * padded[offset : offset + row_count]
    return running


def conv_back(gradient, following, weight):
    row_count = gradient.shape[0]
    tap_count = weight.shape[0]
    padded = jnp.concatenate([gradient, following], axis=0)
    weight_f = weight.astype(jnp.float32)
    running = jnp.zeros(gradient.shape, jnp.float32)
    for offset in range(tap_count):
        running = running + weight_f[tap_count - 1 - offset] * padded[offset : offset + row_count]
    return running


def block_prep(x_block, bc_block, step_block, decay_rate, reset_at):
    block_len = step_block.shape[1]
    nstate = bc_block.shape[1] // 2
    position = jnp.arange(block_len, dtype=jnp.int32)
    segment = position >= reset_at
    cumulated = jnp.cumsum(-decay_rate[:, None] * step_block, axis=1)
    causal = (segment[:, None] == segment[None, :]) & (position[:, None] >= position[None, :])
    kernel = jnp.exp(
        jnp.where(causal[None], cumulated[:, :, None] - cumulated[:, None, :], -jnp.inf)
    )
    entering = jnp.where(segment[None, :], 0.0, jnp.exp(cumulated))
    final_cum = cumulated[:, block_len - 1 :]
    leaving = jnp.where(
        segment[None, :] == segment[block_len - 1], jnp.exp(final_cum - cumulated), 0.0
    )
    carry_out = jnp.where(reset_at >= block_len, jnp.exp(cumulated[:, block_len - 1]), 0.0)
    b_matrix = bc_block[:, :nstate]
    c_matrix = bc_block[:, nstate:]
    gram_mat = contract("tn,sn->ts", c_matrix, b_matrix)
    mixing = (gram_mat[None] * kernel).astype(jnp.bfloat16)
    x_float = x_block.astype(jnp.float32)
    scaled_x = (x_float * jnp.transpose(step_block)[:, :, None]).astype(jnp.bfloat16)
    leaving_x = (x_float * jnp.transpose(leaving * step_block)[:, :, None]).astype(jnp.bfloat16)
    return dict(
        kernel=kernel,
        entering=entering,
        leaving=leaving,
        carry_out=carry_out,
        b_matrix=b_matrix,
        c_matrix=c_matrix,
        gram_mat=gram_mat,
        mixing=mixing,
        scaled_x=scaled_x,
        leaving_x=leaving_x,
    )


def block_state(prepared):
    return contract("shp,sn->hpn", prepared["leaving_x"], prepared["b_matrix"])


def block_out(prepared, x_block, d_skip, state_in):
    state_q = state_in.astype(jnp.bfloat16)
    intra = contract("hts,shp->thp", prepared["mixing"], prepared["scaled_x"])
    y_state = contract("tn,hpn->thp", prepared["c_matrix"], state_q)
    result = (
        intra
        + jnp.transpose(prepared["entering"])[:, :, None] * y_state
        + d_skip[None, :, None] * x_block.astype(jnp.float32)
    )
    return (result.astype(jnp.bfloat16), y_state)


def block_bsum(prepared, output_grad_block):
    enter_dy = (
        output_grad_block.astype(jnp.float32) * jnp.transpose(prepared["entering"])[:, :, None]
    ).astype(jnp.bfloat16)
    return (enter_dy, contract("thp,tn->hpn", enter_dy, prepared["c_matrix"]))


def block_back(
    prepared,
    x_block,
    output_grad_block,
    enter_dy,
    y_state,
    state_in,
    dstate,
    decay_rate,
    d_skip,
    step_block,
):
    block_len = step_block.shape[1]
    kernel = prepared["kernel"]
    dstate_q = dstate.astype(jnp.bfloat16)
    state_q = state_in.astype(jnp.bfloat16)
    response = contract("thp,shp->hts", output_grad_block, prepared["scaled_x"])
    weighed = response * kernel
    z_term = weighed * prepared["gram_mat"][None]
    d_gram = jnp.sum(weighed, axis=0)
    grad_c = contract_exact("ts,sn->tn", d_gram, prepared["b_matrix"]) + contract(
        "thp,hpn->tn", enter_dy, state_q
    )
    grad_b = contract_exact("ts,tn->sn", d_gram, prepared["c_matrix"]) + contract(
        "shp,hpn->sn", prepared["leaving_x"], dstate_q
    )
    d_scaled = contract("hts,thp->shp", prepared["mixing"], output_grad_block)
    d_leaving = contract("sn,hpn->shp", prepared["b_matrix"], dstate_q)
    x_float = x_block.astype(jnp.float32)
    step_t = jnp.transpose(step_block)
    leave_t = jnp.transpose(prepared["leaving"])
    grad_xc = (
        step_t[:, :, None] * d_scaled
        + (leave_t * step_t)[:, :, None] * d_leaving
        + d_skip[None, :, None] * output_grad_block.astype(jnp.float32)
    )
    along_dt = jnp.transpose(jnp.sum(x_float * d_scaled, axis=2))
    along_leave = jnp.transpose(jnp.sum(x_float * d_leaving, axis=2))
    leave_term = prepared["leaving"] * step_block * along_leave
    enter_term = prepared["entering"] * jnp.transpose(
        jnp.sum(output_grad_block.astype(jnp.float32) * y_state, axis=2)
    )
    final_term = jnp.sum(leave_term, axis=1) + prepared["carry_out"] * jnp.sum(
        dstate * state_in, axis=(1, 2)
    )
    is_final = jnp.arange(block_len, dtype=jnp.int32) == block_len - 1
    d_cum = jnp.sum(z_term, axis=2) - jnp.sum(z_term, axis=1) + enter_term - leave_term
    d_cum = d_cum + jnp.where(is_final[None, :], final_term[:, None], 0.0)
    d_log = lax.cumsum(d_cum, axis=1, reverse=True)
    grad_step = along_dt + prepared["leaving"] * along_leave - decay_rate[:, None] * d_log
    return (grad_b, grad_c, grad_xc, grad_step)


def compose(earlier, later):
    return (earlier[0] * later[0], later[0][:, None, None] * earlier[1] + later[1])


def body(x_raw, bc_raw, conv_x_w, conv_bc_w, dt_raw, a_log, d_skip, doc_starts, grad_y):
    tok_rows, channels = x_raw.shape
    head_count = a_log.shape[0]
    head_dim = channels // head_count
    nstate = bc_raw.shape[1] // 2
    rim_rows = conv_x_w.shape[0] - 1
    nblock = doc_starts.shape[0]
    block_len = tok_rows // nblock
    prev_x, prev_bc = shifted(
        (x_raw[tok_rows - rim_rows :], bc_raw[tok_rows - rim_rows :]), "ctx", 1
    )
    x_pre = causal_conv(x_raw, prev_x, conv_x_w)
    bc_pre = causal_conv(bc_raw, prev_bc, conv_bc_w)
    x_conv = jax.nn.silu(x_pre).astype(jnp.bfloat16)
    bc_conv = jax.nn.silu(bc_pre).astype(jnp.bfloat16)
    step_size = jax.nn.softplus(dt_raw)
    decay_rate = jnp.exp(a_log)
    block_id = 0
    x_block = x_conv.reshape(block_len, head_count, head_dim)
    preps = [block_prep(x_block, bc_conv, step_size, decay_rate, doc_starts[block_id])]
    x_blocks = [x_block]
    step_blocks = [step_size]
    dy_blocks = [grad_y.reshape(block_len, head_count, head_dim)]
    state_shape = (head_count, head_dim, nstate)
    identity = (jnp.ones((head_count,), jnp.float32), jnp.zeros(state_shape, jnp.float32))
    block_sums = [block_state(prepared) for prepared in preps]
    dev_carry = jnp.ones((head_count,), jnp.float32)
    dev_state = jnp.zeros(state_shape, jnp.float32)
    block_id = 0
    dev_state = preps[block_id]["carry_out"][:, None, None] * dev_state + block_sums[block_id]
    dev_carry = dev_carry * preps[block_id]["carry_out"]
    chained = entering_2((dev_carry, dev_state), "ctx", compose, identity, False)
    state_in = chained[1]
    block_id = 0
    states = [state_in]
    y_block, y_state = block_out(preps[block_id], x_blocks[block_id], d_skip, state_in)
    y_parts = y_block.reshape(block_len, channels)
    y_states = [y_state]
    block_id = 0
    enter_dy, back_part = block_bsum(preps[block_id], dy_blocks[block_id])
    enter_list = [enter_dy]
    back_list = [back_part]
    dev_grad = jnp.zeros(state_shape, jnp.float32)
    for block_id in reversed(range(nblock)):
        dev_grad = preps[block_id]["carry_out"][:, None, None] * dev_grad + back_list[block_id]
    chained_back = entering_2((dev_carry, dev_grad), "ctx", compose, identity, True)
    dstate = chained_back[1]
    dstates = [dstate] * nblock
    for block_id in reversed(range(nblock)):
        dstates[block_id] = dstate
        dstate = preps[block_id]["carry_out"][:, None, None] * dstate + back_list[block_id]
    block_id = 0
    grad_b, grad_c, grad_xc, grad_step = block_back(
        preps[block_id],
        x_blocks[block_id],
        dy_blocks[block_id],
        enter_list[block_id],
        y_states[block_id],
        states[block_id],
        dstates[block_id],
        decay_rate,
        d_skip,
        step_blocks[block_id],
    )
    grad_b_list = [grad_b]
    grad_c_list = [grad_c]
    grad_xc_list = grad_xc.reshape(block_len, channels)
    grad_step_list = [grad_step]
    grad_bc = jnp.concatenate(
        [jnp.concatenate(grad_b_list, axis=0), jnp.concatenate(grad_c_list, axis=0)], axis=1
    )
    grad_bc_pre = lax.psum(grad_bc, "head") * silu_grad(bc_pre)
    grad_x_pre = grad_xc_list * silu_grad(x_pre)
    next_x, next_bc = shifted((grad_x_pre[:rim_rows], grad_bc_pre[:rim_rows]), "ctx", -1)
    grad_x_raw = conv_back(grad_x_pre, next_x, conv_x_w).astype(jnp.bfloat16)
    grad_bc_part = conv_back(grad_bc_pre, next_bc, conv_bc_w).astype(jnp.bfloat16)
    grad_dt_raw = jnp.concatenate(grad_step_list, axis=1) * jax.nn.sigmoid(dt_raw)
    return (y_parts, grad_x_raw, grad_bc_part, grad_dt_raw)


def solution(mesh):
    in_specs = (
        P("ctx", "head"),
        P("ctx", None),
        P(None, "head"),
        P(),
        P("head", "ctx"),
        P("head"),
        P("head"),
        P("ctx"),
        P("ctx", "head"),
    )
    out_specs = (P("ctx", "head"), P("ctx", "head"), P("ctx", None), P("head", "ctx"))
    return jax.shard_map(body, mesh=mesh, in_specs=in_specs, out_specs=out_specs, check_vma=False)
```

profile of v0, /device:TPU:7, one launch (start us, length us, event | category | flops | bytes accessed | tf_op | source)
XLA Modules:
  0.0 480.1 jit_solution(10345392737826385530)
XLA Ops:
  7.9 3.4 collective-permute-start.1
  11.4 1.2 fusion.93
  16.6 1.2 copy.78
  21.6 3.1 collective-permute-start
  26.8 55.0 %all-reduce = f32[512]{0:T(512)S(1)} all-reduce(f32[512]{0:T(512)S(1)} %dynamic-update-slice), channel_id=2, replica_groups=mesh['ctx'=32,'head'=8] {'ctx'}, use_global_device_ids=true, to_apply=%add | all-reduce | flops 512 | bytes 4096
  84.7 1.2 maximum_convert_fusion
  86.0 76.1 %all-gather.8.cloned.1.call-done = f32[512,64,128]{2,1,0:T(8,128)} async-done(((f32[16,64,128]{2,1,0:T(8,128)}), f32[512,64,128]{2,1,0:T(8,128)}) %all-gather.8.cloned.1.call-update) | async-done | bytes 16777232 | tf_op jit(solution)/shard_map/all_gather | solution.py:15
  162.1 11.8 %rev.7 = f32[32,16,64,128]{3,2,1,0:T(8,128)} reverse(f32[32,16,64,128]{3,2,1,0:T(8,128)} %bitcast.172), dimensions={0} | reverse | bytes 33554432 | tf_op jit(solution)/shard_map/rev | solution.py:17
  173.8 37.6 %while.29 = (s32[]{:T(128)}, f32[16,64,128]{2,1,0:T(8,128)S(1)}, s32[]{:T(128)}, f32[32,16]{1,0:T(8,128)S(1)}, f32[32,16,64,128]{3,2,1,0:T(8,128)}, /*index=5*/s32[]{:T(128)}, s32[]{:T(128)}) while((s32[]{:T(128)}, f32[16,64,128]{2,1,0:T(8,128)S(1)}, s32[]{:T(128)}, f32[32,16]{1,0:T(8,128)S(1)}, f32[32,16,64,128]{3,2,1,0:T(8,128)}, ...), condition=%wide.region_5.6_spmd.clone, body=%wide.region_4.5_spmd.clone.sunk | while | flops 524292 | bytes 1573161 | solution.py:27
  173.9 1.2 fusion.102
  175.1 1.2 fusion.102
  176.3 1.2 fusion.102
  177.5 1.2 fusion.102
  178.7 1.2 fusion.102
  179.9 1.2 fusion.102
  181.1 1.2 fusion.102
  183.6 1.2 fusion.102
  184.8 1.2 fusion.102
  186.0 1.2 fusion.102
  187.2 1.2 fusion.102
  189.6 1.2 fusion.102
  192.1 1.2 fusion.102
  194.5 1.2 fusion.102
  196.9 1.2 fusion.102
  199.4 1.2 fusion.102
  201.8 1.2 fusion.102
  204.2 1.2 fusion.102
  206.6 1.2 fusion.102
  207.9 1.2 fusion.102
  209.1 1.2 fusion.102
  210.3 1.2 fusion.102
  211.5 1.7 fusion.29
  213.2 2.6 copy.80
  215.7 3.0 multiply_multiply_fusion
  218.7 1.3 fusion.36
  220.0 1.6 copy.73
  221.6 1.6 multiply_reduce_fusion.3
  225.3 2.8 collective-permute-start.2
  228.5 3.5 multiply_reduce_fusion
  232.4 4.0 fusion.24
  236.3 125.8 %all-gather.6.cloned.1.call-done = f32[512,64,128]{2,1,0:T(8,128)} async-done(((f32[16,64,128]{2,1,0:T(8,128)}), f32[512,64,128]{2,1,0:T(8,128)}) %all-gather.6.cloned.1.call-update) | async-done | bytes 16777232 | tf_op jit(solution)/shard_map/all_gather | solution.py:15
  362.2 37.6 %while.28 = (s32[]{:T(128)}, f32[16,64,128]{2,1,0:T(8,128)S(1)}, s32[]{:T(128)}, f32[32,16]{1,0:T(8,128)S(1)}, f32[32,16,64,128]{3,2,1,0:T(8,128)}, /*index=5*/s32[]{:T(128)}, s32[]{:T(128)}) while((s32[]{:T(128)}, f32[16,64,128]{2,1,0:T(8,128)S(1)}, s32[]{:T(128)}, f32[32,16]{1,0:T(8,128)S(1)}, f32[32,16,64,128]{3,2,1,0:T(8,128)}, ...), condition=%wide.region_3.4_spmd.clone, body=%wide.region_2.3_spmd.clone.sunk | while | flops 524292 | bytes 1573161 | solution.py:27
  365.8 1.2 fusion.101
  367.0 1.2 fusion.101
  370.7 1.2 fusion.101
  371.9 1.2 fusion.101
  373.1 1.2 fusion.101
  376.8 1.2 fusion.101
  378.0 1.2 fusion.101
  379.2 1.2 fusion.101
  382.8 1.2 fusion.101
  384.0 1.2 fusion.101
  385.3 1.2 fusion.101
  388.9 1.2 fusion.101
  390.1 1.2 fusion.101
  393.7 1.2 fusion.101
  395.0 1.2 fusion.101
  396.2 1.2 fusion.101
  400.0 1.3 fusion.30
  402.9 2.5 fusion.19
  405.7 2.5 reduce-window.16
  408.4 56.9 %all-reduce.3.cloned.1.call-done = f32[256,256]{1,0:T(8,128)} async-done(((f32[256,256]{1,0:T(8,128)}), f32[256,256]{1,0:T(8,128)}) %all-reduce.3.cloned.1.call-update) | async-done | bytes 262160 | tf_op jit(solution)/shard_map/psum | solution.py:258
  466.3 2.5 collective-permute-start.3
  470.5 2.3 collective-permute-done.3
  (191 shorter events, 49.2 us)
Async XLA Ops:
  7.2 18.2 %copy-start.21 = (u32[256]{0:T(256)S(1)}, u32[256]{0:T(256)}, u32[]{:S(2)}) copy-start(u32[256]{0:T(256)} %constant.81) | copy-start | bytes 3076
  7.2 76.0 %copy-start.1 = (f32[16,256]{1,0:T(8,128)S(1)}, f32[16,256]{1,0:T(8,128)}, u32[]{:S(2)}) copy-start(f32[16,256]{1,0:T(8,128)} %param.17) | copy-start | bytes 49156
  7.2 75.4 %copy-start.3 = (bf16[4,1024]{1,0:T(4,128)(2,1)S(1)}, bf16[4,1024]{1,0:T(4,128)(2,1)}, u32[]{:S(2)}) copy-start(bf16[4,1024]{1,0:T(4,128)(2,1)} %param.15) | copy-start | bytes 24580
  7.2 154.9 %all-gather.8.cloned.1.call-start = ((), (), s32[]{:S(2)}) async-start(), calls=%async_computation.2 | async-start | bytes 17301504 | tf_op jit(solution)/shard_map/all_gather | solution.py:15
  7.9 9.9 %collective-permute-start.1 = (bf16[3,256]{1,0:T(4,128)(2,1)S(1)}, bf16[3,256]{1,0:T(4,128)(2,1)S(1)}, u32[]{:S(2)}, u32[]{:S(2)}) collective-permute-start(bf16[3,256]{1,0:T(4,128)(2,1)S(1)} %slice.121), channel_id=1, source_target_pairs={{0,8},{8,16},{16,24},{24,32},{32,40},{40,48},{48,56},{56,64},{64,7... | collective-permute-start | bytes 4616 | tf_op jit(solution)/shard_map/ppermute | solution.py:10
  15.5 69.2 %copy-start.10 = (pred[256]{0:T(512)(128)(4,1)}, pred[256]{0:T(512)(128)(4,1)S(1)}, u32[]{:S(2)}) copy-start(pred[256]{0:T(512)(128)(4,1)S(1)} %get-tuple-element.296) | copy-start | bytes 772
  16.4 68.3 %copy-start.6 = (f32[1,256]{1,0:T(1,128)}, f32[1,256]{1,0:T(1,128)S(1)}, u32[]{:S(2)}) copy-start(f32[1,256]{1,0:T(1,128)S(1)} %get-tuple-element.287) | copy-start | bytes 3076
  16.4 68.3 %copy-start.8 = (f32[1,256]{1,0:T(1,128)}, f32[1,256]{1,0:T(1,128)S(1)}, u32[]{:S(2)}) copy-start(f32[1,256]{1,0:T(1,128)S(1)} %get-tuple-element.288) | copy-start | bytes 3076
  16.6 4.2 copy-start.15
  20.8 341.4 %all-gather.6.cloned.1.call-start = ((), (), s32[]{:S(2)}) async-start(), calls=%async_computation.1 | async-start | bytes 17301504 | tf_op jit(solution)/shard_map/all_gather | solution.py:15
  21.6 63.1 %collective-permute-start = (bf16[3,1024]{1,0:T(4,128)(2,1)S(1)}, bf16[3,1024]{1,0:T(4,128)(2,1)}, u32[]{:S(2)}, u32[]{:S(2)}) collective-permute-start(bf16[3,1024]{1,0:T(4,128)(2,1)S(1)} %slice.112), channel_id=1, source_target_pairs={{0,8},{8,16},{16,24},{24,32},{32,40},{40,48},{48,56},{56,64},{64,7... | collective-permute-start | bytes 18440 | tf_op jit(solution)/shard_map/ppermute | solution.py:10
  82.6 0.6 copy-start.12
  83.6 1.1 copy-start.2
  173.8 37.6 %copy-start.17 = (f32[16]{0:T(128)S(1)}, f32[16]{0:T(128)}, u32[]{:S(2)}) copy-start(f32[16]{0:T(128)} %param.19) | copy-start | bytes 196
  218.7 4.5 copy-start.13
  218.7 4.7 copy-start.16
  224.5 240.7 %all-reduce.3.cloned.1.call-start = ((), (), s32[]{:S(2)}) async-start(), calls=%async_computation | async-start | bytes 524288 | tf_op jit(solution)/shard_map/psum | solution.py:258
  225.3 7.0 %collective-permute-start.2 = (f32[3,1024]{1,0:T(4,128)S(1)}, f32[3,1024]{1,0:T(4,128)S(1)}, u32[]{:S(2)}, u32[]{:S(2)}) collective-permute-start(f32[3,1024]{1,0:T(4,128)S(1)} %slice.165), channel_id=1, source_target_pairs={{8,0},{16,8},{24,16},{32,24},{40,32},{48,40},{56,48},{64,56},{72,6... | collective-permute-start | bytes 36872 | tf_op jit(solution)/shard_map/ppermute | solution.py:10
  399.8 3.1 copy-start.18
  401.7 3.9 copy-start.4
  401.7 3.9 copy-start.5
  401.7 3.9 copy-start.11
  401.7 3.9 copy-start.14
  401.7 3.9 copy-start.20
  402.1 63.1 %copy-start = (f32[256,256]{1,0:T(8,128)S(1)}, f32[256,256]{1,0:T(8,128)}, u32[]{:S(2)}) copy-start(f32[256,256]{1,0:T(8,128)} %get-tuple-element.276) | copy-start | bytes 786436
  402.9 66.0 %copy-start.19 = (f32[16]{0:T(128)S(1)}, f32[16]{0:T(128)}, u32[]{:S(2)}) copy-start(f32[16]{0:T(128)} %get-tuple-element.289) | copy-start | bytes 196
  402.9 69.9 %copy-start.7 = (f32[1,256]{1,0:T(1,128)S(1)}, f32[1,256]{1,0:T(1,128)}, u32[]{:S(2)}) copy-start(f32[1,256]{1,0:T(1,128)} %copy-done.6) | copy-start | bytes 3076
  402.9 69.9 %copy-start.9 = (f32[1,256]{1,0:T(1,128)S(1)}, f32[1,256]{1,0:T(1,128)}, u32[]{:S(2)}) copy-start(f32[1,256]{1,0:T(1,128)} %copy-done.8) | copy-start | bytes 3076
  466.3 6.5 %collective-permute-start.3 = (f32[3,256]{1,0:T(4,128)S(1)}, f32[3,256]{1,0:T(4,128)S(1)}, u32[]{:S(2)}, u32[]{:S(2)}) collective-permute-start(f32[3,256]{1,0:T(4,128)S(1)} %slice.170), channel_id=1, source_target_pairs={{8,0},{16,8},{24,16},{32,24},{40,32},{48,40},{56,48},{64,56},{72,6... | collective-permute-start | bytes 9224 | tf_op jit(solution)/shard_map/ppermute | solution.py:10
Sparse Core Ops, SparseCore 0:
  20.9 141.0 all-gather.7
  224.6 137.4 all-gather.5
  403.0 62.2 all-reduce.2
where the time goes:
time: 487 us; the launch traced here: 480 us
  waiting for transfers between devices  261 us (54%)
  other arithmetic  96.4 us (20%)
  blocking collectives  55 us (11%)
  local copies, waits for them, and re-layouts  24.3 us (5%)
  between operations  15.5 us (3%)
  matrix products  13.8 us (3%)
  starting transfers between devices  11.9 us (2%)
    all_gather x2, waiting for transfers between devices, entering_2(): pieces = jax.tree.map(lambda part: lax.all_gather(part, axis), value)  202 us
    select_n x62, other arithmetic, step(): jnp.where(position < mine, new, old)  72.7 us
    psum x1, waiting for transfers between devices, body(): grad_bc_pre = lax.psum(grad_bc, 'head') * silu_grad(bc_pre)  56.9 us
    unnamed x1, blocking collectives  55 us
    dot_general x10, matrix products, contract(): jnp.einsum(pattern, first_op, second_op, preferred_element_type=jnp.float32)  13.1 us
    ppermute x4, starting transfers between devices, shifted(): return lax.ppermute(x, axis, pairs)  11.8 us
    rev x2, local copies, waits for them, and re-layouts, entering_2(): pieces = jax.tree.map(lambda part: part[::-1], pieces)  11.8 us
  transfers between devices with their start and end apart: 7, of which 4 were waited for; matrix products, arithmetic and copies ran while one was open for 6% of the time, Pallas kernels for 0%

commit v1 on v0

v1 whole, which is shorter than its diff:
```python
import functools

import jax
import jax.numpy as jnp
from jax import lax
from jax.experimental import pallas as pl
from jax.experimental.pallas import tpu as pltpu
from jax.sharding import PartitionSpec as P

F32 = jnp.float32
BF16 = jnp.bfloat16
LANES = 128
RIM = 8
VMEM_LIMIT = 48 * 1024 * 1024
HIGHEST = lax.Precision.HIGHEST


def dot(a, b, dims, precision=None):
    return lax.dot_general(a, b, (dims, ((), ())), precision=precision, preferred_element_type=F32)


def iota(shape, axis):
    return lax.broadcasted_iota(jnp.int32, shape, axis)


def halves(values):
    high = values.astype(BF16)
    return high, (values - high.astype(F32)).astype(BF16)


def sigmoid(values):
    return 1.0 / (1.0 + jnp.exp(-values))


def spread(values, slab, head_dim):
    heads = values.shape[0]
    high, low = halves(values)
    both = jnp.concatenate([high, low], axis=0)
    row = iota((2 * heads, LANES), 0)
    head = iota((2 * heads, LANES), 1) // head_dim + slab * (LANES // head_dim)
    chosen = jnp.where((row == head) | (row == head + heads), 1.0, 0.0).astype(BF16)
    return dot(both, chosen, ((0,), (0,)))


def head_sum(values, slab, head_dim, heads):
    high, low = halves(values)
    both = jnp.concatenate([high, low], axis=1)
    head = (iota((heads, 2 * LANES), 1) % LANES) // head_dim + slab * (LANES // head_dim)
    chosen = jnp.where(iota((heads, 2 * LANES), 0) == head, 1.0, 0.0).astype(BF16)
    return dot(chosen, both, ((1,), (1,)))


def per_head(ref, heads, rows):
    at = iota((heads, rows), 0)
    values = jnp.zeros((heads, rows), F32)
    for head in range(heads):
        values = jnp.where(at == head, ref[head], values)
    return values


def head_values(doc_ref, a_log_ref, dt_ref):
    heads, rows = dt_ref.shape
    doc = doc_ref[0]
    raw = dt_ref[...]
    step = jnp.maximum(raw, 0.0) + jnp.log(1.0 + jnp.exp(-jnp.abs(raw)))
    decay = jnp.exp(per_head(a_log_ref, heads, rows))
    upto = jnp.where(iota((rows, rows), 0) <= iota((rows, rows), 1), 1.0, 0.0)
    drop = -decay * step
    cum = dot(drop, upto, ((1,), (0,)), HIGHEST)
    final = cum[:, rows - 1 :]
    segment = iota((heads, rows), 1) >= doc
    entering = jnp.where(segment, 0.0, jnp.exp(cum))
    outside = jnp.logical_and(iota((heads, rows), 1) < doc, doc < rows)
    leaving = jnp.where(outside, 0.0, jnp.exp(final - cum))
    carry = jnp.where(doc >= rows, jnp.exp(jnp.broadcast_to(final, (heads, rows))), 0.0)
    return dict(
        step=step, decay=decay, drop=drop, cum=cum, entering=entering, leaving=leaving, carry=carry
    )


def load_ext(ext, halo_ref, x_ref, bc_ref):
    channels = x_ref.shape[1]
    rows = x_ref.shape[0]
    ext[0:RIM, :] = halo_ref[...].astype(F32)
    ext[RIM : RIM + rows, 0:channels] = x_ref[...].astype(F32)
    ext[RIM : RIM + rows, channels:] = bc_ref[...].astype(F32)


def filtered(ext, w_ref, at, w_at, rows):
    taps = w_ref.shape[0]
    lanes = pl.ds(at, LANES)
    w = w_ref[:, w_at : w_at + LANES].astype(F32)
    total = w[0:1] * ext[pl.ds(RIM - taps + 1, rows), lanes]
    for tap in range(1, taps):
        total = total + w[tap : tap + 1] * ext[pl.ds(RIM - taps + 1 + tap, rows), lanes]
    return total


def send_kernel(
    head_dim, doc_ref, a_log_ref, x_ref, halo_ref, bc_ref, wx_ref, wbc_ref, dt_ref, dy_ref, send_ref, ext
):
    rows, channels = x_ref.shape
    heads = dt_ref.shape[0]
    part = channels // send_ref.shape[0]
    per_slab = LANES // part
    v = head_values(doc_ref, a_log_ref, dt_ref)
    load_ext(ext, halo_ref, x_ref, bc_ref)
    bc = []
    for half in range(2):
        pre = filtered(ext, wbc_ref, channels + half * LANES, half * LANES, rows)
        bc.append((pre * sigmoid(pre)).astype(BF16))
    leave_step = v["leaving"] * v["step"]
    for slab in range(channels // LANES):
        lanes = slice(slab * LANES, (slab + 1) * LANES)
        pre = filtered(ext, wx_ref, slab * LANES, slab * LANES, rows)
        x_conv = (pre * sigmoid(pre)).astype(BF16).astype(F32)
        leaving_x = (x_conv * spread(leave_step, slab, head_dim)).astype(BF16)
        enter_dy = (dy_ref[:, lanes].astype(F32) * spread(v["entering"], slab, head_dim)).astype(BF16)
        forward = dot(leaving_x, bc[0], ((0,), (0,))).astype(BF16)
        backward = dot(enter_dy, bc[1], ((0,), (0,))).astype(BF16)
        own = slice(slab * per_slab, (slab + 1) * per_slab)
        send_ref[own, 0:part, :] = forward.reshape(per_slab, part, LANES)
        send_ref[own, part : 2 * part, :] = backward.reshape(per_slab, part, LANES)
    high, low = halves(v["carry"][:, 0:LANES])
    at = iota((RIM, LANES), 0)
    for chunk in range(send_ref.shape[0]):
        head = chunk * part // head_dim
        tile = jnp.where(
            at == 0,
            high[head : head + 1].astype(F32),
            jnp.where(at == 1, low[head : head + 1].astype(F32), 0.0),
        )
        send_ref[chunk, 2 * part : 2 * part + RIM, :] = tile.astype(BF16)


def scan_kernel(got_ref, out_ref):
    count, width, lanes = out_ref.shape
    part = width // 2
    forward = jnp.zeros((part, lanes), F32)
    backward = jnp.zeros((part, lanes), F32)

    def carry(at):
        tail = got_ref[at, width : width + RIM, :].astype(F32)
        return tail[0:1] + tail[1:2]

    for at in range(count):
        out_ref[at, 0:part, :] = forward.astype(BF16)
        forward = carry(at) * forward + got_ref[at, 0:part, :].astype(F32)
        back = count - 1 - at
        out_ref[back, part : 2 * part, :] = backward.astype(BF16)
        backward = carry(back) * backward + got_ref[back, part : 2 * part, :].astype(F32)


def intra_kernel(
    head_dim,
    doc_ref,
    a_log_ref,
    skip_ref,
    x_ref,
    halo_ref,
    bc_ref,
    wx_ref,
    wbc_ref,
    dt_ref,
    dy_ref,
    xc_ref,
    lx_ref,
    edy_ref,
    bcc_ref,
    yi_ref,
    gs_ref,
    ls_ref,
    gbc_ref,
    sbc_ref,
    hv_ref,
    ext,
    bias,
    dgram,
):
    rows, channels = x_ref.shape
    heads = dt_ref.shape[0]
    doc = doc_ref[0]
    v = head_values(doc_ref, a_log_ref, dt_ref)
    load_ext(ext, halo_ref, x_ref, bc_ref)
    for half in range(2):
        lanes = slice(half * LANES, (half + 1) * LANES)
        pre = filtered(ext, wbc_ref, channels + half * LANES, half * LANES, rows)
        gate = sigmoid(pre)
        bcc_ref[:, lanes] = (pre * gate).astype(BF16)
        sbc_ref[:, lanes] = gate * (1.0 + pre * (1.0 - gate))
    b_matrix = bcc_ref[:, 0:LANES]
    c_matrix = bcc_ref[:, LANES:]
    gram = dot(c_matrix, b_matrix, ((1,), (1,)))
    t_at, s_at = iota((rows, rows), 0), iota((rows, rows), 1)
    bias[...] = jnp.where((t_at >= s_at) & ((t_at >= doc) == (s_at >= doc)), 0.0, -1e30)
    dgram[...] = jnp.zeros_like(dgram)
    downto = jnp.where(t_at >= s_at, 1.0, 0.0)
    cum = v["cum"]
    cum_t = dot(downto, v["drop"], ((1,), (1,)), HIGHEST)
    skip = per_head(skip_ref, heads, rows)
    leave_step = v["leaving"] * v["step"]
    along_dt = jnp.zeros((heads, rows), F32)
    z_diff = jnp.zeros((heads, rows), F32)
    low_half = iota((rows, LANES), 1) < head_dim
    for slab in range(channels // LANES):
        lanes = slice(slab * LANES, (slab + 1) * LANES)
        pre = filtered(ext, wx_ref, slab * LANES, slab * LANES, rows)
        gate = sigmoid(pre)
        x_bf = (pre * gate).astype(BF16)
        silu_grad = gate * (1.0 + pre * (1.0 - gate))
        x_conv = x_bf.astype(F32)
        xc_ref[:, lanes] = x_bf
        step = spread(v["step"], slab, head_dim)
        leave = spread(leave_step, slab, head_dim)
        enter = spread(v["entering"], slab, head_dim)
        skips = spread(skip, slab, head_dim)
        dy_bf = dy_ref[:, lanes]
        dy = dy_bf.astype(F32)
        lx_ref[:, lanes] = (x_conv * leave).astype(BF16)
        edy_ref[:, lanes] = (dy * enter).astype(BF16)
        scaled = (x_conv * step).astype(BF16)
        intra = jnp.zeros((rows, LANES), F32)
        d_scaled = jnp.zeros((rows, LANES), F32)
        for side in range(LANES // head_dim):
            head = slab * (LANES // head_dim) + side
            mine = low_half if side == 0 else jnp.logical_not(low_half)
            scaled_h = jnp.where(mine, scaled.astype(F32), 0.0).astype(BF16)
            dy_h = jnp.where(mine, dy, 0.0).astype(BF16)
            kernel = jnp.exp((cum_t[:, head : head + 1] - cum[head : head + 1, :]) + bias[...])
            mixing = (gram * kernel).astype(BF16)
            response = dot(dy_h, scaled, ((1,), (1,)))
            dgram[...] += response * kernel
            intra = intra + dot(mixing, scaled_h, ((1,), (0,)))
            d_scaled = d_scaled + dot(mixing, dy_h, ((0,), (0,)))
        yi_ref[:, lanes] = intra + skips * x_conv
        gs_ref[:, lanes] = (step * d_scaled + skips * dy) * silu_grad
        ls_ref[:, lanes] = leave * silu_grad
        along_dt = along_dt + head_sum(x_conv * d_scaled, slab, head_dim, heads)
        z_diff = z_diff + head_sum(
            dy * intra - scaled.astype(F32) * d_scaled, slab, head_dim, heads
        )
    d_gram = dgram[...]
    gbc_ref[:, 0:LANES] = dot(d_gram, c_matrix.astype(F32), ((0,), (0,)), HIGHEST)
    gbc_ref[:, LANES:] = dot(d_gram, b_matrix.astype(F32), ((1,), (0,)), HIGHEST)
    small = [
        leave_step,
        v["leaving"],
        v["entering"],
        along_dt,
        z_diff,
        v["carry"],
        v["decay"],
        sigmoid(dt_ref[...]),
    ]
    for at, values in enumerate(small):
        hv_ref[at] = values


def state_of(st_ref, which):
    count, width, lanes = st_ref.shape
    part = width // 2
    return st_ref[:, which * part : (which + 1) * part, :].reshape(count * part, lanes)


def bc_kernel(
    core_ref, st_ref, lx_ref, edy_ref, b_ref, gbc_ref, sbc_ref, gs_ref, ls_ref, wbc_ref,
    keep_ref, give_ref, halo_ref, ext, total,
):
    rows = lx_ref.shape[0]
    taps = wbc_ref.shape[0]
    channels = lx_ref.shape[1]
    state, dstate = state_of(st_ref, 0), state_of(st_ref, 1)
    grad_b = gbc_ref[:, 0:LANES] + dot(lx_ref[...], dstate, ((1,), (0,)))
    grad_c = gbc_ref[:, LANES:] + dot(edy_ref[...], state, ((1,), (0,)))
    ext[0:rows, 0:LANES] = grad_b * sbc_ref[:, 0:LANES]
    ext[0:rows, LANES:] = grad_c * sbc_ref[:, LANES:]
    ext[rows:, :] = jnp.zeros((RIM, 2 * LANES), F32)
    w = wbc_ref[...].astype(F32)
    out = w[taps - 1 : taps] * ext[0:rows, :]
    for tap in range(taps - 1):
        out = out + w[tap : tap + 1] * ext[pl.ds(taps - 1 - tap, rows), :]
    total[...] = out
    half = rows // 2
    core = core_ref[0]
    keep_ref[...] = total[pl.ds(pl.multiple_of(core * half, half), half), :]
    give_ref[...] = total[pl.ds(pl.multiple_of((1 - core) * half, half), half), :].astype(BF16)
    d_leaving = dot(b_ref[...], dstate, ((1,), (1,)))[0:RIM]
    halo_ref[:, 0:channels] = gs_ref[...] + ls_ref[...] * d_leaving
    halo_ref[:, channels:] = ext[0:RIM, :]


def join_kernel(keep_ref, got_ref, halo_ref, wbc_ref, out_ref, ext):
    half = keep_ref.shape[0]
    taps = wbc_ref.shape[0]
    wide = keep_ref.shape[1]
    channels = halo_ref.shape[1] - wide
    out_ref[0:half, :] = (keep_ref[...] + got_ref[...].astype(F32)).astype(BF16)
    ext[0:RIM, :] = jnp.zeros((RIM, wide), F32)
    ext[RIM:, :] = halo_ref[:, channels:]
    w = wbc_ref[...].astype(F32)
    rim = jnp.zeros((RIM, wide), F32)
    for tap in range(taps - 1):
        rim = rim + w[tap : tap + 1] * ext[pl.ds(taps - 1 - tap, RIM), :]
    out_ref[half:, :] = rim.astype(BF16)


def sum_kernel(*refs):
    out_ref = refs[-1]
    total = refs[0][...].astype(F32)
    for ref in refs[1:-1]:
        total = total + ref[...].astype(F32)
    out_ref[...] = total.astype(BF16)


def last_kernel(core_ref, mine_ref, got_ref, out_ref, total):
    rows = out_ref.shape[0]
    half = rows // 2
    core = core_ref[0]
    total[pl.ds(pl.multiple_of(core * half, half), half), :] = mine_ref[0:half, :].astype(F32)
    total[pl.ds(pl.multiple_of((1 - core) * half, half), half), :] = got_ref[0:half, :].astype(F32)
    total[rows - RIM :, :] += mine_ref[half:, :].astype(F32) + got_ref[half:, :].astype(F32)
    out_ref[...] = total[...].astype(BF16)


def out_kernel(
    head_dim, st_ref, xc_ref, dy_ref, bcc_ref, yi_ref, gs_ref, ls_ref, hv_ref, halo_ref, wx_ref,
    y_ref, gx_ref, gdt_ref, ext,
):
    rows, channels = xc_ref.shape
    heads = hv_ref.shape[1]
    taps = wx_ref.shape[0]
    state, dstate = state_of(st_ref, 0), state_of(st_ref, 1)
    b_matrix, c_matrix = bcc_ref[:, 0:LANES], bcc_ref[:, LANES:]
    leave_step, leaving, entering, along_dt, z_diff, carry, decay, dt_gate = [
        hv_ref[at] for at in range(8)
    ]
    along_leave = jnp.zeros((heads, rows), F32)
    along_enter = jnp.zeros((heads, rows), F32)
    ext[rows:, :] = halo_ref[:, 0:channels]
    for slab in range(channels // LANES):
        lanes = slice(slab * LANES, (slab + 1) * LANES)
        y_state = dot(c_matrix, state[lanes], ((1,), (1,)))
        d_leaving = dot(b_matrix, dstate[lanes], ((1,), (1,)))
        y_ref[:, lanes] = (yi_ref[:, lanes] + spread(entering, slab, head_dim) * y_state).astype(BF16)
        along_leave = along_leave + head_sum(
            xc_ref[:, lanes].astype(F32) * d_leaving, slab, head_dim, heads
        )
        along_enter = along_enter + head_sum(
            dy_ref[:, lanes].astype(F32) * y_state, slab, head_dim, heads
        )
        ext[0:rows, lanes] = gs_ref[:, lanes] + ls_ref[:, lanes] * d_leaving
        w = wx_ref[:, lanes].astype(F32)
        out = w[taps - 1 : taps] * ext[0:rows, lanes]
        for tap in range(taps - 1):
            out = out + w[tap : tap + 1] * ext[pl.ds(taps - 1 - tap, rows), lanes]
        gx_ref[:, lanes] = out.astype(BF16)
    product = state.astype(F32) * dstate.astype(F32)
    owner = iota((heads, channels), 1) // head_dim
    chosen = jnp.where(iota((heads, channels), 0) == owner, 1.0, 0.0)
    overlap = jnp.sum(dot(chosen, product, ((1,), (0,)), HIGHEST), axis=1, keepdims=True)
    leave_term = leave_step * along_leave
    final = jnp.sum(leave_term, axis=1, keepdims=True) + carry * overlap
    d_cum = z_diff + entering * along_enter - leave_term
    d_cum = d_cum + jnp.where(iota((heads, rows), 1) == rows - 1, final, 0.0)
    after = jnp.where(iota((rows, rows), 0) >= iota((rows, rows), 1), 1.0, 0.0)
    d_log = dot(d_cum, after, ((1,), (0,)), HIGHEST)
    gdt_ref[...] = (along_dt + leaving * along_leave - decay * d_log) * dt_gate


def smem():
    return pl.BlockSpec(memory_space=pltpu.SMEM)


def whole(shape):
    return pl.BlockSpec(shape, lambda i: (0,) * len(shape))


def call(kernel, name, out, scalars, arrays, scratch=(), blocks=None):
    blocks = blocks or {}
    many = isinstance(out, list)
    out = [jax.ShapeDtypeStruct(s, d) for s, d in (out if many else [out])]
    specs = [whole(o.shape) for o in out]
    return pl.pallas_call(
        kernel,
        name=name,
        out_shape=out if many else out[0],
        grid=(1,),
        in_specs=[smem() for _ in scalars]
        + [whole(blocks.get(i, a.shape)) for i, a in enumerate(arrays)],
        out_specs=specs if many else specs[0],
        scratch_shapes=list(scratch),
        compiler_params=pltpu.CompilerParams(vmem_limit_bytes=VMEM_LIMIT),
    )(*scalars, *arrays)


def shift_ctx(values, by):
    size = lax.axis_size("ctx")
    pairs = [(i, i + by) for i in range(size) if 0 <= i + by < size]
    return lax.ppermute(values, "ctx", pairs)


def swap_core(values):
    size = lax.axis_size("head")
    return lax.ppermute(values, "head", [(i, i ^ 1) for i in range(size)])


def around(values, by):
    size = lax.axis_size("head")
    return lax.ppermute(values, "head", [(i, (i + 2 * by) % size) for i in range(size)])


def body(x_raw, bc_raw, conv_x_w, conv_bc_w, dt_raw, a_log, d_skip, doc_starts, grad_y):
    rows, channels = x_raw.shape
    heads = a_log.shape[0]
    head_dim = channels // heads
    wide = bc_raw.shape[1]
    count = lax.axis_size("ctx")
    part = channels // count
    core = (lax.axis_index("head") % 2).astype(jnp.int32).reshape(1)
    halo = shift_ctx(jnp.concatenate([x_raw[rows - RIM :], bc_raw[rows - RIM :]], axis=1), 1)
    ext = pltpu.VMEM((rows + RIM, channels + wide), F32)
    send = call(
        functools.partial(send_kernel, head_dim),
        "send",
        ((count, 2 * part + RIM, LANES), BF16),
        [doc_starts, a_log],
        [x_raw, halo, bc_raw, conv_x_w, conv_bc_w, dt_raw, grad_y],
        [ext],
    )
    got = lax.all_to_all(send, "ctx", 0, 0)
    xc, lx, edy, bcc, yi, gs, ls, gbc, sbc, hv = call(
        functools.partial(intra_kernel, head_dim),
        "intra",
        [
            ((rows, channels), BF16),
            ((rows, channels), BF16),
            ((rows, channels), BF16),
            ((rows, wide), BF16),
            ((rows, channels), F32),
            ((rows, channels), F32),
            ((rows, channels), F32),
            ((rows, wide), F32),
            ((rows, wide), F32),
            ((8, heads, rows), F32),
        ],
        [doc_starts, a_log, d_skip],
        [x_raw, halo, bc_raw, conv_x_w, conv_bc_w, dt_raw, grad_y],
        [ext, pltpu.VMEM((rows, rows), F32), pltpu.VMEM((rows, rows), F32)],
    )
    scanned = call(scan_kernel, "scan", ((count, 2 * part, LANES), BF16), [], [got])
    st = lax.all_to_all(scanned, "ctx", 0, 0)
    half = rows // 2
    keep, give, rim = call(
        bc_kernel,
        "grad_bc",
        [((half, wide), F32), ((half, wide), BF16), ((RIM, channels + wide), F32)],
        [core],
        [st, lx, edy, bcc, gbc, sbc, gs, ls, conv_bc_w],
        [pltpu.VMEM((rows + RIM, wide), F32), pltpu.VMEM((rows, wide), F32)],
        {3: (2 * RIM, LANES), 6: (RIM, channels), 7: (RIM, channels)},
    )
    next_rim = shift_ctx(rim, -1)
    other = swap_core(give)
    joined = call(
        join_kernel,
        "join",
        ((half + RIM, wide), BF16),
        [],
        [keep, other, next_rim, conv_bc_w],
        [pltpu.VMEM((2 * RIM, wide), F32)],
    )
    ring = lax.axis_size("head") // 2
    pieces = [joined] + [around(joined, by) for by in range(1, ring)]
    y_out, grad_x, grad_dt = call(
        functools.partial(out_kernel, head_dim),
        "out",
        [((rows, channels), BF16), ((rows, channels), BF16), ((heads, rows), F32)],
        [],
        [st, xc, grad_y, bcc, yi, gs, ls, hv, next_rim, conv_x_w],
        [pltpu.VMEM((rows + RIM, channels), F32)],
    )
    summed = call(sum_kernel, "sum", ((half + RIM, wide), BF16), [], pieces)
    swapped = swap_core(summed)
    grad_bc = call(
        last_kernel,
        "last",
        ((rows, wide), BF16),
        [core],
        [summed, swapped],
        [pltpu.VMEM((rows, wide), F32)],
    )
    return (y_out, grad_x, grad_bc, grad_dt)


def solution(mesh):
    in_specs = (
        P("ctx", "head"),
        P("ctx", None),
        P(None, "head"),
        P(),
        P("head", "ctx"),
        P("head"),
        P("head"),
        P("ctx"),
        P("ctx", "head"),
    )
    out_specs = (P("ctx", "head"), P("ctx", "head"), P("ctx", None), P("head", "ctx"))
    return jax.shard_map(body, mesh=mesh, in_specs=in_specs, out_specs=out_specs, check_vma=False)
```

time: 487 us -> 94.7 us (0.19); the launches traced: 480 us -> 93.9 us
  waiting for transfers between devices: 261 us -> 9.15 us
  other arithmetic: 96.4 us -> 0.01 us
  blocking collectives: 55 us -> 27.6 us
  Pallas kernels: 0 us -> 18.2 us
  between operations: 15.5 us -> 1.45 us
  matrix products: 13.8 us -> 0 us
  starting transfers between devices: 11.9 us -> 22.5 us
  local copies, waits for them, and re-layouts: 24.3 us -> 15 us
    all_gather x2 -> x0, waiting for transfers between devices: 202 us -> none  [entering_2(): pieces = jax.tree.map(lambda part: lax.all_gather(part, axis), value)]
    select_n x62 -> x0, other arithmetic: 72.7 us -> none  [step(): jnp.where(position < mine, new, old)]
    psum x1 -> x0, waiting for transfers between devices: 56.9 us -> none  [body(): grad_bc_pre = lax.psum(grad_bc, 'head') * silu_grad(bc_pre)]
    unnamed x1 -> x0, blocking collectives: 55 us -> none
    all_to_all x0 -> x1, blocking collectives: none -> 27.6 us  [body(): got = lax.all_to_all(send, 'ctx', 0, 0)]
    pallas_call x0 -> x8, Pallas kernels: none -> 18.2 us  [call(): pl.pallas_call(kernel, name=name, out_shape=out if many else out[0], grid...]
    dot_general x12 -> x0, matrix products: 13.8 us -> none  [the longest x10 13.1 us: contract(): jnp.einsum(pattern, first_op, second_op, preferred_element_type=jnp.float32)]
    rev x2 -> x0, local copies, waits for them, and re-layouts: 11.8 us -> none  [entering_2(): pieces = jax.tree.map(lambda part: part[::-1], pieces)]
  transfers between devices with their start and end apart: 7 -> 8, of which waited for: 4 -> 5; matrix products, arithmetic and copies ran while one was open for 6% -> 0% of each run, Pallas kernels for 0% -> 13%
where the time goes in v1:
time: 94.7 us; the launch traced here: 93.9 us
  blocking collectives  27.6 us (29%)
  starting transfers between devices  22.5 us (24%)
  Pallas kernels  18.2 us (19%)
  local copies, waits for them, and re-layouts  15 us (16%)
  waiting for transfers between devices  9.15 us (10%)
  between operations  1.45 us (2%)
    all_to_all x1, blocking collectives, body(): got = lax.all_to_all(send, 'ctx', 0, 0)  27.6 us
    pallas_call x8, Pallas kernels, call(): pl.pallas_call(kernel, name=name, out_shape=out if many else out[0], grid...  18.2 us
    unnamed x52, local copies, waits for them, and re-layouts  14.3 us
    all_to_all x1, starting transfers between devices, body(): st = lax.all_to_all(scanned, 'ctx', 0, 0)  6.75 us
    ppermute x2, starting transfers between devices, shift_ctx(): return lax.ppermute(values, 'ctx', pairs)  6.06 us
    ppermute x2, starting transfers between devices, swap_core(): return lax.ppermute(values, 'head', [(i, i ^ 1) for i in range(size)])  5.81 us
    ppermute x2, waiting for transfers between devices, shift_ctx(): return lax.ppermute(values, 'ctx', pairs)  4.77 us
    ppermute x3, waiting for transfers between devices, around(): lax.ppermute(values, 'head', [(i, (i + 2 * by) % size) for i in range(siz...  4.37 us
  transfers between devices with their start and end apart: 8, of which 5 were waited for; matrix products, arithmetic and copies ran while one was open for 0% of the time, Pallas kernels for 13%

profile of v1, /device:TPU:7, one launch (start us, length us, event | category | flops | bytes accessed | tf_op | source)
XLA Modules:
  0.0 93.9 jit_solution(173258514131159073)
XLA Ops:
  0.6 0.0 slice-start
  0.6 0.0 slice-start.1
  0.7 0.7 slice-done
  1.4 0.0 slice-done.1
  1.4 0.0 copy-start.20
  1.4 0.0 copy-start.21
  1.4 0.0 copy-start.23
  1.4 0.0 copy-start.24
  1.4 3.6 %collective-permute-start = (bf16[8,1280]{1,0:T(8,128)(2,1)S(1)}, bf16[8,1280]{1,0:T(8,128)(2,1)S(1)}, u32[]{:S(2)}, u32[]{:S(2)}) collective-permute-start(bf16[8,1280]{1,0:T(8,128)(2,1)S(1)} %pad_maximum_fusion), channel_id=1, source_target_pairs={{0,8},{8,16},{16,24},{24,32},{32,40},{40,48},{48,56},{56,64},{64,7... | collective-permute-start | bytes 61448 | tf_op jit(solution)/shard_map/ppermute | solution.py:399
  5.6 0.4 collective-permute-done.halo_ref
  6.0 0.0 copy-done.20
  6.1 0.0 copy-done.21
  6.1 0.0 copy-done.23
  6.1 0.0 copy-done.24
  6.1 0.0 copy-start
  6.1 1.0 %copy-done = bf16[256,1024]{1,0:T(8,128)(2,1)S(1)} copy-done((bf16[256,1024]{1,0:T(8,128)(2,1)S(1)}, bf16[256,1024]{1,0:T(8,128)(2,1)}, u32[]{:S(2)}) %copy-start) | copy-done | bytes 524312
  7.1 0.0 copy-start.4
  7.1 1.0 %copy-done.4 = bf16[256,1024]{1,0:T(8,128)(2,1)S(1)} copy-done((bf16[256,1024]{1,0:T(8,128)(2,1)S(1)}, bf16[256,1024]{1,0:T(8,128)(2,1)}, u32[]{:S(2)}) %copy-start.4) | copy-done | bytes 524312
  8.2 0.0 copy-start.8
  8.2 0.9 copy-done.8
  9.1 0.0 copy-start.18
  9.1 3.5 %send.1 = bf16[32,72,128]{2,1,0:T(8,128)(2,1)S(1)} custom-call(s32[1]{0:T(128)S(6)} %copy.13.doc_ref, f32[16]{0:T(128)S(1)} %copy-done.24, bf16[256,1024]{1,0:T(8,128)(2,1)S(1)} %copy-done.4, bf16[8,1280]{1,0:T(8,128)(2,1)S(1)} %collective-permute-done.halo_ref, bf16[256,256]{1,0:T(8,128)(2,1)S(1)} %copy-done.8, bf16[4,1024]{1,0:T(4,128)(2,1)S(1)} %copy-done.20, ...), custom_call_target="tpu_custom_call" | custom-call | tf_op jit(solution)/shard_map/send/pallas_call | solution.py:383
  12.5 0.0 copy-done.18
  12.5 27.6 %all_to_all.10.got_ref = bf16[32,72,128]{2,1,0:T(8,128)(2,1)S(1)} all-to-all(bf16[32,72,128]{2,1,0:T(8,128)(2,1)S(1)} %send.1), channel_id=1, replica_groups=mesh['ctx'=32,'head'=8] {'ctx'}, dimensions={0} | all-to-all | bytes 1179648 | tf_op jit(solution)/shard_map/all_to_all | solution.py:430
  40.2 0.0 copy-start.9
  40.2 0.9 scan.1
  41.1 0.0 copy-start.1
  41.1 6.8 %all-to-all-start.1 = ((bf16[32,64,128]{2,1,0:T(8,128)(2,1)}), bf16[32,64,128]{2,1,0:T(8,128)(2,1)S(1)}, u32[]{:S(2)}, u32[]{:S(2)}) async-start(bf16[32,64,128]{2,1,0:T(8,128)(2,1)} %scan.1), calls=%async_computation.1 | async-start | bytes 1048576 | tf_op jit(solution)/shard_map/all_to_all | solution.py:451
  47.9 0.0 copy-done.9
  47.9 0.0 copy-done.1
  47.9 0.0 copy-done.5
  47.9 0.0 copy-start.19
  48.0 0.7 copy-done.19
  48.7 0.7 copy-done.22
  49.4 0.7 copy-done.25
  50.0 9.1 %intra.1 = (bf16[256,1024]{1,0:T(8,128)(2,1)S(1)}, bf16[256,1024]{1,0:T(8,128)(2,1)S(1)}, bf16[256,1024]{1,0:T(8,128)(2,1)S(1)}, bf16[256,256]{1,0:T(8,128)(2,1)...) custom-call(s32[1]{0:T(128)S(6)} %copy.13.doc_ref, ...), custom_call_target="tpu_custom_call" | custom-call | tf_op jit(solution)/shard_map/intra/pallas_call | solution.py:383
  59.2 1.0 %copy-done.6 = f32[256,1024]{1,0:T(8,128)} copy-done((f32[256,1024]{1,0:T(8,128)}, f32[256,1024]{1,0:T(8,128)S(1)}, u32[]{:S(2)}) %copy-start.6) | copy-done | bytes 1048600
  60.1 0.8 copy-done.10
  60.9 0.8 copy-done.12
  61.7 0.7 copy-done.14
  62.4 0.7 copy-done.16
  63.1 0.0 all-to-all-done.1.st_ref
  63.1 1.2 %copy-done.2 = f32[256,1024]{1,0:T(8,128)S(1)} copy-done((f32[256,1024]{1,0:T(8,128)S(1)}, f32[256,1024]{1,0:T(8,128)}, u32[]{:S(2)}) %copy-start.2) | copy-done | bytes 1048600
  64.3 1.0 %copy-done.11 = bf16[256,1024]{1,0:T(8,128)(2,1)S(1)} copy-done((bf16[256,1024]{1,0:T(8,128)(2,1)S(1)}, bf16[256,1024]{1,0:T(8,128)(2,1)}, u32[]{:S(2)}) %copy-start.11) | copy-done | bytes 524312
  65.4 1.0 %copy-done.13 = bf16[256,1024]{1,0:T(8,128)(2,1)S(1)} copy-done((bf16[256,1024]{1,0:T(8,128)(2,1)S(1)}, bf16[256,1024]{1,0:T(8,128)(2,1)}, u32[]{:S(2)}) %copy-start.13) | copy-done | bytes 524312
  66.4 0.9 %copy-done.15 = f32[256,256]{1,0:T(8,128)S(1)} copy-done((f32[256,256]{1,0:T(8,128)S(1)}, f32[256,256]{1,0:T(8,128)}, u32[]{:S(2)}) %copy-start.15) | copy-done | bytes 262168
  67.4 0.9 %copy-done.17 = f32[256,256]{1,0:T(8,128)S(1)} copy-done((f32[256,256]{1,0:T(8,128)S(1)}, f32[256,256]{1,0:T(8,128)}, u32[]{:S(2)}) %copy-start.17) | copy-done | bytes 262168
  68.3 0.5 grad_bc.1
  68.8 3.1 %collective-permute-start.2 = (bf16[128,256]{1,0:T(8,128)(2,1)S(1)}, bf16[128,256]{1,0:T(8,128)(2,1)S(1)}, u32[]{:S(2)}, u32[]{:S(2)}) collective-permute-start(bf16[128,256]{1,0:T(8,128)(2,1)S(1)} %get-tuple-element.34), channel_id=1, source_target_pairs={{0,1},{1,0},{2,3},{3,2},{4,5},{5,4},{6,7},{7,6},{8,9},{9,8},{10,11... | collective-permute-start | bytes 196616 | tf_op jit(solution)/shard_map/ppermute | solution.py:404
  72.0 2.5 %collective-permute-start.1 = (f32[8,1280]{1,0:T(8,128)S(1)}, f32[8,1280]{1,0:T(8,128)S(1)}, u32[]{:S(2)}, u32[]{:S(2)}) collective-permute-start(f32[8,1280]{1,0:T(8,128)S(1)} %get-tuple-element.30), channel_id=1, source_target_pairs={{8,0},{16,8},{24,16},{32,24},{40,32},{48,40},{56,48},{64,56},{72,6... | collective-permute-start | bytes 122888 | tf_op jit(solution)/shard_map/ppermute | solution.py:399
  74.4 4.4 %collective-permute-done.1.halo_ref = f32[8,1280]{1,0:T(8,128)S(1)} collective-permute-done((f32[8,1280]{1,0:T(8,128)S(1)}, f32[8,1280]{1,0:T(8,128)S(1)}, u32[]{:S(2)}, u32[]{:S(2)}) %collective-permute-start.1) | collective-permute-done | bytes 40992 | tf_op jit(solution)/shard_map/ppermute | solution.py:399
  78.8 0.0 collective-permute-done.2.got_ref
  78.8 2.8 %collective-permute-start.5 = (bf16[136,256]{1,0:T(8,128)(2,1)S(1)}, bf16[136,256]{1,0:T(8,128)(2,1)S(1)}, u32[]{:S(2)}, u32[]{:S(2)}) collective-permute-start(bf16[136,256]{1,0:T(8,128)(2,1)S(1)} %join.1.refs_0_), channel_id=1, source_target_pairs={{0,6},{1,7},{2,0},{3,1},{4,2},{5,3},{6,4},{7,5},{8,14},{9,15},{10,... | collective-permute-start | bytes 208904 | tf_op jit(solution)/shard_map/ppermute | solution.py:409
  81.7 0.3 collective-permute-start.4
  82.0 0.7 collective-permute-start.3
  82.7 0.3 collective-permute-done.5.refs_3_
  83.0 3.4 %collective-permute-done.4.refs_2_ = bf16[136,256]{1,0:T(8,128)(2,1)S(1)} collective-permute-done((bf16[136,256]{1,0:T(8,128)(2,1)S(1)}, bf16[136,256]{1,0:T(8,128)(2,1)S(1)}, u32[]{:S(2)}, u32[]{:S(2)}) %collective-permute-start.4) | collective-permute-done | bytes 69664 | tf_op jit(solution)/shard_map/ppermute | solution.py:409
  86.4 0.7 collective-permute-done.3.refs_1_
  87.1 2.7 %collective-permute-start.6 = (bf16[136,256]{1,0:T(8,128)(2,1)S(1)}, bf16[136,256]{1,0:T(8,128)(2,1)S(1)}, u32[]{:S(2)}, u32[]{:S(2)}) collective-permute-start(bf16[136,256]{1,0:T(8,128)(2,1)S(1)} %sum.1.mine_ref), channel_id=1, source_target_pairs={{0,1},{1,0},{2,3},{3,2},{4,5},{5,4},{6,7},{7,6},{8,9},{9,8},{10,11... | collective-permute-start | bytes 208904 | tf_op jit(solution)/shard_map/ppermute | solution.py:404
  89.8 0.0 copy-done.3
  89.8 0.0 copy-done.7
  89.8 3.4 %out.1 = (bf16[256,1024]{1,0:T(8,128)(2,1)}, bf16[256,1024]{1,0:T(8,128)(2,1)}, f32[16,256]{1,0:T(8,128)}) custom-call(bf16[32,64,128]{2,1,0:T(8,128)(2,1)S(1)} %all-to-all-done.1.st_ref, bf16[256,1024]{1,0:T(8,128)(2,1)S(1)} %get-tuple-element.20.xc_ref, bf16[256,1024]{1,0:T(8,128)(2,1)S(1)} %copy-done.1, ...), custom_call_target="tpu_custom_call" | custom-call | tf_op jit(solution)/shard_map/out/pallas_call | solution.py:383
  93.2 0.0 collective-permute-done.6.got_ref
  93.2 0.7 last.1
  (18 shorter events, 0.1 us)
Async XLA Ops:
  0.6 0.7 slice-start
  0.6 0.7 slice-start.1
  1.4 4.7 %copy-start.20 = (bf16[4,1024]{1,0:T(4,128)(2,1)S(1)}, bf16[4,1024]{1,0:T(4,128)(2,1)}, u32[]{:S(2)}) copy-start(bf16[4,1024]{1,0:T(4,128)(2,1)} %wx_ref.5) | copy-start | bytes 24580
  1.4 4.7 %copy-start.21 = (f32[16,256]{1,0:T(8,128)S(1)}, f32[16,256]{1,0:T(8,128)}, u32[]{:S(2)}) copy-start(f32[16,256]{1,0:T(8,128)} %dt_ref.3) | copy-start | bytes 49156
  1.4 4.7 %copy-start.23 = (bf16[4,256]{1,0:T(4,128)(2,1)S(1)}, bf16[4,256]{1,0:T(4,128)(2,1)}, u32[]{:S(2)}) copy-start(bf16[4,256]{1,0:T(4,128)(2,1)} %wbc_ref.7) | copy-start | bytes 6148
  1.4 4.7 %copy-start.24 = (f32[16]{0:T(128)S(1)}, f32[16]{0:T(128)}, u32[]{:S(2)}) copy-start(f32[16]{0:T(128)} %a_log_ref.3) | copy-start | bytes 196
  1.4 4.7 %collective-permute-start = (bf16[8,1280]{1,0:T(8,128)(2,1)S(1)}, bf16[8,1280]{1,0:T(8,128)(2,1)S(1)}, u32[]{:S(2)}, u32[]{:S(2)}) collective-permute-start(bf16[8,1280]{1,0:T(8,128)(2,1)S(1)} %pad_maximum_fusion), channel_id=1, source_target_pairs={{0,8},{8,16},{16,24},{24,32},{32,40},{40,48},{48,56},{56,64},{64,7... | collective-permute-start | bytes 61448 | tf_op jit(solution)/shard_map/ppermute | solution.py:399
  6.1 1.0 %copy-start = (bf16[256,1024]{1,0:T(8,128)(2,1)S(1)}, bf16[256,1024]{1,0:T(8,128)(2,1)}, u32[]{:S(2)}) copy-start(bf16[256,1024]{1,0:T(8,128)(2,1)} %dy_ref.5) | copy-start | bytes 1572868
  7.1 1.0 %copy-start.4 = (bf16[256,1024]{1,0:T(8,128)(2,1)S(1)}, bf16[256,1024]{1,0:T(8,128)(2,1)}, u32[]{:S(2)}) copy-start(bf16[256,1024]{1,0:T(8,128)(2,1)} %x_ref.3) | copy-start | bytes 1572868
  8.2 0.9 copy-start.8
  9.1 3.5 %copy-start.18 = (bf16[8,1280]{1,0:T(8,128)(2,1)}, bf16[8,1280]{1,0:T(8,128)(2,1)S(1)}, u32[]{:S(2)}) copy-start(bf16[8,1280]{1,0:T(8,128)(2,1)S(1)} %collective-permute-done.halo_ref) | copy-start | bytes 61444
  40.2 7.7 %copy-start.9 = (bf16[256,256]{1,0:T(8,128)(2,1)S(1)}, bf16[256,256]{1,0:T(8,128)(2,1)}, u32[]{:S(2)}) copy-start(bf16[256,256]{1,0:T(8,128)(2,1)} %bc_ref.3) | copy-start | bytes 393220
  41.1 6.8 %copy-start.1 = (bf16[256,1024]{1,0:T(8,128)(2,1)S(1)}, bf16[256,1024]{1,0:T(8,128)(2,1)}, u32[]{:S(2)}) copy-start(bf16[256,1024]{1,0:T(8,128)(2,1)} %dy_ref.5) | copy-start | bytes 1572868
  41.1 6.8 %copy-start.5 = (bf16[256,1024]{1,0:T(8,128)(2,1)S(1)}, bf16[256,1024]{1,0:T(8,128)(2,1)}, u32[]{:S(2)}) copy-start(bf16[256,1024]{1,0:T(8,128)(2,1)} %x_ref.3) | copy-start | bytes 1572868
  41.1 22.0 %all-to-all-start.1 = ((bf16[32,64,128]{2,1,0:T(8,128)(2,1)}), bf16[32,64,128]{2,1,0:T(8,128)(2,1)S(1)}, u32[]{:S(2)}, u32[]{:S(2)}) async-start(bf16[32,64,128]{2,1,0:T(8,128)(2,1)} %scan.1), calls=%async_computation.1 | async-start | bytes 1048576 | tf_op jit(solution)/shard_map/all_to_all | solution.py:451
  47.9 0.7 copy-start.19
  48.7 0.7 copy-start.22
  49.4 0.7 copy-start.25
  59.2 1.0 %copy-start.6 = (f32[256,1024]{1,0:T(8,128)}, f32[256,1024]{1,0:T(8,128)S(1)}, u32[]{:S(2)}) copy-start(f32[256,1024]{1,0:T(8,128)S(1)} %get-tuple-element.22.yi_ref) | copy-start | bytes 3145732
  60.1 0.8 copy-start.10
  60.9 0.8 copy-start.12
  61.7 0.7 copy-start.14
  62.4 0.7 copy-start.16
  63.1 1.2 %copy-start.2 = (f32[256,1024]{1,0:T(8,128)S(1)}, f32[256,1024]{1,0:T(8,128)}, u32[]{:S(2)}) copy-start(f32[256,1024]{1,0:T(8,128)} %get-tuple-element.24.ls_ref) | copy-start | bytes 3145732
  64.3 1.0 %copy-start.11 = (bf16[256,1024]{1,0:T(8,128)(2,1)S(1)}, bf16[256,1024]{1,0:T(8,128)(2,1)}, u32[]{:S(2)}) copy-start(bf16[256,1024]{1,0:T(8,128)(2,1)} %copy-done.10) | copy-start | bytes 1572868
  65.4 1.0 %copy-start.13 = (bf16[256,1024]{1,0:T(8,128)(2,1)S(1)}, bf16[256,1024]{1,0:T(8,128)(2,1)}, u32[]{:S(2)}) copy-start(bf16[256,1024]{1,0:T(8,128)(2,1)} %copy-done.12) | copy-start | bytes 1572868
  66.4 0.9 %copy-start.15 = (f32[256,256]{1,0:T(8,128)S(1)}, f32[256,256]{1,0:T(8,128)}, u32[]{:S(2)}) copy-start(f32[256,256]{1,0:T(8,128)} %copy-done.14) | copy-start | bytes 786436
  67.4 0.9 %copy-start.17 = (f32[256,256]{1,0:T(8,128)S(1)}, f32[256,256]{1,0:T(8,128)}, u32[]{:S(2)}) copy-start(f32[256,256]{1,0:T(8,128)} %copy-done.16) | copy-start | bytes 786436
  68.3 21.5 %copy-start.3 = (f32[256,1024]{1,0:T(8,128)S(1)}, f32[256,1024]{1,0:T(8,128)}, u32[]{:S(2)}) copy-start(f32[256,1024]{1,0:T(8,128)} %get-tuple-element.24.ls_ref) | copy-start | bytes 3145732
  68.3 21.5 %copy-start.7 = (f32[256,1024]{1,0:T(8,128)S(1)}, f32[256,1024]{1,0:T(8,128)}, u32[]{:S(2)}) copy-start(f32[256,1024]{1,0:T(8,128)} %copy-done.6) | copy-start | bytes 3145732
  68.8 10.0 %collective-permute-start.2 = (bf16[128,256]{1,0:T(8,128)(2,1)S(1)}, bf16[128,256]{1,0:T(8,128)(2,1)S(1)}, u32[]{:S(2)}, u32[]{:S(2)}) collective-permute-start(bf16[128,256]{1,0:T(8,128)(2,1)S(1)} %get-tuple-element.34), channel_id=1, source_target_pairs={{0,1},{1,0},{2,3},{3,2},{4,5},{5,4},{6,7},{7,6},{8,9},{9,8},{10,11... | collective-permute-start | bytes 196616 | tf_op jit(solution)/shard_map/ppermute | solution.py:404
  72.0 6.8 %collective-permute-start.1 = (f32[8,1280]{1,0:T(8,128)S(1)}, f32[8,1280]{1,0:T(8,128)S(1)}, u32[]{:S(2)}, u32[]{:S(2)}) collective-permute-start(f32[8,1280]{1,0:T(8,128)S(1)} %get-tuple-element.30), channel_id=1, source_target_pairs={{8,0},{16,8},{24,16},{32,24},{40,32},{48,40},{56,48},{64,56},{72,6... | collective-permute-start | bytes 122888 | tf_op jit(solution)/shard_map/ppermute | solution.py:399
  78.8 4.2 %collective-permute-start.5 = (bf16[136,256]{1,0:T(8,128)(2,1)S(1)}, bf16[136,256]{1,0:T(8,128)(2,1)S(1)}, u32[]{:S(2)}, u32[]{:S(2)}) collective-permute-start(bf16[136,256]{1,0:T(8,128)(2,1)S(1)} %join.1.refs_0_), channel_id=1, source_target_pairs={{0,6},{1,7},{2,0},{3,1},{4,2},{5,3},{6,4},{7,5},{8,14},{9,15},{10,... | collective-permute-start | bytes 208904 | tf_op jit(solution)/shard_map/ppermute | solution.py:409
  81.7 4.7 %collective-permute-start.4 = (bf16[136,256]{1,0:T(8,128)(2,1)S(1)}, bf16[136,256]{1,0:T(8,128)(2,1)S(1)}, u32[]{:S(2)}, u32[]{:S(2)}) collective-permute-start(bf16[136,256]{1,0:T(8,128)(2,1)S(1)} %join.1.refs_0_), channel_id=1, source_target_pairs={{0,4},{1,5},{2,6},{3,7},{4,0},{5,1},{6,2},{7,3},{8,12},{9,13},{10,... | collective-permute-start | bytes 208904 | tf_op jit(solution)/shard_map/ppermute | solution.py:409
  82.0 5.1 %collective-permute-start.3 = (bf16[136,256]{1,0:T(8,128)(2,1)S(1)}, bf16[136,256]{1,0:T(8,128)(2,1)S(1)}, u32[]{:S(2)}, u32[]{:S(2)}) collective-permute-start(bf16[136,256]{1,0:T(8,128)(2,1)S(1)} %join.1.refs_0_), channel_id=1, source_target_pairs={{0,2},{1,3},{2,4},{3,5},{4,6},{5,7},{6,0},{7,1},{8,10},{9,11},{10,... | collective-permute-start | bytes 208904 | tf_op jit(solution)/shard_map/ppermute | solution.py:409
  87.1 6.1 %collective-permute-start.6 = (bf16[136,256]{1,0:T(8,128)(2,1)S(1)}, bf16[136,256]{1,0:T(8,128)(2,1)S(1)}, u32[]{:S(2)}, u32[]{:S(2)}) collective-permute-start(bf16[136,256]{1,0:T(8,128)(2,1)S(1)} %sum.1.mine_ref), channel_id=1, source_target_pairs={{0,1},{1,0},{2,3},{3,2},{4,5},{5,4},{6,7},{7,6},{8,9},{9,8},{10,11... | collective-permute-start | bytes 208904 | tf_op jit(solution)/shard_map/ppermute | solution.py:404

commit v2 on v1

--- a/solution.py
+++ b/solution.py
@@ -11,7 +11,7 @@
 BF16 = jnp.bfloat16
 LANES = 128
 RIM = 8
-VMEM_LIMIT = 48 * 1024 * 1024
+VMEM_LIMIT = 24 * 1024 * 1024
 HIGHEST = lax.Precision.HIGHEST
 
 
@@ -78,12 +78,28 @@
     )
 
 
-def load_ext(ext, halo_ref, x_ref, bc_ref):
-    channels = x_ref.shape[1]
-    rows = x_ref.shape[0]
-    ext[0:RIM, :] = halo_ref[...].astype(F32)
-    ext[RIM : RIM + rows, 0:channels] = x_ref[...].astype(F32)
-    ext[RIM : RIM + rows, channels:] = bc_ref[...].astype(F32)
+def lanes_of(slab):
+    return slice(slab * LANES, (slab + 1) * LANES)
+
+
+def fetch(source, target, sems):
+    copies = []
+    for slab in range(source.shape[1] // LANES):
+        part = (slice(None), lanes_of(slab))
+        copies.append(pltpu.make_async_copy(source.at[part], target.at[part], sems.at[slab]))
+        copies[-1].start()
+    return copies
+
+
+def put(source, target, sem, at):
+    copy = pltpu.make_async_copy(source.at[at], target.at[at], sem)
+    copy.start()
+    return copy
+
+
+def load_ext(ext, halo_ref, values, at, lanes):
+    ext[0:RIM, at] = halo_ref[:, at].astype(F32)
+    ext[RIM : RIM + values.shape[0], at] = values[:, lanes].astype(F32)
 
 
 def filtered(ext, w_ref, at, w_at, rows):
@@ -97,43 +113,54 @@
 
 
 def send_kernel(
-    head_dim, doc_ref, a_log_ref, x_ref, halo_ref, bc_ref, wx_ref, wbc_ref, dt_ref, dy_ref, send_ref, ext
+    head_dim, doc_ref, a_log_ref, x_hbm, dy_hbm, bc_hbm, halo_ref, wx_ref, wbc_ref, dt_ref,
+    send_hbm, x_ref, dy_ref, bc_ref, send_ref, ext, x_sems, dy_sems, bc_sems, out_sems,
 ):
     rows, channels = x_ref.shape
-    heads = dt_ref.shape[0]
     part = channels // send_ref.shape[0]
     per_slab = LANES // part
+    bc_in = fetch(bc_hbm, bc_ref, bc_sems)
+    x_in = fetch(x_hbm, x_ref, x_sems)
+    dy_in = fetch(dy_hbm, dy_ref, dy_sems)
     v = head_values(doc_ref, a_log_ref, dt_ref)
-    load_ext(ext, halo_ref, x_ref, bc_ref)
+    leave_step = v["leaving"] * v["step"]
+    high, low = halves(v["carry"][:, 0:LANES])
+    at = iota((RIM, LANES), 0)
     bc = []
     for half in range(2):
+        bc_in[half].wait()
+        load_ext(ext, halo_ref, bc_ref, lanes_of(channels // LANES + half), lanes_of(half))
         pre = filtered(ext, wbc_ref, channels + half * LANES, half * LANES, rows)
         bc.append((pre * sigmoid(pre)).astype(BF16))
-    leave_step = v["leaving"] * v["step"]
+    sent = []
     for slab in range(channels // LANES):
-        lanes = slice(slab * LANES, (slab + 1) * LANES)
+        lanes = lanes_of(slab)
+        x_in[slab].wait()
+        load_ext(ext, halo_ref, x_ref, lanes, lanes)
         pre = filtered(ext, wx_ref, slab * LANES, slab * LANES, rows)
         x_conv = (pre * sigmoid(pre)).astype(BF16).astype(F32)
         leaving_x = (x_conv * spread(leave_step, slab, head_dim)).astype(BF16)
+        dy_in[slab].wait()
         enter_dy = (dy_ref[:, lanes].astype(F32) * spread(v["entering"], slab, head_dim)).astype(BF16)
         forward = dot(leaving_x, bc[0], ((0,), (0,))).astype(BF16)
         backward = dot(enter_dy, bc[1], ((0,), (0,))).astype(BF16)
         own = slice(slab * per_slab, (slab + 1) * per_slab)
         send_ref[own, 0:part, :] = forward.reshape(per_slab, part, LANES)
         send_ref[own, part : 2 * part, :] = backward.reshape(per_slab, part, LANES)
-    high, low = halves(v["carry"][:, 0:LANES])
-    at = iota((RIM, LANES), 0)
-    for chunk in range(send_ref.shape[0]):
-        head = chunk * part // head_dim
-        tile = jnp.where(
-            at == 0,
-            high[head : head + 1].astype(F32),
-            jnp.where(at == 1, low[head : head + 1].astype(F32), 0.0),
-        )
-        send_ref[chunk, 2 * part : 2 * part + RIM, :] = tile.astype(BF16)
-
-
-def scan_kernel(got_ref, out_ref):
+        for chunk in range(slab * per_slab, (slab + 1) * per_slab):
+            head = chunk * part // head_dim
+            tile = jnp.where(
+                at == 0,
+                high[head : head + 1].astype(F32),
+                jnp.where(at == 1, low[head : head + 1].astype(F32), 0.0),
+            )
+            send_ref[chunk, 2 * part : 2 * part + RIM, :] = tile.astype(BF16)
+        sent.append(put(send_ref, send_hbm, out_sems.at[slab], (own,)))
+    for copy in sent:
+        copy.wait()
+
+
+def scan_kernel(got_ref, out_hbm, out_ref, sems):
     count, width, lanes = out_ref.shape
     part = width // 2
     forward = jnp.zeros((part, lanes), F32)
@@ -143,47 +170,39 @@
         tail = got_ref[at, width : width + RIM, :].astype(F32)
         return tail[0:1] + tail[1:2]
 
+    sent = []
     for at in range(count):
         out_ref[at, 0:part, :] = forward.astype(BF16)
         forward = carry(at) * forward + got_ref[at, 0:part, :].astype(F32)
         back = count - 1 - at
         out_ref[back, part : 2 * part, :] = backward.astype(BF16)
         backward = carry(back) * backward + got_ref[back, part : 2 * part, :].astype(F32)
+        low, high = min(at, back), max(at, back)
+        if at >= count // 2 and (at + 1) % 4 == 0:
+            sent.append(put(out_ref, out_hbm, sems.at[len(sent)], (slice(high - 3, high + 1),)))
+            sent.append(put(out_ref, out_hbm, sems.at[len(sent)], (slice(low, low + 4),)))
+    for copy in sent:
+        copy.wait()
 
 
 def intra_kernel(
-    head_dim,
-    doc_ref,
-    a_log_ref,
-    skip_ref,
-    x_ref,
-    halo_ref,
-    bc_ref,
-    wx_ref,
-    wbc_ref,
-    dt_ref,
-    dy_ref,
-    xc_ref,
-    lx_ref,
-    edy_ref,
-    bcc_ref,
-    yi_ref,
-    gs_ref,
-    ls_ref,
-    gbc_ref,
-    sbc_ref,
-    hv_ref,
-    ext,
-    bias,
-    dgram,
+    head_dim, doc_ref, a_log_ref, skip_ref, x_hbm, dy_hbm, bc_hbm, halo_ref, wx_ref, wbc_ref, dt_ref,
+    xc_hbm, yi_hbm, gs_hbm, ls_hbm,
+    lx_ref, edy_ref, bcc_ref, gbc_ref, sbc_ref, hv_ref, rim_ref,
+    x_ref, dy_ref, bc_ref, xc_ref, yi_ref, gs_ref, ls_ref, ext, bias, dgram,
+    x_sems, dy_sems, bc_sems, out_sems,
 ):
     rows, channels = x_ref.shape
     heads = dt_ref.shape[0]
     doc = doc_ref[0]
+    bc_in = fetch(bc_hbm, bc_ref, bc_sems)
+    x_in = fetch(x_hbm, x_ref, x_sems)
+    dy_in = fetch(dy_hbm, dy_ref, dy_sems)
     v = head_values(doc_ref, a_log_ref, dt_ref)
-    load_ext(ext, halo_ref, x_ref, bc_ref)
     for half in range(2):
-        lanes = slice(half * LANES, (half + 1) * LANES)
+        lanes = lanes_of(half)
+        bc_in[half].wait()
+        load_ext(ext, halo_ref, bc_ref, lanes_of(channels // LANES + half), lanes)
         pre = filtered(ext, wbc_ref, channels + half * LANES, half * LANES, rows)
         gate = sigmoid(pre)
         bcc_ref[:, lanes] = (pre * gate).astype(BF16)
@@ -202,8 +221,12 @@
     along_dt = jnp.zeros((heads, rows), F32)
     z_diff = jnp.zeros((heads, rows), F32)
     low_half = iota((rows, LANES), 1) < head_dim
+    sent = []
     for slab in range(channels // LANES):
-        lanes = slice(slab * LANES, (slab + 1) * LANES)
+        lanes = lanes_of(slab)
+        x_in[slab].wait()
+        load_ext(ext, halo_ref, x_ref, lanes, lanes)
+        dy_in[slab].wait()
         pre = filtered(ext, wx_ref, slab * LANES, slab * LANES, rows)
         gate = sigmoid(pre)
         x_bf = (pre * gate).astype(BF16)
@@ -235,6 +258,13 @@
         yi_ref[:, lanes] = intra + skips * x_conv
         gs_ref[:, lanes] = (step * d_scaled + skips * dy) * silu_grad
         ls_ref[:, lanes] = leave * silu_grad
+        rim_ref[0, :, lanes] = gs_ref[0:RIM, lanes]
+        rim_ref[1, :, lanes] = ls_ref[0:RIM, lanes]
+        at = (slice(None), lanes)
+        for which, (mine, out) in enumerate(
+            ((xc_ref, xc_hbm), (yi_ref, yi_hbm), (gs_ref, gs_hbm), (ls_ref, ls_hbm))
+        ):
+            sent.append(put(mine, out, out_sems.at[slab * 4 + which], at))
         along_dt = along_dt + head_sum(x_conv * d_scaled, slab, head_dim, heads)
         z_diff = z_diff + head_sum(
             dy * intra - scaled.astype(F32) * d_scaled, slab, head_dim, heads
@@ -254,6 +284,8 @@
     ]
     for at, values in enumerate(small):
         hv_ref[at] = values
+    for copy in sent:
+        copy.wait()
 
 
 def state_of(st_ref, which):
@@ -263,7 +295,7 @@
 
 
 def bc_kernel(
-    core_ref, st_ref, lx_ref, edy_ref, b_ref, gbc_ref, sbc_ref, gs_ref, ls_ref, wbc_ref,
+    core_ref, st_ref, lx_ref, edy_ref, b_ref, gbc_ref, sbc_ref, rim_ref, wbc_ref,
     keep_ref, give_ref, halo_ref, ext, total,
 ):
     rows = lx_ref.shape[0]
@@ -284,8 +316,8 @@
     core = core_ref[0]
     keep_ref[...] = total[pl.ds(pl.multiple_of(core * half, half), half), :]
     give_ref[...] = total[pl.ds(pl.multiple_of((1 - core) * half, half), half), :].astype(BF16)
-    d_leaving = dot(b_ref[...], dstate, ((1,), (1,)))[0:RIM]
-    halo_ref[:, 0:channels] = gs_ref[...] + ls_ref[...] * d_leaving
+    d_leaving = dot(b_ref[0 : 2 * RIM, 0:LANES], dstate, ((1,), (1,)))[0:RIM]
+    halo_ref[:, 0:channels] = rim_ref[0] + rim_ref[1] * d_leaving
     halo_ref[:, channels:] = ext[0:RIM, :]
 
 
@@ -323,12 +355,19 @@
 
 
 def out_kernel(
-    head_dim, st_ref, xc_ref, dy_ref, bcc_ref, yi_ref, gs_ref, ls_ref, hv_ref, halo_ref, wx_ref,
-    y_ref, gx_ref, gdt_ref, ext,
+    head_dim, xc_hbm, dy_hbm, yi_hbm, gs_hbm, ls_hbm, st_ref, bcc_ref, hv_ref, halo_ref, wx_ref,
+    y_hbm, gx_hbm, gdt_ref,
+    xc_ref, dy_ref, yi_ref, gs_ref, ls_ref, y_ref, gx_ref, ext,
+    xc_sems, dy_sems, yi_sems, gs_sems, ls_sems, out_sems,
 ):
     rows, channels = xc_ref.shape
     heads = hv_ref.shape[1]
     taps = wx_ref.shape[0]
+    yi_in = fetch(yi_hbm, yi_ref, yi_sems)
+    gs_in = fetch(gs_hbm, gs_ref, gs_sems)
+    ls_in = fetch(ls_hbm, ls_ref, ls_sems)
+    xc_in = fetch(xc_hbm, xc_ref, xc_sems)
+    dy_in = fetch(dy_hbm, dy_ref, dy_sems)
     state, dstate = state_of(st_ref, 0), state_of(st_ref, 1)
     b_matrix, c_matrix = bcc_ref[:, 0:LANES], bcc_ref[:, LANES:]
     leave_step, leaving, entering, along_dt, z_diff, carry, decay, dt_gate = [
@@ -337,23 +376,30 @@
     along_leave = jnp.zeros((heads, rows), F32)
     along_enter = jnp.zeros((heads, rows), F32)
     ext[rows:, :] = halo_ref[:, 0:channels]
+    sent = []
     for slab in range(channels // LANES):
-        lanes = slice(slab * LANES, (slab + 1) * LANES)
+        lanes = lanes_of(slab)
+        at = (slice(None), lanes)
         y_state = dot(c_matrix, state[lanes], ((1,), (1,)))
         d_leaving = dot(b_matrix, dstate[lanes], ((1,), (1,)))
-        y_ref[:, lanes] = (yi_ref[:, lanes] + spread(entering, slab, head_dim) * y_state).astype(BF16)
-        along_leave = along_leave + head_sum(
-            xc_ref[:, lanes].astype(F32) * d_leaving, slab, head_dim, heads
-        )
-        along_enter = along_enter + head_sum(
-            dy_ref[:, lanes].astype(F32) * y_state, slab, head_dim, heads
-        )
-        ext[0:rows, lanes] = gs_ref[:, lanes] + ls_ref[:, lanes] * d_leaving
+        yi_in[slab].wait()
+        y_ref[at] = (yi_ref[at] + spread(entering, slab, head_dim) * y_state).astype(BF16)
+        sent.append(put(y_ref, y_hbm, out_sems.at[2 * slab], at))
+        gs_in[slab].wait()
+        ls_in[slab].wait()
+        ext[0:rows, lanes] = gs_ref[at] + ls_ref[at] * d_leaving
         w = wx_ref[:, lanes].astype(F32)
         out = w[taps - 1 : taps] * ext[0:rows, lanes]
         for tap in range(taps - 1):
             out = out + w[tap : tap + 1] * ext[pl.ds(taps - 1 - tap, rows), lanes]
-        gx_ref[:, lanes] = out.astype(BF16)
+        gx_ref[at] = out.astype(BF16)
+        sent.append(put(gx_ref, gx_hbm, out_sems.at[2 * slab + 1], at))
+        xc_in[slab].wait()
+        dy_in[slab].wait()
+        along_leave = along_leave + head_sum(
+            xc_ref[at].astype(F32) * d_leaving, slab, head_dim, heads
+        )
+        along_enter = along_enter + head_sum(dy_ref[at].astype(F32) * y_state, slab, head_dim, heads)
     product = state.astype(F32) * dstate.astype(F32)
     owner = iota((heads, channels), 1) // head_dim
     chosen = jnp.where(iota((heads, channels), 0) == owner, 1.0, 0.0)
@@ -365,32 +411,36 @@
     after = jnp.where(iota((rows, rows), 0) >= iota((rows, rows), 1), 1.0, 0.0)
     d_log = dot(d_cum, after, ((1,), (0,)), HIGHEST)
     gdt_ref[...] = (along_dt + leaving * along_leave - decay * d_log) * dt_gate
+    for copy in sent:
+        copy.wait()
 
 
 def smem():
     return pl.BlockSpec(memory_space=pltpu.SMEM)
 
 
-def whole(shape):
-    return pl.BlockSpec(shape, lambda i: (0,) * len(shape))
-
-
-def call(kernel, name, out, scalars, arrays, scratch=(), blocks=None):
-    blocks = blocks or {}
-    many = isinstance(out, list)
-    out = [jax.ShapeDtypeStruct(s, d) for s, d in (out if many else [out])]
-    specs = [whole(o.shape) for o in out]
+def vmem():
+    return pl.BlockSpec(memory_space=pltpu.VMEM)
+
+
+def hbm():
+    return pl.BlockSpec(memory_space=pltpu.HBM)
+
+
+def call(kernel, name, scalars, far, near, far_out, near_out, scratch=()):
+    far = [pltpu.with_memory_space_constraint(a, pltpu.HBM) for a in far]
+    out = [pltpu.HBM(s, d) for s, d in far_out] + [jax.ShapeDtypeStruct(s, d) for s, d in near_out]
+    specs = [hbm() for _ in far_out] + [vmem() for _ in near_out]
+    many = len(out) > 1
     return pl.pallas_call(
         kernel,
         name=name,
         out_shape=out if many else out[0],
-        grid=(1,),
-        in_specs=[smem() for _ in scalars]
-        + [whole(blocks.get(i, a.shape)) for i, a in enumerate(arrays)],
+        in_specs=[smem() for _ in scalars] + [hbm() for _ in far] + [vmem() for _ in near],
         out_specs=specs if many else specs[0],
         scratch_shapes=list(scratch),
         compiler_params=pltpu.CompilerParams(vmem_limit_bytes=VMEM_LIMIT),
-    )(*scalars, *arrays)
+    )(*scalars, *far, *near)
 
 
 def shift_ctx(values, by):
@@ -418,55 +468,81 @@
     part = channels // count
     core = (lax.axis_index("head") % 2).astype(jnp.int32).reshape(1)
     halo = shift_ctx(jnp.concatenate([x_raw[rows - RIM :], bc_raw[rows - RIM :]], axis=1), 1)
+    slabs = channels // LANES
+    wide_bf, wide_f = ((rows, channels), BF16), ((rows, channels), F32)
+    sems = pltpu.SemaphoreType.DMA
+    inputs = [pltpu.VMEM(*wide_bf), pltpu.VMEM(*wide_bf), pltpu.VMEM((rows, wide), BF16)]
+    input_sems = [sems((slabs,)), sems((slabs,)), sems((wide // LANES,))]
     ext = pltpu.VMEM((rows + RIM, channels + wide), F32)
+    sent = ((count, 2 * part + RIM, LANES), BF16)
+    states = ((count, 2 * part, LANES), BF16)
     send = call(
         functools.partial(send_kernel, head_dim),
         "send",
-        ((count, 2 * part + RIM, LANES), BF16),
         [doc_starts, a_log],
-        [x_raw, halo, bc_raw, conv_x_w, conv_bc_w, dt_raw, grad_y],
-        [ext],
+        [x_raw, grad_y, bc_raw],
+        [halo, conv_x_w, conv_bc_w, dt_raw],
+        [sent],
+        [],
+        [*inputs, pltpu.VMEM(*sent), ext, *input_sems, sems((slabs,))],
     )
     got = lax.all_to_all(send, "ctx", 0, 0)
-    xc, lx, edy, bcc, yi, gs, ls, gbc, sbc, hv = call(
+    xc, yi, gs, ls, lx, edy, bcc, gbc, sbc, hv, first = call(
         functools.partial(intra_kernel, head_dim),
         "intra",
+        [doc_starts, a_log, d_skip],
+        [x_raw, grad_y, bc_raw],
+        [halo, conv_x_w, conv_bc_w, dt_raw],
+        [wide_bf, wide_f, wide_f, wide_f],
         [
-            ((rows, channels), BF16),
-            ((rows, channels), BF16),
-            ((rows, channels), BF16),
+            wide_bf,
+            wide_bf,
             ((rows, wide), BF16),
-            ((rows, channels), F32),
-            ((rows, channels), F32),
-            ((rows, channels), F32),
             ((rows, wide), F32),
             ((rows, wide), F32),
             ((8, heads, rows), F32),
+            ((2, RIM, channels), F32),
         ],
-        [doc_starts, a_log, d_skip],
-        [x_raw, halo, bc_raw, conv_x_w, conv_bc_w, dt_raw, grad_y],
-        [ext, pltpu.VMEM((rows, rows), F32), pltpu.VMEM((rows, rows), F32)],
-    )
-    scanned = call(scan_kernel, "scan", ((count, 2 * part, LANES), BF16), [], [got])
+        [
+            *inputs,
+            pltpu.VMEM(*wide_bf),
+            pltpu.VMEM(*wide_f),
+            pltpu.VMEM(*wide_f),
+            pltpu.VMEM(*wide_f),
+            ext,
+            pltpu.VMEM((rows, rows), F32),
+            pltpu.VMEM((rows, rows), F32),
+            *input_sems,
+            sems((4 * slabs,)),
+        ],
+    )
+    got, hv = lax.optimization_barrier((got, hv))
+    scanned = call(
+        scan_kernel, "scan", [], [], [got], [states], [], [pltpu.VMEM(*states), sems((count // 4,))]
+    )
     st = lax.all_to_all(scanned, "ctx", 0, 0)
     half = rows // 2
     keep, give, rim = call(
         bc_kernel,
         "grad_bc",
+        [core],
+        [],
+        [st, lx, edy, bcc, gbc, sbc, first, conv_bc_w],
+        [],
         [((half, wide), F32), ((half, wide), BF16), ((RIM, channels + wide), F32)],
-        [core],
-        [st, lx, edy, bcc, gbc, sbc, gs, ls, conv_bc_w],
         [pltpu.VMEM((rows + RIM, wide), F32), pltpu.VMEM((rows, wide), F32)],
-        {3: (2 * RIM, LANES), 6: (RIM, channels), 7: (RIM, channels)},
     )
     next_rim = shift_ctx(rim, -1)
     other = swap_core(give)
+    message = ((half + RIM, wide), BF16)
     joined = call(
         join_kernel,
         "join",
-        ((half + RIM, wide), BF16),
+        [],
         [],
         [keep, other, next_rim, conv_bc_w],
+        [],
+        [message],
         [pltpu.VMEM((2 * RIM, wide), F32)],
     )
     ring = lax.axis_size("head") // 2
@@ -474,19 +550,35 @@
     y_out, grad_x, grad_dt = call(
         functools.partial(out_kernel, head_dim),
         "out",
-        [((rows, channels), BF16), ((rows, channels), BF16), ((heads, rows), F32)],
-        [],
-        [st, xc, grad_y, bcc, yi, gs, ls, hv, next_rim, conv_x_w],
-        [pltpu.VMEM((rows + RIM, channels), F32)],
-    )
-    summed = call(sum_kernel, "sum", ((half + RIM, wide), BF16), [], pieces)
+        [],
+        [xc, grad_y, yi, gs, ls],
+        [st, bcc, hv, next_rim, conv_x_w],
+        [wide_bf, wide_bf],
+        [((heads, rows), F32)],
+        [
+            pltpu.VMEM(*wide_bf),
+            pltpu.VMEM(*wide_bf),
+            pltpu.VMEM(*wide_f),
+            pltpu.VMEM(*wide_f),
+            pltpu.VMEM(*wide_f),
+            pltpu.VMEM(*wide_bf),
+            pltpu.VMEM(*wide_bf),
+            pltpu.VMEM((rows + RIM, channels), F32),
+            *[sems((slabs,)) for _ in range(5)],
+            sems((2 * slabs,)),
+        ],
+    )
+    pieces, grad_dt = lax.optimization_barrier((pieces, grad_dt))
+    summed = call(sum_kernel, "sum", [], [], pieces, [], [message])
     swapped = swap_core(summed)
     grad_bc = call(
         last_kernel,
         "last",
-        ((rows, wide), BF16),
         [core],
+        [],
         [summed, swapped],
+        [],
+        [((rows, wide), BF16)],
         [pltpu.VMEM((rows, wide), F32)],
     )
     return (y_out, grad_x, grad_bc, grad_dt)

time: 94.7 us -> 89.8 us (0.948)
  blocking collectives: 27.6 us -> 0 us
  waiting for transfers between devices: 9.15 us -> 25.8 us
  local copies, waits for them, and re-layouts: 15 us -> 0.73 us
  starting transfers between devices: 22.5 us -> 34 us
  Pallas kernels: 18.2 us -> 27 us
    all_to_all x1 -> x0, blocking collectives: 27.6 us -> none  [body(): got = lax.all_to_all(send, 'ctx', 0, 0)]
    all_to_all x1, waiting for transfers between devices: 0.01 us -> 14.6 us  [body(): st = lax.all_to_all(scanned, 'ctx', 0, 0)]
    unnamed x52 -> x10, local copies, waits for them, and re-layouts: 14.3 us -> 0.02 us
    all_to_all x0 -> x1, starting transfers between devices: none -> 11.9 us  [body(): got = lax.all_to_all(send, 'ctx', 0, 0)]
    pallas_call x8, Pallas kernels: 18.2 us -> 27 us  [call(): pl.pallas_call(kernel, name=name, out_shape=out if many else out[0], in_s...]
    all_to_all x0 -> x1, waiting for transfers between devices: none -> 5.46 us  [body(): got = lax.all_to_all(send, 'ctx', 0, 0)]
    ppermute x3, waiting for transfers between devices: 4.37 us -> 0.01 us  [around(): lax.ppermute(values, 'head', [(i, (i + 2 * by) % size) for i in range(siz...]
  transfers between devices with their start and end apart: 8 -> 9, of which waited for: 5 -> 5; matrix products, arithmetic and copies ran while one was open for 0% -> 0% of each run, Pallas kernels for 13% -> 20%
where the time goes in v2:
time: 89.8 us; the launch traced here: 89 us
  starting transfers between devices  34 us (38%)
  Pallas kernels  27 us (30%)
  waiting for transfers between devices  25.8 us (29%)
  between operations  1.46 us (2%)
    pallas_call x8, Pallas kernels, call(): pl.pallas_call(kernel, name=name, out_shape=out if many else out[0], in_s...  27 us
    all_to_all x1, waiting for transfers between devices, body(): st = lax.all_to_all(scanned, 'ctx', 0, 0)  14.6 us
    all_to_all x1, starting transfers between devices, body(): got = lax.all_to_all(send, 'ctx', 0, 0)  11.9 us
    all_to_all x1, starting transfers between devices, body(): st = lax.all_to_all(scanned, 'ctx', 0, 0)  6.63 us
    ppermute x2, starting transfers between devices, shift_ctx(): return lax.ppermute(values, 'ctx', pairs)  6.06 us
    ppermute x2, starting transfers between devices, swap_core(): return lax.ppermute(values, 'head', [(i, i ^ 1) for i in range(size)])  5.62 us
    all_to_all x1, waiting for transfers between devices, body(): got = lax.all_to_all(send, 'ctx', 0, 0)  5.46 us
    ppermute x2, waiting for transfers between devices, shift_ctx(): return lax.ppermute(values, 'ctx', pairs)  4.77 us
  transfers between devices with their start and end apart: 9, of which 5 were waited for; matrix products, arithmetic and copies ran while one was open for 0% of the time, Pallas kernels for 20%

profile of v2, /device:TPU:7, one launch (start us, length us, event | category | flops | bytes accessed | tf_op | source)
XLA Modules:
  0.0 89.0 jit_solution(4193435597823976060)
XLA Ops:
  0.6 0.0 slice-start
  0.6 0.0 slice-start.1
  0.7 0.7 slice-done
  1.4 0.0 slice-done.1
  1.4 0.0 copy-start
  1.4 0.0 copy-start.1
  1.4 0.0 copy-start.2
  1.4 0.0 copy-start.3
  1.4 3.6 %collective-permute-start = (bf16[8,1280]{1,0:T(8,128)(2,1)S(1)}, bf16[8,1280]{1,0:T(8,128)(2,1)S(1)}, u32[]{:S(2)}, u32[]{:S(2)}) collective-permute-start(bf16[8,1280]{1,0:T(8,128)(2,1)S(1)} %pad_maximum_fusion), channel_id=1, source_target_pairs={{0,8},{8,16},{16,24},{24,32},{32,40},{40,48},{48,56},{56,64},{64,7... | collective-permute-start | bytes 61448 | tf_op jit(solution)/shard_map/ppermute | solution.py:449
  5.6 0.4 collective-permute-done.halo_ref
  6.0 0.0 copy-done
  6.1 0.0 copy-done.1
  6.1 0.0 copy-done.2
  6.1 0.0 copy-done.3
  6.1 7.1 %send.1 = bf16[32,72,128]{2,1,0:T(8,128)(2,1)} custom-call(s32[1]{0:T(128)S(6)} %copy.13.doc_ref, f32[16]{0:T(128)S(1)} %copy-done.3, bf16[256,1024]{1,0:T(8,128)(2,1)} %x_hbm.3, bf16[256,1024]{1,0:T(8,128)(2,1)} %dy_hbm.5, bf16[256,256]{1,0:T(8,128)(2,1)} %bc_hbm.3, bf16[8,1280]{1,0:T(8,128)(2,1)S(1)} %collective-permute-done.halo_ref, ...), custom_call_target="tpu_custom_call" | custom-call | tf_op jit(solution)/shard_map/send/pallas_call | solution.py:435
  13.2 0.0 copy-start.4
  13.2 11.9 %all-to-all-start = ((bf16[32,72,128]{2,1,0:T(8,128)(2,1)}), bf16[32,72,128]{2,1,0:T(8,128)(2,1)S(1)}, u32[]{:S(2)}, u32[]{:S(2)}) async-start(bf16[32,72,128]{2,1,0:T(8,128)(2,1)} %send.1), calls=%async_computation | async-start | bytes 1179648 | tf_op jit(solution)/shard_map/all_to_all | solution.py:489
  25.1 0.0 copy-done.4
  25.1 10.5 %intra.1 = (bf16[256,1024]{1,0:T(8,128)(2,1)}, f32[256,1024]{1,0:T(8,128)}, f32[256,1024]{1,0:T(8,128)}, f32[256,1024]{1,0:T(8,128)}, bf16[256,1024]{1,0:T(8,128...) custom-call(s32[1]{0:T(128)S(6)} %copy.13.doc_ref, ...), custom_call_target="tpu_custom_call" | custom-call | tf_op jit(solution)/shard_map/intra/pallas_call | solution.py:435
  35.6 5.5 %all-to-all-done.got_ref = bf16[32,72,128]{2,1,0:T(8,128)(2,1)S(1)} async-done(((bf16[32,72,128]{2,1,0:T(8,128)(2,1)}), bf16[32,72,128]{2,1,0:T(8,128)(2,1)S(1)}, u32[]{:S(2)}, u32[]{:S(2)}) %all-to-all-start) | async-done | bytes 589856 | tf_op jit(solution)/shard_map/all_to_all | solution.py:489
  41.0 0.9 %scan.1 = bf16[32,64,128]{2,1,0:T(8,128)(2,1)} custom-call(bf16[32,72,128]{2,1,0:T(8,128)(2,1)S(1)} %all-to-all-done.got_ref), custom_call_target="tpu_custom_call" | custom-call | tf_op jit(solution)/shard_map/scan/pallas_call | solution.py:435
  42.0 6.6 %all-to-all-start.1 = ((bf16[32,64,128]{2,1,0:T(8,128)(2,1)}), bf16[32,64,128]{2,1,0:T(8,128)(2,1)S(1)}, u32[]{:S(2)}, u32[]{:S(2)}) async-start(bf16[32,64,128]{2,1,0:T(8,128)(2,1)} %scan.1), calls=%async_computation.1 | async-start | bytes 1048576 | tf_op jit(solution)/shard_map/all_to_all | solution.py:523
  48.6 14.6 %all-to-all-done.1.st_ref = bf16[32,64,128]{2,1,0:T(8,128)(2,1)S(1)} async-done(((bf16[32,64,128]{2,1,0:T(8,128)(2,1)}), bf16[32,64,128]{2,1,0:T(8,128)(2,1)S(1)}, u32[]{:S(2)}, u32[]{:S(2)}) %all-to-all-start.1) | async-done | bytes 524320 | tf_op jit(solution)/shard_map/all_to_all | solution.py:523
  63.3 0.5 grad_bc.1
  63.8 3.5 %collective-permute-start.2 = (bf16[128,256]{1,0:T(8,128)(2,1)S(1)}, bf16[128,256]{1,0:T(8,128)(2,1)S(1)}, u32[]{:S(2)}, u32[]{:S(2)}) collective-permute-start(bf16[128,256]{1,0:T(8,128)(2,1)S(1)} %get-tuple-element.45), channel_id=1, source_target_pairs={{0,1},{1,0},{2,3},{3,2},{4,5},{5,4},{6,7},{7,6},{8,9},{9,8},{10,11... | collective-permute-start | bytes 196616 | tf_op jit(solution)/shard_map/ppermute | solution.py:454
  67.3 2.5 %collective-permute-start.1 = (f32[8,1280]{1,0:T(8,128)S(1)}, f32[8,1280]{1,0:T(8,128)S(1)}, u32[]{:S(2)}, u32[]{:S(2)}) collective-permute-start(f32[8,1280]{1,0:T(8,128)S(1)} %get-tuple-element.41), channel_id=1, source_target_pairs={{8,0},{16,8},{24,16},{32,24},{40,32},{48,40},{56,48},{64,56},{72,6... | collective-permute-start | bytes 122888 | tf_op jit(solution)/shard_map/ppermute | solution.py:449
  69.8 4.4 %collective-permute-done.1.halo_ref = f32[8,1280]{1,0:T(8,128)S(1)} collective-permute-done((f32[8,1280]{1,0:T(8,128)S(1)}, f32[8,1280]{1,0:T(8,128)S(1)}, u32[]{:S(2)}, u32[]{:S(2)}) %collective-permute-start.1) | collective-permute-done | bytes 40992 | tf_op jit(solution)/shard_map/ppermute | solution.py:449
  74.1 0.0 collective-permute-done.2.got_ref
  74.2 2.8 %collective-permute-start.5 = (bf16[136,256]{1,0:T(8,128)(2,1)S(1)}, bf16[136,256]{1,0:T(8,128)(2,1)S(1)}, u32[]{:S(2)}, u32[]{:S(2)}) collective-permute-start(bf16[136,256]{1,0:T(8,128)(2,1)S(1)} %join.1.refs_0_), channel_id=1, source_target_pairs={{0,6},{1,7},{2,0},{3,1},{4,2},{5,3},{6,4},{7,5},{8,14},{9,15},{10,... | collective-permute-start | bytes 208904 | tf_op jit(solution)/shard_map/ppermute | solution.py:459
  77.0 0.3 collective-permute-start.4
  77.3 0.7 collective-permute-start.3
  78.0 7.2 %out.1 = (bf16[256,1024]{1,0:T(8,128)(2,1)}, bf16[256,1024]{1,0:T(8,128)(2,1)}, f32[16,256]{1,0:T(8,128)}) custom-call(bf16[256,1024]{1,0:T(8,128)(2,1)} %get-tuple-element.28.xc_hbm, bf16[256,1024]{1,0:T(8,128)(2,1)} %dy_hbm.5, f32[256,1024]{1,0:T(8,128)} %get-tuple-element.29.yi_hbm, f32[256,1024]{1,0:T(8,128)} %get-tuple-element.30.gs_hbm, ...), custom_call_target="tpu_custom_call" | custom-call | tf_op jit(solution)/shard_map/out/pallas_call | solution.py:435
  85.2 0.0 collective-permute-done.5.refs_3_
  85.2 0.0 collective-permute-done.4.refs_2_
  85.2 0.0 collective-permute-done.3.refs_1_
  85.3 2.1 %collective-permute-start.6 = (bf16[136,256]{1,0:T(8,128)(2,1)S(1)}, bf16[136,256]{1,0:T(8,128)(2,1)S(1)}, u32[]{:S(2)}, u32[]{:S(2)}) collective-permute-start(bf16[136,256]{1,0:T(8,128)(2,1)S(1)} %sum.1.mine_ref), channel_id=1, source_target_pairs={{0,1},{1,0},{2,3},{3,2},{4,5},{5,4},{6,7},{7,6},{8,9},{9,8},{10,11... | collective-permute-start | bytes 208904 | tf_op jit(solution)/shard_map/ppermute | solution.py:454
  87.4 0.9 %collective-permute-done.6.got_ref = bf16[136,256]{1,0:T(8,128)(2,1)S(1)} collective-permute-done((bf16[136,256]{1,0:T(8,128)(2,1)S(1)}, bf16[136,256]{1,0:T(8,128)(2,1)S(1)}, u32[]{:S(2)}, u32[]{:S(2)}) %collective-permute-start.6) | collective-permute-done | bytes 69664 | tf_op jit(solution)/shard_map/ppermute | solution.py:454
  88.3 0.7 last.1
  (3 shorter events, 0.1 us)
Async XLA Ops:
  0.6 0.7 slice-start
  0.6 0.7 slice-start.1
  1.4 4.7 %copy-start = (bf16[4,1024]{1,0:T(4,128)(2,1)S(1)}, bf16[4,1024]{1,0:T(4,128)(2,1)}, u32[]{:S(2)}) copy-start(bf16[4,1024]{1,0:T(4,128)(2,1)} %wx_ref.5) | copy-start | bytes 24580
  1.4 4.7 %copy-start.1 = (f32[16,256]{1,0:T(8,128)S(1)}, f32[16,256]{1,0:T(8,128)}, u32[]{:S(2)}) copy-start(f32[16,256]{1,0:T(8,128)} %dt_ref.3) | copy-start | bytes 49156
  1.4 4.7 %copy-start.2 = (bf16[4,256]{1,0:T(4,128)(2,1)S(1)}, bf16[4,256]{1,0:T(4,128)(2,1)}, u32[]{:S(2)}) copy-start(bf16[4,256]{1,0:T(4,128)(2,1)} %wbc_ref.7) | copy-start | bytes 6148
  1.4 4.7 %copy-start.3 = (f32[16]{0:T(128)S(1)}, f32[16]{0:T(128)}, u32[]{:S(2)}) copy-start(f32[16]{0:T(128)} %a_log_ref.3) | copy-start | bytes 196
  1.4 4.7 %collective-permute-start = (bf16[8,1280]{1,0:T(8,128)(2,1)S(1)}, bf16[8,1280]{1,0:T(8,128)(2,1)S(1)}, u32[]{:S(2)}, u32[]{:S(2)}) collective-permute-start(bf16[8,1280]{1,0:T(8,128)(2,1)S(1)} %pad_maximum_fusion), channel_id=1, source_target_pairs={{0,8},{8,16},{16,24},{24,32},{32,40},{40,48},{48,56},{56,64},{64,7... | collective-permute-start | bytes 61448 | tf_op jit(solution)/shard_map/ppermute | solution.py:449
  13.2 11.9 %copy-start.4 = (f32[16]{0:T(128)S(1)}, f32[16]{0:T(128)}, u32[]{:S(2)}) copy-start(f32[16]{0:T(128)} %skip_ref.1) | copy-start | bytes 196
  13.2 27.9 %all-to-all-start = ((bf16[32,72,128]{2,1,0:T(8,128)(2,1)}), bf16[32,72,128]{2,1,0:T(8,128)(2,1)S(1)}, u32[]{:S(2)}, u32[]{:S(2)}) async-start(bf16[32,72,128]{2,1,0:T(8,128)(2,1)} %send.1), calls=%async_computation | async-start | bytes 1179648 | tf_op jit(solution)/shard_map/all_to_all | solution.py:489
  42.0 21.3 %all-to-all-start.1 = ((bf16[32,64,128]{2,1,0:T(8,128)(2,1)}), bf16[32,64,128]{2,1,0:T(8,128)(2,1)S(1)}, u32[]{:S(2)}, u32[]{:S(2)}) async-start(bf16[32,64,128]{2,1,0:T(8,128)(2,1)} %scan.1), calls=%async_computation.1 | async-start | bytes 1048576 | tf_op jit(solution)/shard_map/all_to_all | solution.py:523
  63.8 10.4 %collective-permute-start.2 = (bf16[128,256]{1,0:T(8,128)(2,1)S(1)}, bf16[128,256]{1,0:T(8,128)(2,1)S(1)}, u32[]{:S(2)}, u32[]{:S(2)}) collective-permute-start(bf16[128,256]{1,0:T(8,128)(2,1)S(1)} %get-tuple-element.45), channel_id=1, source_target_pairs={{0,1},{1,0},{2,3},{3,2},{4,5},{5,4},{6,7},{7,6},{8,9},{9,8},{10,11... | collective-permute-start | bytes 196616 | tf_op jit(solution)/shard_map/ppermute | solution.py:454
  67.3 6.8 %collective-permute-start.1 = (f32[8,1280]{1,0:T(8,128)S(1)}, f32[8,1280]{1,0:T(8,128)S(1)}, u32[]{:S(2)}, u32[]{:S(2)}) collective-permute-start(f32[8,1280]{1,0:T(8,128)S(1)} %get-tuple-element.41), channel_id=1, source_target_pairs={{8,0},{16,8},{24,16},{32,24},{40,32},{48,40},{56,48},{64,56},{72,6... | collective-permute-start | bytes 122888 | tf_op jit(solution)/shard_map/ppermute | solution.py:449
  74.2 11.0 %collective-permute-start.5 = (bf16[136,256]{1,0:T(8,128)(2,1)S(1)}, bf16[136,256]{1,0:T(8,128)(2,1)S(1)}, u32[]{:S(2)}, u32[]{:S(2)}) collective-permute-start(bf16[136,256]{1,0:T(8,128)(2,1)S(1)} %join.1.refs_0_), channel_id=1, source_target_pairs={{0,6},{1,7},{2,0},{3,1},{4,2},{5,3},{6,4},{7,5},{8,14},{9,15},{10,... | collective-permute-start | bytes 208904 | tf_op jit(solution)/shard_map/ppermute | solution.py:459
  77.0 8.2 %collective-permute-start.4 = (bf16[136,256]{1,0:T(8,128)(2,1)S(1)}, bf16[136,256]{1,0:T(8,128)(2,1)S(1)}, u32[]{:S(2)}, u32[]{:S(2)}) collective-permute-start(bf16[136,256]{1,0:T(8,128)(2,1)S(1)} %join.1.refs_0_), channel_id=1, source_target_pairs={{0,4},{1,5},{2,6},{3,7},{4,0},{5,1},{6,2},{7,3},{8,12},{9,13},{10,... | collective-permute-start | bytes 208904 | tf_op jit(solution)/shard_map/ppermute | solution.py:459
  77.3 7.9 %collective-permute-start.3 = (bf16[136,256]{1,0:T(8,128)(2,1)S(1)}, bf16[136,256]{1,0:T(8,128)(2,1)S(1)}, u32[]{:S(2)}, u32[]{:S(2)}) collective-permute-start(bf16[136,256]{1,0:T(8,128)(2,1)S(1)} %join.1.refs_0_), channel_id=1, source_target_pairs={{0,2},{1,3},{2,4},{3,5},{4,6},{5,7},{6,0},{7,1},{8,10},{9,11},{10,... | collective-permute-start | bytes 208904 | tf_op jit(solution)/shard_map/ppermute | solution.py:459
  85.3 3.0 %collective-permute-start.6 = (bf16[136,256]{1,0:T(8,128)(2,1)S(1)}, bf16[136,256]{1,0:T(8,128)(2,1)S(1)}, u32[]{:S(2)}, u32[]{:S(2)}) collective-permute-start(bf16[136,256]{1,0:T(8,128)(2,1)S(1)} %sum.1.mine_ref), channel_id=1, source_target_pairs={{0,1},{1,0},{2,3},{3,2},{4,5},{5,4},{6,7},{7,6},{8,9},{9,8},{10,11... | collective-permute-start | bytes 208904 | tf_op jit(solution)/shard_map/ppermute | solution.py:454

commit v3 on v2

--- a/solution.py
+++ b/solution.py
@@ -83,12 +83,20 @@
 
 
 def fetch(source, target, sems):
-    copies = []
-    for slab in range(source.shape[1] // LANES):
-        part = (slice(None), lanes_of(slab))
-        copies.append(pltpu.make_async_copy(source.at[part], target.at[part], sems.at[slab]))
-        copies[-1].start()
+    pieces = sems.shape[0]
+    width = source.shape[1] // pieces
+    copies = {}
+    for piece in range(pieces):
+        at = (slice(None), slice(piece * width, (piece + 1) * width))
+        copy = pltpu.make_async_copy(source.at[at], target.at[at], sems.at[piece])
+        copy.start()
+        copies[piece * width // LANES] = copy
     return copies
+
+
+def arrived(copies, slab):
+    if slab in copies:
+        copies[slab].wait()
 
 
 def put(source, target, sem, at):
@@ -98,7 +106,10 @@
 
 
 def load_ext(ext, halo_ref, values, at, lanes):
-    ext[0:RIM, at] = halo_ref[:, at].astype(F32)
+    if halo_ref is None:
+        ext[0:RIM, at] = jnp.zeros((RIM, LANES), F32)
+    else:
+        ext[0:RIM, at] = halo_ref[:, at].astype(F32)
     ext[RIM : RIM + values.shape[0], at] = values[:, lanes].astype(F32)
 
 
@@ -112,13 +123,12 @@
     return total
 
 
-def send_kernel(
-    head_dim, doc_ref, a_log_ref, x_hbm, dy_hbm, bc_hbm, halo_ref, wx_ref, wbc_ref, dt_ref,
-    send_hbm, x_ref, dy_ref, bc_ref, send_ref, ext, x_sems, dy_sems, bc_sems, out_sems,
+def gather_kernel(
+    head_dim, part, doc_ref, a_log_ref, x_hbm, dy_hbm, bc_hbm, wx_ref, wbc_ref, dt_ref,
+    sum_ref, ls_ref, edy_ref, top_ref, tail_ref,
+    x_ref, dy_ref, bc_ref, ext, x_sems, dy_sems, bc_sems,
 ):
     rows, channels = x_ref.shape
-    part = channels // send_ref.shape[0]
-    per_slab = LANES // part
     bc_in = fetch(bc_hbm, bc_ref, bc_sems)
     x_in = fetch(x_hbm, x_ref, x_sems)
     dy_in = fetch(dy_hbm, dy_ref, dy_sems)
@@ -126,36 +136,74 @@
     leave_step = v["leaving"] * v["step"]
     high, low = halves(v["carry"][:, 0:LANES])
     at = iota((RIM, LANES), 0)
+    below = iota((rows, LANES), 0) >= RIM
+    for chunk in range(tail_ref.shape[0]):
+        head = chunk * part // head_dim
+        tile = jnp.where(
+            at == 0,
+            high[head : head + 1].astype(F32),
+            jnp.where(at == 1, low[head : head + 1].astype(F32), 0.0),
+        )
+        tail_ref[chunk] = tile.astype(BF16)
     bc = []
     for half in range(2):
-        bc_in[half].wait()
-        load_ext(ext, halo_ref, bc_ref, lanes_of(channels // LANES + half), lanes_of(half))
+        arrived(bc_in, half)
+        load_ext(ext, None, bc_ref, lanes_of(channels // LANES + half), lanes_of(half))
         pre = filtered(ext, wbc_ref, channels + half * LANES, half * LANES, rows)
         bc.append((pre * sigmoid(pre)).astype(BF16))
-    sent = []
     for slab in range(channels // LANES):
         lanes = lanes_of(slab)
-        x_in[slab].wait()
-        load_ext(ext, halo_ref, x_ref, lanes, lanes)
+        arrived(x_in, slab)
+        load_ext(ext, None, x_ref, lanes, lanes)
         pre = filtered(ext, wx_ref, slab * LANES, slab * LANES, rows)
         x_conv = (pre * sigmoid(pre)).astype(BF16).astype(F32)
-        leaving_x = (x_conv * spread(leave_step, slab, head_dim)).astype(BF16)
-        dy_in[slab].wait()
-        enter_dy = (dy_ref[:, lanes].astype(F32) * spread(v["entering"], slab, head_dim)).astype(BF16)
-        forward = dot(leaving_x, bc[0], ((0,), (0,))).astype(BF16)
-        backward = dot(enter_dy, bc[1], ((0,), (0,))).astype(BF16)
+        leave = spread(leave_step, slab, head_dim)
+        leaving_x = jnp.where(below, x_conv * leave, 0.0).astype(BF16)
+        arrived(dy_in, slab)
+        enter_dy = dy_ref[:, lanes].astype(F32) * spread(v["entering"], slab, head_dim)
+        sum_ref[0, lanes, :] = dot(leaving_x, bc[0], ((0,), (0,)))
+        sum_ref[1, lanes, :] = dot(jnp.where(below, enter_dy, 0.0).astype(BF16), bc[1], ((0,), (0,)))
+        ls_ref[:, lanes] = leave[0:RIM]
+        edy_ref[:, lanes] = enter_dy[0:RIM]
+    top_ref[...] = ext[RIM : 2 * RIM, :]
+
+
+def send_kernel(
+    halo_ref, sum_ref, ls_ref, edy_ref, top_ref, tail_ref, wx_ref, wbc_ref,
+    send_hbm, send_ref, ext, sems,
+):
+    channels = ls_ref.shape[1]
+    part = channels // send_ref.shape[0]
+    per_slab = LANES // part
+    ext[0:RIM, :] = halo_ref[...].astype(F32)
+    ext[RIM:, :] = top_ref[...]
+    none = jnp.zeros((RIM, LANES), F32)
+
+    def conv(w_ref, at, w_at):
+        pre = filtered(ext, w_ref, at, w_at, RIM)
+        return (pre * sigmoid(pre)).astype(BF16).astype(F32)
+
+    bc = [
+        jnp.concatenate([conv(wbc_ref, channels + at, at), none], axis=0).astype(BF16)
+        for at in (0, LANES)
+    ]
+    slabs = channels // LANES
+    sent = []
+    for slab in range(slabs):
+        lanes = lanes_of(slab)
+        leaving_x = conv(wx_ref, slab * LANES, slab * LANES) * ls_ref[:, lanes]
+        leaving_x = jnp.concatenate([leaving_x, none], axis=0).astype(BF16)
+        enter_dy = jnp.concatenate([edy_ref[:, lanes], none], axis=0).astype(BF16)
+        forward = (sum_ref[0, lanes, :] + dot(leaving_x, bc[0], ((0,), (0,)))).astype(BF16)
+        backward = (sum_ref[1, lanes, :] + dot(enter_dy, bc[1], ((0,), (0,)))).astype(BF16)
         own = slice(slab * per_slab, (slab + 1) * per_slab)
         send_ref[own, 0:part, :] = forward.reshape(per_slab, part, LANES)
         send_ref[own, part : 2 * part, :] = backward.reshape(per_slab, part, LANES)
-        for chunk in range(slab * per_slab, (slab + 1) * per_slab):
-            head = chunk * part // head_dim
-            tile = jnp.where(
-                at == 0,
-                high[head : head + 1].astype(F32),
-                jnp.where(at == 1, low[head : head + 1].astype(F32), 0.0),
-            )
-            send_ref[chunk, 2 * part : 2 * part + RIM, :] = tile.astype(BF16)
-        sent.append(put(send_ref, send_hbm, out_sems.at[slab], (own,)))
+        send_ref[own, 2 * part : 2 * part + RIM, :] = tail_ref[own]
+        group = slabs // sems.shape[0]
+        if slab % group == group - 1:
+            ready = slice((slab + 1 - group) * per_slab, (slab + 1) * per_slab)
+            sent.append(put(send_ref, send_hbm, sems.at[slab // group], (ready,)))
     for copy in sent:
         copy.wait()
 
@@ -201,7 +249,7 @@
     v = head_values(doc_ref, a_log_ref, dt_ref)
     for half in range(2):
         lanes = lanes_of(half)
-        bc_in[half].wait()
+        arrived(bc_in, half)
         load_ext(ext, halo_ref, bc_ref, lanes_of(channels // LANES + half), lanes)
         pre = filtered(ext, wbc_ref, channels + half * LANES, half * LANES, rows)
         gate = sigmoid(pre)
@@ -224,9 +272,9 @@
     sent = []
     for slab in range(channels // LANES):
         lanes = lanes_of(slab)
-        x_in[slab].wait()
+        arrived(x_in, slab)
         load_ext(ext, halo_ref, x_ref, lanes, lanes)
-        dy_in[slab].wait()
+        arrived(dy_in, slab)
         pre = filtered(ext, wx_ref, slab * LANES, slab * LANES, rows)
         gate = sigmoid(pre)
         x_bf = (pre * gate).astype(BF16)
@@ -260,11 +308,13 @@
         ls_ref[:, lanes] = leave * silu_grad
         rim_ref[0, :, lanes] = gs_ref[0:RIM, lanes]
         rim_ref[1, :, lanes] = ls_ref[0:RIM, lanes]
-        at = (slice(None), lanes)
-        for which, (mine, out) in enumerate(
-            ((xc_ref, xc_hbm), (yi_ref, yi_hbm), (gs_ref, gs_hbm), (ls_ref, ls_hbm))
-        ):
-            sent.append(put(mine, out, out_sems.at[slab * 4 + which], at))
+        group = channels // LANES // (out_sems.shape[0] // 4)
+        if slab % group == group - 1:
+            at = (slice(None), slice((slab + 1 - group) * LANES, (slab + 1) * LANES))
+            for which, (mine, out) in enumerate(
+                ((xc_ref, xc_hbm), (yi_ref, yi_hbm), (gs_ref, gs_hbm), (ls_ref, ls_hbm))
+            ):
+                sent.append(put(mine, out, out_sems.at[slab // group * 4 + which], at))
         along_dt = along_dt + head_sum(x_conv * d_scaled, slab, head_dim, heads)
         z_diff = z_diff + head_sum(
             dy * intra - scaled.astype(F32) * d_scaled, slab, head_dim, heads
@@ -300,7 +350,6 @@
 ):
     rows = lx_ref.shape[0]
     taps = wbc_ref.shape[0]
-    channels = lx_ref.shape[1]
     state, dstate = state_of(st_ref, 0), state_of(st_ref, 1)
     grad_b = gbc_ref[:, 0:LANES] + dot(lx_ref[...], dstate, ((1,), (0,)))
     grad_c = gbc_ref[:, LANES:] + dot(edy_ref[...], state, ((1,), (0,)))
@@ -317,6 +366,7 @@
     keep_ref[...] = total[pl.ds(pl.multiple_of(core * half, half), half), :]
     give_ref[...] = total[pl.ds(pl.multiple_of((1 - core) * half, half), half), :].astype(BF16)
     d_leaving = dot(b_ref[0 : 2 * RIM, 0:LANES], dstate, ((1,), (1,)))[0:RIM]
+    channels = rim_ref.shape[2]
     halo_ref[:, 0:channels] = rim_ref[0] + rim_ref[1] * d_leaving
     halo_ref[:, channels:] = ext[0:RIM, :]
 
@@ -325,10 +375,9 @@
     half = keep_ref.shape[0]
     taps = wbc_ref.shape[0]
     wide = keep_ref.shape[1]
-    channels = halo_ref.shape[1] - wide
     out_ref[0:half, :] = (keep_ref[...] + got_ref[...].astype(F32)).astype(BF16)
     ext[0:RIM, :] = jnp.zeros((RIM, wide), F32)
-    ext[RIM:, :] = halo_ref[:, channels:]
+    ext[RIM:, :] = halo_ref[:, halo_ref.shape[1] - wide :]
     w = wbc_ref[...].astype(F32)
     rim = jnp.zeros((RIM, wide), F32)
     for tap in range(taps - 1):
@@ -354,52 +403,77 @@
     out_ref[...] = total[...].astype(BF16)
 
 
-def out_kernel(
-    head_dim, xc_hbm, dy_hbm, yi_hbm, gs_hbm, ls_hbm, st_ref, bcc_ref, hv_ref, halo_ref, wx_ref,
-    y_hbm, gx_hbm, gdt_ref,
-    xc_ref, dy_ref, yi_ref, gs_ref, ls_ref, y_ref, gx_ref, ext,
-    xc_sems, dy_sems, yi_sems, gs_sems, ls_sems, out_sems,
+def y_kernel(
+    head_dim, dy_hbm, yi_hbm, st_ref, bcc_ref, hv_ref,
+    y_hbm, enter_ref, dy_ref, yi_ref, y_ref, dy_sems, yi_sems, sems,
+):
+    rows, channels = dy_ref.shape
+    heads = hv_ref.shape[1]
+    slabs = channels // LANES
+    yi_in = fetch(yi_hbm, yi_ref, yi_sems)
+    dy_in = fetch(dy_hbm, dy_ref, dy_sems)
+    state = state_of(st_ref, 0)
+    c_matrix = bcc_ref[:, LANES:]
+    entering = hv_ref[2]
+    along_enter = jnp.zeros((heads, rows), F32)
+    sent = []
+    for slab in range(slabs):
+        lanes = lanes_of(slab)
+        y_state = dot(c_matrix, state[lanes], ((1,), (1,)))
+        arrived(yi_in, slab)
+        y_ref[:, lanes] = (yi_ref[:, lanes] + spread(entering, slab, head_dim) * y_state).astype(BF16)
+        group = slabs // sems.shape[0]
+        if slab % group == group - 1:
+            at = (slice(None), slice((slab + 1 - group) * LANES, (slab + 1) * LANES))
+            sent.append(put(y_ref, y_hbm, sems.at[slab // group], at))
+        arrived(dy_in, slab)
+        along_enter = along_enter + head_sum(
+            dy_ref[:, lanes].astype(F32) * y_state, slab, head_dim, heads
+        )
+    enter_ref[...] = along_enter
+    for copy in sent:
+        copy.wait()
+
+
+def x_kernel(
+    head_dim, xc_hbm, gs_hbm, ls_hbm, st_ref, bcc_ref, hv_ref, enter_ref, halo_ref, wx_ref,
+    gx_hbm, gdt_ref, xc_ref, gs_ref, ls_ref, gx_ref, ext, xc_sems, gs_sems, ls_sems, sems,
 ):
     rows, channels = xc_ref.shape
     heads = hv_ref.shape[1]
     taps = wx_ref.shape[0]
-    yi_in = fetch(yi_hbm, yi_ref, yi_sems)
+    slabs = channels // LANES
     gs_in = fetch(gs_hbm, gs_ref, gs_sems)
     ls_in = fetch(ls_hbm, ls_ref, ls_sems)
     xc_in = fetch(xc_hbm, xc_ref, xc_sems)
-    dy_in = fetch(dy_hbm, dy_ref, dy_sems)
     state, dstate = state_of(st_ref, 0), state_of(st_ref, 1)
-    b_matrix, c_matrix = bcc_ref[:, 0:LANES], bcc_ref[:, LANES:]
+    b_matrix = bcc_ref[:, 0:LANES]
     leave_step, leaving, entering, along_dt, z_diff, carry, decay, dt_gate = [
         hv_ref[at] for at in range(8)
     ]
+    along_enter = enter_ref[...]
     along_leave = jnp.zeros((heads, rows), F32)
-    along_enter = jnp.zeros((heads, rows), F32)
     ext[rows:, :] = halo_ref[:, 0:channels]
     sent = []
-    for slab in range(channels // LANES):
+    for slab in range(slabs):
         lanes = lanes_of(slab)
-        at = (slice(None), lanes)
-        y_state = dot(c_matrix, state[lanes], ((1,), (1,)))
         d_leaving = dot(b_matrix, dstate[lanes], ((1,), (1,)))
-        yi_in[slab].wait()
-        y_ref[at] = (yi_ref[at] + spread(entering, slab, head_dim) * y_state).astype(BF16)
-        sent.append(put(y_ref, y_hbm, out_sems.at[2 * slab], at))
-        gs_in[slab].wait()
-        ls_in[slab].wait()
-        ext[0:rows, lanes] = gs_ref[at] + ls_ref[at] * d_leaving
+        arrived(gs_in, slab)
+        arrived(ls_in, slab)
+        ext[0:rows, lanes] = gs_ref[:, lanes] + ls_ref[:, lanes] * d_leaving
         w = wx_ref[:, lanes].astype(F32)
         out = w[taps - 1 : taps] * ext[0:rows, lanes]
         for tap in range(taps - 1):
             out = out + w[tap : tap + 1] * ext[pl.ds(taps - 1 - tap, rows), lanes]
-        gx_ref[at] = out.astype(BF16)
-        sent.append(put(gx_ref, gx_hbm, out_sems.at[2 * slab + 1], at))
-        xc_in[slab].wait()
-        dy_in[slab].wait()
+        gx_ref[:, lanes] = out.astype(BF16)
+        group = slabs // sems.shape[0]
+        if slab % group == group - 1:
+            at = (slice(None), slice((slab + 1 - group) * LANES, (slab + 1) * LANES))
+            sent.append(put(gx_ref, gx_hbm, sems.at[slab // group], at))
+        arrived(xc_in, slab)
         along_leave = along_leave + head_sum(
-            xc_ref[at].astype(F32) * d_leaving, slab, head_dim, heads
+            xc_ref[:, lanes].astype(F32) * d_leaving, slab, head_dim, heads
         )
-        along_enter = along_enter + head_sum(dy_ref[at].astype(F32) * y_state, slab, head_dim, heads)
     product = state.astype(F32) * dstate.astype(F32)
     owner = iota((heads, channels), 1) // head_dim
     chosen = jnp.where(iota((heads, channels), 0) == owner, 1.0, 0.0)
@@ -468,23 +542,39 @@
     part = channels // count
     core = (lax.axis_index("head") % 2).astype(jnp.int32).reshape(1)
     halo = shift_ctx(jnp.concatenate([x_raw[rows - RIM :], bc_raw[rows - RIM :]], axis=1), 1)
-    slabs = channels // LANES
     wide_bf, wide_f = ((rows, channels), BF16), ((rows, channels), F32)
     sems = pltpu.SemaphoreType.DMA
+    two = sems((2,))
     inputs = [pltpu.VMEM(*wide_bf), pltpu.VMEM(*wide_bf), pltpu.VMEM((rows, wide), BF16)]
-    input_sems = [sems((slabs,)), sems((slabs,)), sems((wide // LANES,))]
+    input_sems = [two, two, sems((1,))]
     ext = pltpu.VMEM((rows + RIM, channels + wide), F32)
     sent = ((count, 2 * part + RIM, LANES), BF16)
     states = ((count, 2 * part, LANES), BF16)
-    send = call(
-        functools.partial(send_kernel, head_dim),
-        "send",
+    sums, leave_top, dy_top, top, tail = call(
+        functools.partial(gather_kernel, head_dim, part),
+        "gather",
         [doc_starts, a_log],
         [x_raw, grad_y, bc_raw],
-        [halo, conv_x_w, conv_bc_w, dt_raw],
+        [conv_x_w, conv_bc_w, dt_raw],
+        [],
+        [
+            ((2, channels, LANES), F32),
+            ((RIM, channels), F32),
+            ((RIM, channels), F32),
+            ((RIM, channels + wide), F32),
+            ((count, RIM, LANES), BF16),
+        ],
+        [*inputs, ext, *input_sems],
+    )
+    send = call(
+        send_kernel,
+        "send",
+        [],
+        [],
+        [halo, sums, leave_top, dy_top, top, tail, conv_x_w, conv_bc_w],
         [sent],
         [],
-        [*inputs, pltpu.VMEM(*sent), ext, *input_sems, sems((slabs,))],
+        [pltpu.VMEM(*sent), pltpu.VMEM((2 * RIM, channels + wide), F32), two],
     )
     got = lax.all_to_all(send, "ctx", 0, 0)
     xc, yi, gs, ls, lx, edy, bcc, gbc, sbc, hv, first = call(
@@ -513,7 +603,7 @@
             pltpu.VMEM((rows, rows), F32),
             pltpu.VMEM((rows, rows), F32),
             *input_sems,
-            sems((4 * slabs,)),
+            sems((8,)),
         ],
     )
     got, hv = lax.optimization_barrier((got, hv))
@@ -529,11 +619,34 @@
         [],
         [st, lx, edy, bcc, gbc, sbc, first, conv_bc_w],
         [],
-        [((half, wide), F32), ((half, wide), BF16), ((RIM, channels + wide), F32)],
+        [
+            ((half, wide), F32),
+            ((half, wide), BF16),
+            ((RIM, channels + wide), F32),
+        ],
         [pltpu.VMEM((rows + RIM, wide), F32), pltpu.VMEM((rows, wide), F32)],
     )
     next_rim = shift_ctx(rim, -1)
     other = swap_core(give)
+    st, keep = lax.optimization_barrier((st, keep))
+    y_out, along_enter = call(
+        functools.partial(y_kernel, head_dim),
+        "y_out",
+        [],
+        [grad_y, yi],
+        [st, bcc, hv],
+        [wide_bf],
+        [((heads, rows), F32)],
+        [
+            pltpu.VMEM(*wide_bf),
+            pltpu.VMEM(*wide_f),
+            pltpu.VMEM(*wide_bf),
+            two,
+            two,
+            two,
+        ],
+    )
+    other, next_rim, along_enter = lax.optimization_barrier((other, next_rim, along_enter))
     message = ((half + RIM, wide), BF16)
     joined = call(
         join_kernel,
@@ -547,25 +660,24 @@
     )
     ring = lax.axis_size("head") // 2
     pieces = [joined] + [around(joined, by) for by in range(1, ring)]
-    y_out, grad_x, grad_dt = call(
-        functools.partial(out_kernel, head_dim),
-        "out",
-        [],
-        [xc, grad_y, yi, gs, ls],
-        [st, bcc, hv, next_rim, conv_x_w],
-        [wide_bf, wide_bf],
+    grad_x, grad_dt = call(
+        functools.partial(x_kernel, head_dim),
+        "grad_x",
+        [],
+        [xc, gs, ls],
+        [st, bcc, hv, along_enter, next_rim, conv_x_w],
+        [wide_bf],
         [((heads, rows), F32)],
         [
             pltpu.VMEM(*wide_bf),
-            pltpu.VMEM(*wide_bf),
-            pltpu.VMEM(*wide_f),
             pltpu.VMEM(*wide_f),
             pltpu.VMEM(*wide_f),
             pltpu.VMEM(*wide_bf),
-            pltpu.VMEM(*wide_bf),
             pltpu.VMEM((rows + RIM, channels), F32),
-            *[sems((slabs,)) for _ in range(5)],
-            sems((2 * slabs,)),
+            two,
+            two,
+            two,
+            two,
         ],
     )
     pieces, grad_dt = lax.optimization_barrier((pieces, grad_dt))

time: 89.8 us -> 84.3 us (0.939)
  waiting for transfers between devices: 25.8 us -> 23.8 us
  starting transfers between devices: 34 us -> 32.2 us
  Pallas kernels: 27 us -> 25.5 us
    ppermute x2, waiting for transfers between devices: 4.77 us -> 1.27 us  [shift_ctx(): return lax.ppermute(values, 'ctx', pairs)]
    all_to_all x1, starting transfers between devices: 11.9 us -> 10.4 us  [body(): got = lax.all_to_all(send, 'ctx', 0, 0)]
    pallas_call x8 -> x10, Pallas kernels: 27 us -> 25.5 us  [call(): pl.pallas_call(kernel, name=name, out_shape=out if many else out[0], in_s...]
    all_to_all x1, waiting for transfers between devices: 5.46 us -> 6.89 us  [body(): got = lax.all_to_all(send, 'ctx', 0, 0)]
  transfers between devices with their start and end apart: 9 -> 9, of which waited for: 5 -> 4; matrix products, arithmetic and copies ran while one was open for 0% -> 0% of each run, Pallas kernels for 20% -> 26%
where the time goes in v3:
time: 84.3 us; the launch traced here: 83.8 us
  starting transfers between devices  32.2 us (38%)
  Pallas kernels  25.5 us (30%)
  waiting for transfers between devices  23.8 us (28%)
  between operations  1.5 us (2%)
    pallas_call x10, Pallas kernels, call(): pl.pallas_call(kernel, name=name, out_shape=out if many else out[0], in_s...  25.5 us
    all_to_all x1, waiting for transfers between devices, body(): st = lax.all_to_all(scanned, 'ctx', 0, 0)  14.8 us
    all_to_all x1, starting transfers between devices, body(): got = lax.all_to_all(send, 'ctx', 0, 0)  10.4 us
    all_to_all x1, waiting for transfers between devices, body(): got = lax.all_to_all(send, 'ctx', 0, 0)  6.89 us
    ppermute x2, starting transfers between devices, shift_ctx(): return lax.ppermute(values, 'ctx', pairs)  6.07 us
    all_to_all x1, starting transfers between devices, body(): st = lax.all_to_all(scanned, 'ctx', 0, 0)  5.96 us
    ppermute x2, starting transfers between devices, swap_core(): return lax.ppermute(values, 'head', [(i, i ^ 1) for i in range(size)])  5.9 us
    ppermute x3, starting transfers between devices, around(): lax.ppermute(values, 'head', [(i, (i + 2 * by) % size) for i in range(siz...  3.85 us
  transfers between devices with their start and end apart: 9, of which 4 were waited for; matrix products, arithmetic and copies ran while one was open for 0% of the time, Pallas kernels for 26%

profile of v3, /device:TPU:7, one launch (start us, length us, event | category | flops | bytes accessed | tf_op | source)
XLA Modules:
  0.0 83.8 jit_solution(16050299366578930515)
XLA Ops:
  0.6 0.0 slice-start
  0.6 0.0 slice-start.1
  0.7 0.7 slice-done
  1.4 0.0 slice-done.1
  1.4 0.0 copy-start
  1.4 0.0 copy-start.1
  1.4 0.0 copy-start.2
  1.4 0.0 copy-start.3
  1.4 3.6 %collective-permute-start = (bf16[8,1280]{1,0:T(8,128)(2,1)S(1)}, bf16[8,1280]{1,0:T(8,128)(2,1)S(1)}, u32[]{:S(2)}, u32[]{:S(2)}) collective-permute-start(bf16[8,1280]{1,0:T(8,128)(2,1)S(1)} %pad_maximum_fusion), channel_id=1, source_target_pairs={{0,8},{8,16},{16,24},{24,32},{32,40},{40,48},{48,56},{56,64},{64,7... | collective-permute-start | bytes 61448 | tf_op jit(solution)/shard_map/ppermute | solution.py:523
  5.6 0.0 copy-done
  5.6 0.0 copy-done.1
  5.7 0.0 copy-done.2
  5.7 0.0 copy-done.3
  5.7 4.6 %gather.1 = (f32[2,1024,128]{2,1,0:T(8,128)S(1)}, f32[8,1024]{1,0:T(8,128)S(1)}, f32[8,1024]{1,0:T(8,128)S(1)}, f32[8,1280]{1,0:T(8,128)S(1)}, bf16[32,8,128]{2,1,0:T(8,128)(2,1)S(1)}) custom-call(s32[1]{0:T(128)S(6)} %copy.13.doc_ref, f32[16]{0:T(128)S(1)} %copy-done.3, bf16[256,1024]{1,0:T(8,128)(2,1)} %x_hbm.3, bf16[256,1024]{1,0:T(8,128)(2,1)} %dy_hbm.5, ...), custom_call_target="tpu_custom_call" | custom-call | tf_op jit(solution)/shard_map/gather/pallas_call | solution.py:509
  10.3 0.0 collective-permute-done.halo_ref
  10.3 1.2 %send.1 = bf16[32,72,128]{2,1,0:T(8,128)(2,1)} custom-call(bf16[8,1280]{1,0:T(8,128)(2,1)S(1)} %collective-permute-done.halo_ref, f32[2,1024,128]{2,1,0:T(8,128)S(1)} %get-tuple-element.40.sum_ref, f32[8,1024]{1,0:T(8,128)S(1)} %get-tuple-element.41.ls_ref, f32[8,1024]{1,0:T(8,128)S(1)} %get-tuple-element.42.edy_ref, ...), custom_call_target="tpu_custom_call" | custom-call | tf_op jit(solution)/shard_map/send/pallas_call | solution.py:509
  11.5 0.0 copy-start.4
  11.5 10.4 %all-to-all-start = ((bf16[32,72,128]{2,1,0:T(8,128)(2,1)}), bf16[32,72,128]{2,1,0:T(8,128)(2,1)S(1)}, u32[]{:S(2)}, u32[]{:S(2)}) async-start(bf16[32,72,128]{2,1,0:T(8,128)(2,1)} %send.1), calls=%async_computation | async-start | bytes 1179648 | tf_op jit(solution)/shard_map/all_to_all | solution.py:579
  21.9 0.0 copy-done.4
  21.9 10.0 %intra.1 = (bf16[256,1024]{1,0:T(8,128)(2,1)}, f32[256,1024]{1,0:T(8,128)}, f32[256,1024]{1,0:T(8,128)}, f32[256,1024]{1,0:T(8,128)}, bf16[256,1024]{1,0:T(8,128...) custom-call(s32[1]{0:T(128)S(6)} %copy.13.doc_ref, ...), custom_call_target="tpu_custom_call" | custom-call | tf_op jit(solution)/shard_map/intra/pallas_call | solution.py:509
  31.9 6.9 %all-to-all-done.got_ref = bf16[32,72,128]{2,1,0:T(8,128)(2,1)S(1)} async-done(((bf16[32,72,128]{2,1,0:T(8,128)(2,1)}), bf16[32,72,128]{2,1,0:T(8,128)(2,1)S(1)}, u32[]{:S(2)}, u32[]{:S(2)}) %all-to-all-start) | async-done | bytes 589856 | tf_op jit(solution)/shard_map/all_to_all | solution.py:579
  38.8 0.9 %scan.1 = bf16[32,64,128]{2,1,0:T(8,128)(2,1)} custom-call(bf16[32,72,128]{2,1,0:T(8,128)(2,1)S(1)} %all-to-all-done.got_ref), custom_call_target="tpu_custom_call" | custom-call | tf_op jit(solution)/shard_map/scan/pallas_call | solution.py:509
  39.7 6.0 %all-to-all-start.1 = ((bf16[32,64,128]{2,1,0:T(8,128)(2,1)}), bf16[32,64,128]{2,1,0:T(8,128)(2,1)S(1)}, u32[]{:S(2)}, u32[]{:S(2)}) async-start(bf16[32,64,128]{2,1,0:T(8,128)(2,1)} %scan.1), calls=%async_computation.1 | async-start | bytes 1048576 | tf_op jit(solution)/shard_map/all_to_all | solution.py:613
  45.7 14.8 %all-to-all-done.1.st_ref = bf16[32,64,128]{2,1,0:T(8,128)(2,1)S(1)} async-done(((bf16[32,64,128]{2,1,0:T(8,128)(2,1)}), bf16[32,64,128]{2,1,0:T(8,128)(2,1)S(1)}, u32[]{:S(2)}, u32[]{:S(2)}) %all-to-all-start.1) | async-done | bytes 524320 | tf_op jit(solution)/shard_map/all_to_all | solution.py:613
  60.5 0.5 grad_bc.1
  61.0 3.4 %collective-permute-start.1 = (bf16[128,256]{1,0:T(8,128)(2,1)S(1)}, bf16[128,256]{1,0:T(8,128)(2,1)S(1)}, u32[]{:S(2)}, u32[]{:S(2)}) collective-permute-start(bf16[128,256]{1,0:T(8,128)(2,1)S(1)} %get-tuple-element.60), channel_id=1, source_target_pairs={{0,1},{1,0},{2,3},{3,2},{4,5},{5,4},{6,7},{7,6},{8,9},{9,8},{10,11... | collective-permute-start | bytes 196616 | tf_op jit(solution)/shard_map/ppermute | solution.py:528
  64.3 2.5 %collective-permute-start.2 = (f32[8,1280]{1,0:T(8,128)S(1)}, f32[8,1280]{1,0:T(8,128)S(1)}, u32[]{:S(2)}, u32[]{:S(2)}) collective-permute-start(f32[8,1280]{1,0:T(8,128)S(1)} %get-tuple-element.61), channel_id=1, source_target_pairs={{8,0},{16,8},{24,16},{32,24},{40,32},{48,40},{56,48},{64,56},{72,6... | collective-permute-start | bytes 122888 | tf_op jit(solution)/shard_map/ppermute | solution.py:523
  66.8 3.1 %y_out.1 = (bf16[256,1024]{1,0:T(8,128)(2,1)}, f32[16,256]{1,0:T(8,128)S(1)}) custom-call(bf16[256,1024]{1,0:T(8,128)(2,1)} %dy_hbm.5, f32[256,1024]{1,0:T(8,128)} %get-tuple-element.39.yi_hbm, bf16[32,64,128]{2,1,0:T(8,128)(2,1)S(1)} %all-to-all-done.1.st_ref, bf16[256,256]{1,0:T(8,128)(2,1)S(1)} %get-tuple-element.49.b_ref.bcc_ref, ...), custom_call_target="tpu_custom_call" | custom-call | tf_op jit(solution)/shard_map/y_out/pallas_call | solution.py:509
  69.9 1.3 %collective-permute-done.2.halo_ref = f32[8,1280]{1,0:T(8,128)S(1)} collective-permute-done((f32[8,1280]{1,0:T(8,128)S(1)}, f32[8,1280]{1,0:T(8,128)S(1)}, u32[]{:S(2)}, u32[]{:S(2)}) %collective-permute-start.2) | collective-permute-done | bytes 40992 | tf_op jit(solution)/shard_map/ppermute | solution.py:523
  71.2 0.0 collective-permute-done.1.got_ref
  71.2 2.8 %collective-permute-start.5 = (bf16[136,256]{1,0:T(8,128)(2,1)S(1)}, bf16[136,256]{1,0:T(8,128)(2,1)S(1)}, u32[]{:S(2)}, u32[]{:S(2)}) collective-permute-start(bf16[136,256]{1,0:T(8,128)(2,1)S(1)} %join.1.refs_0_), channel_id=1, source_target_pairs={{0,6},{1,7},{2,0},{3,1},{4,2},{5,3},{6,4},{7,5},{8,14},{9,15},{10,... | collective-permute-start | bytes 208904 | tf_op jit(solution)/shard_map/ppermute | solution.py:533
  74.0 0.4 collective-permute-start.4
  74.4 0.7 collective-permute-start.3
  75.1 4.5 %grad_x.1 = (bf16[256,1024]{1,0:T(8,128)(2,1)}, f32[16,256]{1,0:T(8,128)}) custom-call(bf16[256,1024]{1,0:T(8,128)(2,1)} %get-tuple-element.57.xc_hbm, f32[256,1024]{1,0:T(8,128)} %get-tuple-element.58.gs_hbm, f32[256,1024]{1,0:T(8,128)} %get-tuple-element.59.ls_hbm, bf16[32,64,128]{2,1,0:T(8,128)(2,1)S(1)} %all-to-all-done.1.st_ref, ...), custom_call_target="tpu_custom_call" | custom-call | tf_op jit(solution)/shard_map/grad_x/pallas_call | solution.py:509
  79.5 0.0 collective-permute-done.5.refs_3_
  79.6 0.0 collective-permute-done.4.refs_2_
  79.6 0.0 collective-permute-done.3.refs_1_
  79.6 2.5 %collective-permute-start.6 = (bf16[136,256]{1,0:T(8,128)(2,1)S(1)}, bf16[136,256]{1,0:T(8,128)(2,1)S(1)}, u32[]{:S(2)}, u32[]{:S(2)}) collective-permute-start(bf16[136,256]{1,0:T(8,128)(2,1)S(1)} %sum.1.mine_ref), channel_id=1, source_target_pairs={{0,1},{1,0},{2,3},{3,2},{4,5},{5,4},{6,7},{7,6},{8,9},{9,8},{10,11... | collective-permute-start | bytes 208904 | tf_op jit(solution)/shard_map/ppermute | solution.py:528
  82.2 0.9 %collective-permute-done.6.got_ref = bf16[136,256]{1,0:T(8,128)(2,1)S(1)} collective-permute-done((bf16[136,256]{1,0:T(8,128)(2,1)S(1)}, bf16[136,256]{1,0:T(8,128)(2,1)S(1)}, u32[]{:S(2)}, u32[]{:S(2)}) %collective-permute-start.6) | collective-permute-done | bytes 69664 | tf_op jit(solution)/shard_map/ppermute | solution.py:528
  83.1 0.7 last.1
  (3 shorter events, 0.1 us)
Async XLA Ops:
  0.6 0.7 slice-start
  0.6 0.7 slice-start.1
  1.4 4.3 %copy-start = (bf16[4,1024]{1,0:T(4,128)(2,1)S(1)}, bf16[4,1024]{1,0:T(4,128)(2,1)}, u32[]{:S(2)}) copy-start(bf16[4,1024]{1,0:T(4,128)(2,1)} %wx_ref.7) | copy-start | bytes 24580
  1.4 4.3 %copy-start.1 = (f32[16,256]{1,0:T(8,128)S(1)}, f32[16,256]{1,0:T(8,128)}, u32[]{:S(2)}) copy-start(f32[16,256]{1,0:T(8,128)} %dt_ref.3) | copy-start | bytes 49156
  1.4 4.3 %copy-start.2 = (bf16[4,256]{1,0:T(4,128)(2,1)S(1)}, bf16[4,256]{1,0:T(4,128)(2,1)}, u32[]{:S(2)}) copy-start(bf16[4,256]{1,0:T(4,128)(2,1)} %wbc_ref.9) | copy-start | bytes 6148
  1.4 4.3 %copy-start.3 = (f32[16]{0:T(128)S(1)}, f32[16]{0:T(128)}, u32[]{:S(2)}) copy-start(f32[16]{0:T(128)} %a_log_ref.3) | copy-start | bytes 196
  1.4 8.9 %collective-permute-start = (bf16[8,1280]{1,0:T(8,128)(2,1)S(1)}, bf16[8,1280]{1,0:T(8,128)(2,1)S(1)}, u32[]{:S(2)}, u32[]{:S(2)}) collective-permute-start(bf16[8,1280]{1,0:T(8,128)(2,1)S(1)} %pad_maximum_fusion), channel_id=1, source_target_pairs={{0,8},{8,16},{16,24},{24,32},{32,40},{40,48},{48,56},{56,64},{64,7... | collective-permute-start | bytes 61448 | tf_op jit(solution)/shard_map/ppermute | solution.py:523
  11.5 10.4 %copy-start.4 = (f32[16]{0:T(128)S(1)}, f32[16]{0:T(128)}, u32[]{:S(2)}) copy-start(f32[16]{0:T(128)} %skip_ref.1) | copy-start | bytes 196
  11.5 27.3 %all-to-all-start = ((bf16[32,72,128]{2,1,0:T(8,128)(2,1)}), bf16[32,72,128]{2,1,0:T(8,128)(2,1)S(1)}, u32[]{:S(2)}, u32[]{:S(2)}) async-start(bf16[32,72,128]{2,1,0:T(8,128)(2,1)} %send.1), calls=%async_computation | async-start | bytes 1179648 | tf_op jit(solution)/shard_map/all_to_all | solution.py:579
  39.7 20.8 %all-to-all-start.1 = ((bf16[32,64,128]{2,1,0:T(8,128)(2,1)}), bf16[32,64,128]{2,1,0:T(8,128)(2,1)S(1)}, u32[]{:S(2)}, u32[]{:S(2)}) async-start(bf16[32,64,128]{2,1,0:T(8,128)(2,1)} %scan.1), calls=%async_computation.1 | async-start | bytes 1048576 | tf_op jit(solution)/shard_map/all_to_all | solution.py:613
  61.0 10.2 %collective-permute-start.1 = (bf16[128,256]{1,0:T(8,128)(2,1)S(1)}, bf16[128,256]{1,0:T(8,128)(2,1)S(1)}, u32[]{:S(2)}, u32[]{:S(2)}) collective-permute-start(bf16[128,256]{1,0:T(8,128)(2,1)S(1)} %get-tuple-element.60), channel_id=1, source_target_pairs={{0,1},{1,0},{2,3},{3,2},{4,5},{5,4},{6,7},{7,6},{8,9},{9,8},{10,11... | collective-permute-start | bytes 196616 | tf_op jit(solution)/shard_map/ppermute | solution.py:528
  64.3 6.8 %collective-permute-start.2 = (f32[8,1280]{1,0:T(8,128)S(1)}, f32[8,1280]{1,0:T(8,128)S(1)}, u32[]{:S(2)}, u32[]{:S(2)}) collective-permute-start(f32[8,1280]{1,0:T(8,128)S(1)} %get-tuple-element.61), channel_id=1, source_target_pairs={{8,0},{16,8},{24,16},{32,24},{40,32},{48,40},{56,48},{64,56},{72,6... | collective-permute-start | bytes 122888 | tf_op jit(solution)/shard_map/ppermute | solution.py:523
  71.2 8.3 %collective-permute-start.5 = (bf16[136,256]{1,0:T(8,128)(2,1)S(1)}, bf16[136,256]{1,0:T(8,128)(2,1)S(1)}, u32[]{:S(2)}, u32[]{:S(2)}) collective-permute-start(bf16[136,256]{1,0:T(8,128)(2,1)S(1)} %join.1.refs_0_), channel_id=1, source_target_pairs={{0,6},{1,7},{2,0},{3,1},{4,2},{5,3},{6,4},{7,5},{8,14},{9,15},{10,... | collective-permute-start | bytes 208904 | tf_op jit(solution)/shard_map/ppermute | solution.py:533
  74.0 5.5 %collective-permute-start.4 = (bf16[136,256]{1,0:T(8,128)(2,1)S(1)}, bf16[136,256]{1,0:T(8,128)(2,1)S(1)}, u32[]{:S(2)}, u32[]{:S(2)}) collective-permute-start(bf16[136,256]{1,0:T(8,128)(2,1)S(1)} %join.1.refs_0_), channel_id=1, source_target_pairs={{0,4},{1,5},{2,6},{3,7},{4,0},{5,1},{6,2},{7,3},{8,12},{9,13},{10,... | collective-permute-start | bytes 208904 | tf_op jit(solution)/shard_map/ppermute | solution.py:533
  74.4 5.2 %collective-permute-start.3 = (bf16[136,256]{1,0:T(8,128)(2,1)S(1)}, bf16[136,256]{1,0:T(8,128)(2,1)S(1)}, u32[]{:S(2)}, u32[]{:S(2)}) collective-permute-start(bf16[136,256]{1,0:T(8,128)(2,1)S(1)} %join.1.refs_0_), channel_id=1, source_target_pairs={{0,2},{1,3},{2,4},{3,5},{4,6},{5,7},{6,0},{7,1},{8,10},{9,11},{10,... | collective-permute-start | bytes 208904 | tf_op jit(solution)/shard_map/ppermute | solution.py:533
  79.6 3.4 %collective-permute-start.6 = (bf16[136,256]{1,0:T(8,128)(2,1)S(1)}, bf16[136,256]{1,0:T(8,128)(2,1)S(1)}, u32[]{:S(2)}, u32[]{:S(2)}) collective-permute-start(bf16[136,256]{1,0:T(8,128)(2,1)S(1)} %sum.1.mine_ref), channel_id=1, source_target_pairs={{0,1},{1,0},{2,3},{3,2},{4,5},{5,4},{6,7},{7,6},{8,9},{9,8},{10,11... | collective-permute-start | bytes 208904 | tf_op jit(solution)/shard_map/ppermute | solution.py:528

commit v4 on v3

--- a/solution.py
+++ b/solution.py
@@ -29,17 +29,24 @@
 
 
 def sigmoid(values):
-    return 1.0 / (1.0 + jnp.exp(-values))
-
-
-def spread(values, slab, head_dim):
-    heads = values.shape[0]
-    high, low = halves(values)
-    both = jnp.concatenate([high, low], axis=0)
+    return 0.5 * jnp.tanh(0.5 * values) + 0.5
+
+
+def diagonal(size):
+    return jnp.where(iota((size, size), 0) == iota((size, size), 1), 1.0, 0.0).astype(BF16)
+
+
+def columns(values):
+    both = jnp.concatenate(halves(values), axis=0)
+    return dot(diagonal(values.shape[1]), both, ((1,), (1,))).astype(BF16)
+
+
+def spread(pairs, slab, head_dim):
+    heads = pairs.shape[1] // 2
     row = iota((2 * heads, LANES), 0)
     head = iota((2 * heads, LANES), 1) // head_dim + slab * (LANES // head_dim)
     chosen = jnp.where((row == head) | (row == head + heads), 1.0, 0.0).astype(BF16)
-    return dot(both, chosen, ((0,), (0,)))
+    return dot(pairs, chosen, ((1,), (0,)))
 
 
 def head_sum(values, slab, head_dim, heads):
@@ -124,7 +131,7 @@
 
 
 def gather_kernel(
-    head_dim, part, doc_ref, a_log_ref, x_hbm, dy_hbm, bc_hbm, wx_ref, wbc_ref, dt_ref,
+    head_dim, doc_ref, a_log_ref, x_hbm, dy_hbm, bc_hbm, wx_ref, wbc_ref, dt_ref,
     sum_ref, ls_ref, edy_ref, top_ref, tail_ref,
     x_ref, dy_ref, bc_ref, ext, x_sems, dy_sems, bc_sems,
 ):
@@ -133,24 +140,21 @@
     x_in = fetch(x_hbm, x_ref, x_sems)
     dy_in = fetch(dy_hbm, dy_ref, dy_sems)
     v = head_values(doc_ref, a_log_ref, dt_ref)
-    leave_step = v["leaving"] * v["step"]
-    high, low = halves(v["carry"][:, 0:LANES])
+    leave_step = columns(v["leaving"] * v["step"])
+    entering = columns(v["entering"])
+    heads = dt_ref.shape[0]
+    own = iota((heads, LANES), 0) == iota((heads, LANES), 1)
+    carry = jnp.sum(jnp.where(own, v["carry"][:, 0:LANES], 0.0), axis=0, keepdims=True)
+    high, low = [half.astype(F32) for half in halves(carry)]
     at = iota((RIM, LANES), 0)
+    tail_ref[...] = jnp.where(at == 0, high, jnp.where(at == 1, low, 0.0)).astype(BF16)
     below = iota((rows, LANES), 0) >= RIM
-    for chunk in range(tail_ref.shape[0]):
-        head = chunk * part // head_dim
-        tile = jnp.where(
-            at == 0,
-            high[head : head + 1].astype(F32),
-            jnp.where(at == 1, low[head : head + 1].astype(F32), 0.0),
-        )
-        tail_ref[chunk] = tile.astype(BF16)
     bc = []
     for half in range(2):
         arrived(bc_in, half)
         load_ext(ext, None, bc_ref, lanes_of(channels // LANES + half), lanes_of(half))
         pre = filtered(ext, wbc_ref, channels + half * LANES, half * LANES, rows)
-        bc.append((pre * sigmoid(pre)).astype(BF16))
+        bc.append((pre * sigmoid(pre)).T.astype(BF16))
     for slab in range(channels // LANES):
         lanes = lanes_of(slab)
         arrived(x_in, slab)
@@ -160,21 +164,25 @@
         leave = spread(leave_step, slab, head_dim)
         leaving_x = jnp.where(below, x_conv * leave, 0.0).astype(BF16)
         arrived(dy_in, slab)
-        enter_dy = dy_ref[:, lanes].astype(F32) * spread(v["entering"], slab, head_dim)
-        sum_ref[0, lanes, :] = dot(leaving_x, bc[0], ((0,), (0,)))
-        sum_ref[1, lanes, :] = dot(jnp.where(below, enter_dy, 0.0).astype(BF16), bc[1], ((0,), (0,)))
+        enter_dy = dy_ref[:, lanes].astype(F32) * spread(entering, slab, head_dim)
+        sum_ref[0, :, lanes] = dot(bc[0], leaving_x, ((1,), (0,)))
+        masked = jnp.where(below, enter_dy, 0.0).astype(BF16)
+        sum_ref[1, :, lanes] = dot(bc[1], masked, ((1,), (0,)))
         ls_ref[:, lanes] = leave[0:RIM]
         edy_ref[:, lanes] = enter_dy[0:RIM]
     top_ref[...] = ext[RIM : 2 * RIM, :]
 
 
+def chunk_of(across, side, which):
+    return 16 * across + 2 * side + which
+
+
 def send_kernel(
-    halo_ref, sum_ref, ls_ref, edy_ref, top_ref, tail_ref, wx_ref, wbc_ref,
-    send_hbm, send_ref, ext, sems,
+    halo_ref, sum_ref, ls_ref, edy_ref, top_ref, tail_ref, wx_ref, wbc_ref, send_ref, ext,
 ):
     channels = ls_ref.shape[1]
-    part = channels // send_ref.shape[0]
-    per_slab = LANES // part
+    count = send_ref.shape[0]
+    tall = 2 * RIM
     ext[0:RIM, :] = halo_ref[...].astype(F32)
     ext[RIM:, :] = top_ref[...]
     none = jnp.zeros((RIM, LANES), F32)
@@ -183,61 +191,64 @@
         pre = filtered(ext, w_ref, at, w_at, RIM)
         return (pre * sigmoid(pre)).astype(BF16).astype(F32)
 
-    bc = [
-        jnp.concatenate([conv(wbc_ref, channels + at, at), none], axis=0).astype(BF16)
-        for at in (0, LANES)
-    ]
+    bc = []
+    for at in (0, LANES):
+        top = jnp.concatenate([conv(wbc_ref, channels + at, at), none], axis=0).astype(BF16)
+        bc.append(dot(top, diagonal(tall), ((0,), (0,))).astype(BF16))
+    tail = tail_ref[...]
+    for chunk in range(count):
+        send_ref[chunk, send_ref.shape[1] - RIM :, :] = tail
     slabs = channels // LANES
-    sent = []
     for slab in range(slabs):
         lanes = lanes_of(slab)
+        across, tile = slab // (slabs // 2), slab % (slabs // 2)
         leaving_x = conv(wx_ref, slab * LANES, slab * LANES) * ls_ref[:, lanes]
-        leaving_x = jnp.concatenate([leaving_x, none], axis=0).astype(BF16)
-        enter_dy = jnp.concatenate([edy_ref[:, lanes], none], axis=0).astype(BF16)
-        forward = (sum_ref[0, lanes, :] + dot(leaving_x, bc[0], ((0,), (0,)))).astype(BF16)
-        backward = (sum_ref[1, lanes, :] + dot(enter_dy, bc[1], ((0,), (0,)))).astype(BF16)
-        own = slice(slab * per_slab, (slab + 1) * per_slab)
-        send_ref[own, 0:part, :] = forward.reshape(per_slab, part, LANES)
-        send_ref[own, part : 2 * part, :] = backward.reshape(per_slab, part, LANES)
-        send_ref[own, 2 * part : 2 * part + RIM, :] = tail_ref[own]
-        group = slabs // sems.shape[0]
-        if slab % group == group - 1:
-            ready = slice((slab + 1 - group) * per_slab, (slab + 1) * per_slab)
-            sent.append(put(send_ref, send_hbm, sems.at[slab // group], (ready,)))
+        enter_dy = edy_ref[:, lanes]
+        for which, top in enumerate((leaving_x, enter_dy)):
+            top = jnp.concatenate([top, none], axis=0).astype(BF16)
+            total = (sum_ref[which, :, lanes] + dot(bc[which], top, ((1,), (0,)))).astype(BF16)
+            for side in range(LANES // tall):
+                piece = total[side * tall : (side + 1) * tall]
+                send_ref[chunk_of(across, side, which), tile * tall : (tile + 1) * tall, :] = piece
+
+
+def scan_kernel(head_dim, got_ref, out_hbm, out_ref, tails, carries, sems):
+    count, width, lanes = out_ref.shape
+    tall = 2 * RIM
+    tiles = width // tall
+    me = lax.axis_index("ctx")
+    backward = lax.rem(me, 2)
+    across = me // (count // 2)
+    for at in range(count):
+        tails[RIM * at : RIM * (at + 1), :] = got_ref[at, width : width + RIM, :].astype(F32)
+    shape = (lanes, tiles * lanes)
+    head = iota(shape, 1) // head_dim + across * (tiles * lanes // head_dim)
+    chosen = jnp.where(iota(shape, 0) == head, 1.0, 0.0).astype(BF16)
+    carries[...] = dot(tails[...].astype(BF16), chosen, ((1,), (0,)))
+    states = [jnp.zeros((tall, lanes), F32) for _ in range(tiles)]
+    sent = []
+    pieces = sems.shape[0]
+    group = count // pieces
+    for step in range(count):
+        at = jnp.where(backward == 1, count - 1 - step, step)
+        carry = carries[pl.ds(pl.multiple_of(at * RIM, RIM), RIM), :]
+        carry = carry[0:1] + carry[1:2]
+        for tile in range(tiles):
+            rows = slice(tile * tall, (tile + 1) * tall)
+            out_ref[at, rows, :] = states[tile].astype(BF16)
+            states[tile] = carry[:, lanes_of(tile)] * states[tile] + got_ref[at, rows, :].astype(F32)
+        if step % group == group - 1:
+            first = jnp.where(backward == 1, count - 1 - step, step + 1 - group)
+            sent.append(put(out_ref, out_hbm, sems.at[step // group], (pl.ds(first, group),)))
     for copy in sent:
         copy.wait()
 
 
-def scan_kernel(got_ref, out_hbm, out_ref, sems):
-    count, width, lanes = out_ref.shape
-    part = width // 2
-    forward = jnp.zeros((part, lanes), F32)
-    backward = jnp.zeros((part, lanes), F32)
-
-    def carry(at):
-        tail = got_ref[at, width : width + RIM, :].astype(F32)
-        return tail[0:1] + tail[1:2]
-
-    sent = []
-    for at in range(count):
-        out_ref[at, 0:part, :] = forward.astype(BF16)
-        forward = carry(at) * forward + got_ref[at, 0:part, :].astype(F32)
-        back = count - 1 - at
-        out_ref[back, part : 2 * part, :] = backward.astype(BF16)
-        backward = carry(back) * backward + got_ref[back, part : 2 * part, :].astype(F32)
-        low, high = min(at, back), max(at, back)
-        if at >= count // 2 and (at + 1) % 4 == 0:
-            sent.append(put(out_ref, out_hbm, sems.at[len(sent)], (slice(high - 3, high + 1),)))
-            sent.append(put(out_ref, out_hbm, sems.at[len(sent)], (slice(low, low + 4),)))
-    for copy in sent:
-        copy.wait()
-
-
 def intra_kernel(
     head_dim, doc_ref, a_log_ref, skip_ref, x_hbm, dy_hbm, bc_hbm, halo_ref, wx_ref, wbc_ref, dt_ref,
-    xc_hbm, yi_hbm, gs_hbm, ls_hbm,
+    gs_hbm, ls_hbm, yi_ref,
     lx_ref, edy_ref, bcc_ref, gbc_ref, sbc_ref, hv_ref, rim_ref,
-    x_ref, dy_ref, bc_ref, xc_ref, yi_ref, gs_ref, ls_ref, ext, bias, dgram,
+    x_ref, dy_ref, bc_ref, gs_ref, ls_ref, ext, bias, dgram,
     x_sems, dy_sems, bc_sems, out_sems,
 ):
     rows, channels = x_ref.shape
@@ -265,7 +276,9 @@
     cum = v["cum"]
     cum_t = dot(downto, v["drop"], ((1,), (1,)), HIGHEST)
     skip = per_head(skip_ref, heads, rows)
-    leave_step = v["leaving"] * v["step"]
+    leave_step = columns(v["leaving"] * v["step"])
+    entering, steps = columns(v["entering"]), columns(v["step"])
+    skip = columns(skip)
     along_dt = jnp.zeros((heads, rows), F32)
     z_diff = jnp.zeros((heads, rows), F32)
     low_half = iota((rows, LANES), 1) < head_dim
@@ -280,10 +293,9 @@
         x_bf = (pre * gate).astype(BF16)
         silu_grad = gate * (1.0 + pre * (1.0 - gate))
         x_conv = x_bf.astype(F32)
-        xc_ref[:, lanes] = x_bf
-        step = spread(v["step"], slab, head_dim)
+        step = spread(steps, slab, head_dim)
         leave = spread(leave_step, slab, head_dim)
-        enter = spread(v["entering"], slab, head_dim)
+        enter = spread(entering, slab, head_dim)
         skips = spread(skip, slab, head_dim)
         dy_bf = dy_ref[:, lanes]
         dy = dy_bf.astype(F32)
@@ -308,13 +320,11 @@
         ls_ref[:, lanes] = leave * silu_grad
         rim_ref[0, :, lanes] = gs_ref[0:RIM, lanes]
         rim_ref[1, :, lanes] = ls_ref[0:RIM, lanes]
-        group = channels // LANES // (out_sems.shape[0] // 4)
+        group = channels // LANES // (out_sems.shape[0] // 2)
         if slab % group == group - 1:
             at = (slice(None), slice((slab + 1 - group) * LANES, (slab + 1) * LANES))
-            for which, (mine, out) in enumerate(
-                ((xc_ref, xc_hbm), (yi_ref, yi_hbm), (gs_ref, gs_hbm), (ls_ref, ls_hbm))
-            ):
-                sent.append(put(mine, out, out_sems.at[slab // group * 4 + which], at))
+            sent.append(put(gs_ref, gs_hbm, out_sems.at[slab // group * 2], at))
+            sent.append(put(ls_ref, ls_hbm, out_sems.at[slab // group * 2 + 1], at))
         along_dt = along_dt + head_sum(x_conv * d_scaled, slab, head_dim, heads)
         z_diff = z_diff + head_sum(
             dy * intra - scaled.astype(F32) * d_scaled, slab, head_dim, heads
@@ -323,14 +333,13 @@
     gbc_ref[:, 0:LANES] = dot(d_gram, c_matrix.astype(F32), ((0,), (0,)), HIGHEST)
     gbc_ref[:, LANES:] = dot(d_gram, b_matrix.astype(F32), ((1,), (0,)), HIGHEST)
     small = [
-        leave_step,
-        v["leaving"],
+        v["step"],
         v["entering"],
         along_dt,
         z_diff,
         v["carry"],
         v["decay"],
-        sigmoid(dt_ref[...]),
+        1.0 / (1.0 + jnp.exp(-dt_ref[...])),
     ]
     for at, values in enumerate(small):
         hv_ref[at] = values
@@ -338,10 +347,15 @@
         copy.wait()
 
 
-def state_of(st_ref, which):
-    count, width, lanes = st_ref.shape
-    part = width // 2
-    return st_ref[:, which * part : (which + 1) * part, :].reshape(count * part, lanes)
+def state_of(st_ref, which, slab):
+    tall = 2 * RIM
+    tiles = st_ref.shape[1] // tall
+    across, tile = slab // tiles, slab % tiles
+    sides = LANES // tall
+    rows = slice(tile * tall, (tile + 1) * tall)
+    return jnp.concatenate(
+        [st_ref[chunk_of(across, side, which), rows, :] for side in range(sides)], axis=0
+    )
 
 
 def bc_kernel(
@@ -350,9 +364,13 @@
 ):
     rows = lx_ref.shape[0]
     taps = wbc_ref.shape[0]
-    state, dstate = state_of(st_ref, 0), state_of(st_ref, 1)
-    grad_b = gbc_ref[:, 0:LANES] + dot(lx_ref[...], dstate, ((1,), (0,)))
-    grad_c = gbc_ref[:, LANES:] + dot(edy_ref[...], state, ((1,), (0,)))
+    slabs = lx_ref.shape[1] // LANES
+    state, dstate = [
+        jnp.concatenate([state_of(st_ref, which, slab) for slab in range(slabs)], axis=1)
+        for which in range(2)
+    ]
+    grad_b = gbc_ref[:, 0:LANES] + dot(lx_ref[...], dstate, ((1,), (1,)))
+    grad_c = gbc_ref[:, LANES:] + dot(edy_ref[...], state, ((1,), (1,)))
     ext[0:rows, 0:LANES] = grad_b * sbc_ref[:, 0:LANES]
     ext[0:rows, LANES:] = grad_c * sbc_ref[:, LANES:]
     ext[rows:, :] = jnp.zeros((RIM, 2 * LANES), F32)
@@ -365,7 +383,7 @@
     core = core_ref[0]
     keep_ref[...] = total[pl.ds(pl.multiple_of(core * half, half), half), :]
     give_ref[...] = total[pl.ds(pl.multiple_of((1 - core) * half, half), half), :].astype(BF16)
-    d_leaving = dot(b_ref[0 : 2 * RIM, 0:LANES], dstate, ((1,), (1,)))[0:RIM]
+    d_leaving = dot(b_ref[0 : 2 * RIM, 0:LANES], dstate, ((1,), (0,)))[0:RIM]
     channels = rim_ref.shape[2]
     halo_ref[:, 0:channels] = rim_ref[0] + rim_ref[1] * d_leaving
     halo_ref[:, channels:] = ext[0:RIM, :]
@@ -403,88 +421,81 @@
     out_ref[...] = total[...].astype(BF16)
 
 
-def y_kernel(
-    head_dim, dy_hbm, yi_hbm, st_ref, bcc_ref, hv_ref,
-    y_hbm, enter_ref, dy_ref, yi_ref, y_ref, dy_sems, yi_sems, sems,
-):
-    rows, channels = dy_ref.shape
+def y_kernel(head_dim, st_ref, bcc_ref, hv_ref, yi_ref, edy_ref, y_hbm, enter_ref, y_ref, ys_ref, sems):
+    rows, channels = edy_ref.shape
     heads = hv_ref.shape[1]
     slabs = channels // LANES
-    yi_in = fetch(yi_hbm, yi_ref, yi_sems)
-    dy_in = fetch(dy_hbm, dy_ref, dy_sems)
-    state = state_of(st_ref, 0)
+    group = slabs // sems.shape[0]
     c_matrix = bcc_ref[:, LANES:]
-    entering = hv_ref[2]
-    along_enter = jnp.zeros((heads, rows), F32)
+    entering = columns(hv_ref[1])
     sent = []
     for slab in range(slabs):
         lanes = lanes_of(slab)
-        y_state = dot(c_matrix, state[lanes], ((1,), (1,)))
-        arrived(yi_in, slab)
+        y_state = dot(c_matrix, state_of(st_ref, 0, slab), ((1,), (0,)))
+        ys_ref[:, lanes] = y_state
         y_ref[:, lanes] = (yi_ref[:, lanes] + spread(entering, slab, head_dim) * y_state).astype(BF16)
-        group = slabs // sems.shape[0]
         if slab % group == group - 1:
             at = (slice(None), slice((slab + 1 - group) * LANES, (slab + 1) * LANES))
             sent.append(put(y_ref, y_hbm, sems.at[slab // group], at))
-        arrived(dy_in, slab)
-        along_enter = along_enter + head_sum(
-            dy_ref[:, lanes].astype(F32) * y_state, slab, head_dim, heads
+    enter_term = jnp.zeros((heads, rows), F32)
+    for slab in range(slabs):
+        lanes = lanes_of(slab)
+        enter_term = enter_term + head_sum(
+            edy_ref[:, lanes].astype(F32) * ys_ref[:, lanes], slab, head_dim, heads
         )
-    enter_ref[...] = along_enter
+    enter_ref[...] = enter_term
     for copy in sent:
         copy.wait()
 
 
 def x_kernel(
-    head_dim, xc_hbm, gs_hbm, ls_hbm, st_ref, bcc_ref, hv_ref, enter_ref, halo_ref, wx_ref,
-    gx_hbm, gdt_ref, xc_ref, gs_ref, ls_ref, gx_ref, ext, xc_sems, gs_sems, ls_sems, sems,
+    head_dim, gs_hbm, ls_hbm, st_ref, bcc_ref, hv_ref, lx_ref, enter_ref, halo_ref, wx_ref,
+    gx_hbm, gdt_ref, gs_ref, ls_ref, gx_ref, ext, gs_sems, ls_sems, sems,
 ):
-    rows, channels = xc_ref.shape
+    rows, channels = lx_ref.shape
     heads = hv_ref.shape[1]
     taps = wx_ref.shape[0]
     slabs = channels // LANES
+    group = slabs // sems.shape[0]
     gs_in = fetch(gs_hbm, gs_ref, gs_sems)
     ls_in = fetch(ls_hbm, ls_ref, ls_sems)
-    xc_in = fetch(xc_hbm, xc_ref, xc_sems)
-    state, dstate = state_of(st_ref, 0), state_of(st_ref, 1)
     b_matrix = bcc_ref[:, 0:LANES]
-    leave_step, leaving, entering, along_dt, z_diff, carry, decay, dt_gate = [
-        hv_ref[at] for at in range(8)
-    ]
-    along_enter = enter_ref[...]
-    along_leave = jnp.zeros((heads, rows), F32)
+    step, _, along_dt, z_diff, carry, decay, dt_gate = [hv_ref[at] for at in range(7)]
+    leave_term = jnp.zeros((heads, rows), F32)
+    overlap = jnp.zeros((heads, LANES), F32)
+    for slab in range(slabs):
+        lanes = lanes_of(slab)
+        dstate = state_of(st_ref, 1, slab)
+        product = state_of(st_ref, 0, slab).astype(F32) * dstate.astype(F32)
+        head = iota((heads, LANES), 1) // head_dim + slab * (LANES // head_dim)
+        own = iota((heads, LANES), 0) == head
+        overlap = overlap + jnp.where(own, jnp.sum(product, axis=0, keepdims=True), 0.0)
+        d_leaving = dot(b_matrix, dstate, ((1,), (0,)))
+        ext[0:rows, lanes] = d_leaving
+        leave_term = leave_term + head_sum(
+            lx_ref[:, lanes].astype(F32) * d_leaving, slab, head_dim, heads
+        )
+    final = jnp.sum(leave_term, axis=1, keepdims=True) + carry * jnp.sum(overlap, axis=1, keepdims=True)
+    d_cum = z_diff + enter_ref[...] - leave_term
+    d_cum = d_cum + jnp.where(iota((heads, rows), 1) == rows - 1, final, 0.0)
+    after = jnp.where(iota((rows, rows), 0) >= iota((rows, rows), 1), 1.0, 0.0)
+    d_log = dot(d_cum, after, ((1,), (0,)), HIGHEST)
+    gdt_ref[...] = (along_dt + leave_term / step - decay * d_log) * dt_gate
     ext[rows:, :] = halo_ref[:, 0:channels]
     sent = []
     for slab in range(slabs):
         lanes = lanes_of(slab)
-        d_leaving = dot(b_matrix, dstate[lanes], ((1,), (1,)))
         arrived(gs_in, slab)
         arrived(ls_in, slab)
-        ext[0:rows, lanes] = gs_ref[:, lanes] + ls_ref[:, lanes] * d_leaving
+        ext[0:rows, lanes] = gs_ref[:, lanes] + ls_ref[:, lanes] * ext[0:rows, lanes]
         w = wx_ref[:, lanes].astype(F32)
         out = w[taps - 1 : taps] * ext[0:rows, lanes]
         for tap in range(taps - 1):
             out = out + w[tap : tap + 1] * ext[pl.ds(taps - 1 - tap, rows), lanes]
         gx_ref[:, lanes] = out.astype(BF16)
-        group = slabs // sems.shape[0]
         if slab % group == group - 1:
             at = (slice(None), slice((slab + 1 - group) * LANES, (slab + 1) * LANES))
             sent.append(put(gx_ref, gx_hbm, sems.at[slab // group], at))
-        arrived(xc_in, slab)
-        along_leave = along_leave + head_sum(
-            xc_ref[:, lanes].astype(F32) * d_leaving, slab, head_dim, heads
-        )
-    product = state.astype(F32) * dstate.astype(F32)
-    owner = iota((heads, channels), 1) // head_dim
-    chosen = jnp.where(iota((heads, channels), 0) == owner, 1.0, 0.0)
-    overlap = jnp.sum(dot(chosen, product, ((1,), (0,)), HIGHEST), axis=1, keepdims=True)
-    leave_term = leave_step * along_leave
-    final = jnp.sum(leave_term, axis=1, keepdims=True) + carry * overlap
-    d_cum = z_diff + entering * along_enter - leave_term
-    d_cum = d_cum + jnp.where(iota((heads, rows), 1) == rows - 1, final, 0.0)
-    after = jnp.where(iota((rows, rows), 0) >= iota((rows, rows), 1), 1.0, 0.0)
-    d_log = dot(d_cum, after, ((1,), (0,)), HIGHEST)
-    gdt_ref[...] = (along_dt + leaving * along_leave - decay * d_log) * dt_gate
     for copy in sent:
         copy.wait()
 
@@ -551,18 +562,18 @@
     sent = ((count, 2 * part + RIM, LANES), BF16)
     states = ((count, 2 * part, LANES), BF16)
     sums, leave_top, dy_top, top, tail = call(
-        functools.partial(gather_kernel, head_dim, part),
+        functools.partial(gather_kernel, head_dim),
         "gather",
         [doc_starts, a_log],
         [x_raw, grad_y, bc_raw],
         [conv_x_w, conv_bc_w, dt_raw],
         [],
         [
-            ((2, channels, LANES), F32),
+            ((2, LANES, channels), F32),
             ((RIM, channels), F32),
             ((RIM, channels), F32),
             ((RIM, channels + wide), F32),
-            ((count, RIM, LANES), BF16),
+            ((RIM, LANES), BF16),
         ],
         [*inputs, ext, *input_sems],
     )
@@ -572,43 +583,54 @@
         [],
         [],
         [halo, sums, leave_top, dy_top, top, tail, conv_x_w, conv_bc_w],
+        [],
         [sent],
-        [],
-        [pltpu.VMEM(*sent), pltpu.VMEM((2 * RIM, channels + wide), F32), two],
+        [pltpu.VMEM((2 * RIM, channels + wide), F32)],
     )
     got = lax.all_to_all(send, "ctx", 0, 0)
-    xc, yi, gs, ls, lx, edy, bcc, gbc, sbc, hv, first = call(
+    scanned = call(
+        functools.partial(scan_kernel, head_dim),
+        "scan",
+        [],
+        [],
+        [got],
+        [states],
+        [],
+        [
+            pltpu.VMEM(*states),
+            pltpu.VMEM((count * RIM, LANES), F32),
+            pltpu.VMEM((count * RIM, channels // 2), F32),
+            sems((4,)),
+        ],
+    )
+    scanned, dt_later = lax.optimization_barrier((scanned, dt_raw))
+    gs, ls, yi, lx, edy, bcc, gbc, sbc, hv, first = call(
         functools.partial(intra_kernel, head_dim),
         "intra",
         [doc_starts, a_log, d_skip],
         [x_raw, grad_y, bc_raw],
-        [halo, conv_x_w, conv_bc_w, dt_raw],
-        [wide_bf, wide_f, wide_f, wide_f],
+        [halo, conv_x_w, conv_bc_w, dt_later],
+        [wide_f, wide_f],
         [
+            wide_f,
             wide_bf,
             wide_bf,
             ((rows, wide), BF16),
             ((rows, wide), F32),
             ((rows, wide), F32),
-            ((8, heads, rows), F32),
+            ((7, heads, rows), F32),
             ((2, RIM, channels), F32),
         ],
         [
             *inputs,
-            pltpu.VMEM(*wide_bf),
-            pltpu.VMEM(*wide_f),
             pltpu.VMEM(*wide_f),
             pltpu.VMEM(*wide_f),
             ext,
             pltpu.VMEM((rows, rows), F32),
             pltpu.VMEM((rows, rows), F32),
             *input_sems,
-            sems((8,)),
+            sems((4,)),
         ],
-    )
-    got, hv = lax.optimization_barrier((got, hv))
-    scanned = call(
-        scan_kernel, "scan", [], [], [got], [states], [], [pltpu.VMEM(*states), sems((count // 4,))]
     )
     st = lax.all_to_all(scanned, "ctx", 0, 0)
     half = rows // 2
@@ -629,24 +651,17 @@
     next_rim = shift_ctx(rim, -1)
     other = swap_core(give)
     st, keep = lax.optimization_barrier((st, keep))
-    y_out, along_enter = call(
+    y_out, enter_term = call(
         functools.partial(y_kernel, head_dim),
         "y_out",
         [],
-        [grad_y, yi],
-        [st, bcc, hv],
+        [],
+        [st, bcc, hv, yi, edy],
         [wide_bf],
         [((heads, rows), F32)],
-        [
-            pltpu.VMEM(*wide_bf),
-            pltpu.VMEM(*wide_f),
-            pltpu.VMEM(*wide_bf),
-            two,
-            two,
-            two,
-        ],
-    )
-    other, next_rim, along_enter = lax.optimization_barrier((other, next_rim, along_enter))
+        [pltpu.VMEM(*wide_bf), pltpu.VMEM(*wide_f), two],
+    )
+    other, next_rim, enter_term = lax.optimization_barrier((other, next_rim, enter_term))
     message = ((half + RIM, wide), BF16)
     joined = call(
         join_kernel,
@@ -664,17 +679,15 @@
         functools.partial(x_kernel, head_dim),
         "grad_x",
         [],
-        [xc, gs, ls],
-        [st, bcc, hv, along_enter, next_rim, conv_x_w],
+        [gs, ls],
+        [st, bcc, hv, lx, enter_term, next_rim, conv_x_w],
         [wide_bf],
         [((heads, rows), F32)],
         [
-            pltpu.VMEM(*wide_bf),
             pltpu.VMEM(*wide_f),
             pltpu.VMEM(*wide_f),
             pltpu.VMEM(*wide_bf),
             pltpu.VMEM((rows + RIM, channels), F32),
-            two,
             two,
             two,
             two,

time: 84.3 us -> 83.4 us (0.989)
  blocking collectives: 0 us -> 27 us
  waiting for transfers between devices: 23.8 us -> 8.91 us
  starting transfers between devices: 32.2 us -> 22.1 us
  Pallas kernels: 25.5 us -> 22.1 us
    all_to_all x0 -> x1, blocking collectives: none -> 27 us  [body(): got = lax.all_to_all(send, 'ctx', 0, 0)]
    all_to_all x1 -> x0, starting transfers between devices: 10.4 us -> none  [body(): got = lax.all_to_all(send, 'ctx', 0, 0)]
    all_to_all x1, waiting for transfers between devices: 14.8 us -> 4.95 us  [body(): st = lax.all_to_all(scanned, 'ctx', 0, 0)]
    all_to_all x1 -> x0, waiting for transfers between devices: 6.89 us -> none  [body(): got = lax.all_to_all(send, 'ctx', 0, 0)]
    pallas_call x10, Pallas kernels: 25.5 us -> 22.1 us  [call(): pl.pallas_call(kernel, name=name, out_shape=out if many else out[0], in_s...]
    ppermute x2, waiting for transfers between devices: 1.27 us -> 3.05 us  [shift_ctx(): return lax.ppermute(values, 'ctx', pairs)]
  transfers between devices with their start and end apart: 9 -> 8, of which waited for: 4 -> 3; matrix products, arithmetic and copies ran while one was open for 0% -> 0% of each run, Pallas kernels for 26% -> 23%
where the time goes in v4:
time: 83.4 us; the launch traced here: 83 us
  blocking collectives  27 us (32%)
  starting transfers between devices  22.1 us (26%)
  Pallas kernels  22.1 us (26%)
  waiting for transfers between devices  8.91 us (11%)
  between operations  1.49 us (2%)
  local copies, waits for them, and re-layouts  1.37 us (2%)
    all_to_all x1, blocking collectives, body(): got = lax.all_to_all(send, 'ctx', 0, 0)  27 us
    pallas_call x10, Pallas kernels, call(): pl.pallas_call(kernel, name=name, out_shape=out if many else out[0], in_s...  22.1 us
    ppermute x2, starting transfers between devices, swap_core(): return lax.ppermute(values, 'head', [(i, i ^ 1) for i in range(size)])  6.18 us
    ppermute x2, starting transfers between devices, shift_ctx(): return lax.ppermute(values, 'ctx', pairs)  6.06 us
    all_to_all x1, starting transfers between devices, body(): st = lax.all_to_all(scanned, 'ctx', 0, 0)  5.96 us
    all_to_all x1, waiting for transfers between devices, body(): st = lax.all_to_all(scanned, 'ctx', 0, 0)  4.95 us
    ppermute x3, starting transfers between devices, around(): lax.ppermute(values, 'head', [(i, (i + 2 * by) % size) for i in range(siz...  3.85 us
    ppermute x2, waiting for transfers between devices, shift_ctx(): return lax.ppermute(values, 'ctx', pairs)  3.05 us
  transfers between devices with their start and end apart: 8, of which 3 were waited for; matrix products, arithmetic and copies ran while one was open for 0% of the time, Pallas kernels for 23%

profile of v4, /device:TPU:7, one launch (start us, length us, event | category | flops | bytes accessed | tf_op | source)
XLA Modules:
  0.0 83.0 jit_solution(5294970661126060597)
XLA Ops:
  0.6 0.0 slice-start
  0.6 0.0 slice-start.1
  0.7 0.7 slice-done
  1.4 0.0 slice-done.1
  1.4 0.0 copy-start
  1.4 0.0 copy-start.1
  1.4 0.0 copy-start.2
  1.4 0.0 copy-start.3
  1.4 3.6 %collective-permute-start = (bf16[8,1280]{1,0:T(8,128)(2,1)S(1)}, bf16[8,1280]{1,0:T(8,128)(2,1)S(1)}, u32[]{:S(2)}, u32[]{:S(2)}) collective-permute-start(bf16[8,1280]{1,0:T(8,128)(2,1)S(1)} %pad_maximum_fusion), channel_id=1, source_target_pairs={{0,8},{8,16},{16,24},{24,32},{32,40},{40,48},{48,56},{56,64},{64,7... | collective-permute-start | bytes 61448 | tf_op jit(solution)/shard_map/ppermute | solution.py:534
  5.6 0.0 copy-done
  5.6 0.0 copy-done.1
  5.7 0.0 copy-done.2
  5.7 0.0 copy-done.3
  5.7 4.3 %gather.1 = (f32[2,128,1024]{2,1,0:T(8,128)S(1)}, f32[8,1024]{1,0:T(8,128)S(1)}, f32[8,1024]{1,0:T(8,128)S(1)}, f32[8,1280]{1,0:T(8,128)S(1)}, bf16[8,128]{1,0:T(8,128)(2,1)S(1)}) custom-call(s32[1]{0:T(128)S(6)} %copy.13.doc_ref, f32[16]{0:T(128)S(1)} %copy-done.3, bf16[256,1024]{1,0:T(8,128)(2,1)} %x_hbm.3, bf16[256,1024]{1,0:T(8,128)(2,1)} %dy_hbm.3, ...), custom_call_target="tpu_custom_call" | custom-call | tf_op jit(solution)/shard_map/gather/pallas_call | solution.py:520
  10.0 0.0 collective-permute-done.halo_ref
  10.0 0.5 send.1
  10.5 27.0 %all_to_all.10.got_ref = bf16[32,72,128]{2,1,0:T(8,128)(2,1)S(1)} all-to-all(bf16[32,72,128]{2,1,0:T(8,128)(2,1)S(1)} %send.1), channel_id=1, replica_groups=mesh['ctx'=32,'head'=8] {'ctx'}, dimensions={0} | all-to-all | bytes 1179648 | tf_op jit(solution)/shard_map/all_to_all | solution.py:590
  37.5 1.2 %scan.1 = bf16[32,64,128]{2,1,0:T(8,128)(2,1)} custom-call(bf16[32,72,128]{2,1,0:T(8,128)(2,1)S(1)} %all_to_all.10.got_ref), custom_call_target="tpu_custom_call" | custom-call | tf_op jit(solution)/shard_map/scan/pallas_call | solution.py:520
  38.7 6.0 %all-to-all-start.1 = ((bf16[32,64,128]{2,1,0:T(8,128)(2,1)}), bf16[32,64,128]{2,1,0:T(8,128)(2,1)S(1)}, u32[]{:S(2)}, u32[]{:S(2)}) async-start(bf16[32,64,128]{2,1,0:T(8,128)(2,1)} %scan.1), calls=%async_computation.1 | async-start | bytes 1048576 | tf_op jit(solution)/shard_map/all_to_all | solution.py:635
  44.7 0.0 copy-start.4
  44.7 0.6 copy-done.4
  45.4 9.2 %intra.1 = (f32[256,1024]{1,0:T(8,128)}, f32[256,1024]{1,0:T(8,128)}, f32[256,1024]{1,0:T(8,128)S(1)}, bf16[256,1024]{1,0:T(8,128)(2,1)S(1)}, bf16[256,1024]{1,0...) custom-call(s32[1]{0:T(128)S(6)} %copy.13.doc_ref, ...), custom_call_target="tpu_custom_call" | custom-call | tf_op jit(solution)/shard_map/intra/pallas_call | solution.py:520
  54.5 5.0 %all-to-all-done.1.st_ref = bf16[32,64,128]{2,1,0:T(8,128)(2,1)S(1)} async-done(((bf16[32,64,128]{2,1,0:T(8,128)(2,1)}), bf16[32,64,128]{2,1,0:T(8,128)(2,1)S(1)}, u32[]{:S(2)}, u32[]{:S(2)}) %all-to-all-start.1) | async-done | bytes 524320 | tf_op jit(solution)/shard_map/all_to_all | solution.py:635
  59.5 0.5 grad_bc.1
  60.0 3.5 %collective-permute-start.1 = (bf16[128,256]{1,0:T(8,128)(2,1)S(1)}, bf16[128,256]{1,0:T(8,128)(2,1)S(1)}, u32[]{:S(2)}, u32[]{:S(2)}) collective-permute-start(bf16[128,256]{1,0:T(8,128)(2,1)S(1)} %get-tuple-element.58), channel_id=1, source_target_pairs={{0,1},{1,0},{2,3},{3,2},{4,5},{5,4},{6,7},{7,6},{8,9},{9,8},{10,11... | collective-permute-start | bytes 196616 | tf_op jit(solution)/shard_map/ppermute | solution.py:539
  63.5 2.5 %collective-permute-start.2 = (f32[8,1280]{1,0:T(8,128)S(1)}, f32[8,1280]{1,0:T(8,128)S(1)}, u32[]{:S(2)}, u32[]{:S(2)}) collective-permute-start(f32[8,1280]{1,0:T(8,128)S(1)} %get-tuple-element.59), channel_id=1, source_target_pairs={{8,0},{16,8},{24,16},{32,24},{40,32},{48,40},{56,48},{64,56},{72,6... | collective-permute-start | bytes 122888 | tf_op jit(solution)/shard_map/ppermute | solution.py:534
  66.0 1.3 %y_out.1 = (bf16[256,1024]{1,0:T(8,128)(2,1)}, f32[16,256]{1,0:T(8,128)S(1)}) custom-call(bf16[32,64,128]{2,1,0:T(8,128)(2,1)S(1)} %all-to-all-done.1.st_ref, bf16[256,256]{1,0:T(8,128)(2,1)S(1)} %get-tuple-element.47.b_ref.bcc_ref, f32[7,16,256]{2,1,0:T(8,128)S(1)} %get-tuple-element.53.hv_ref, f32[256,1024]{1,0:T(8,128)S(1)} %get-tuple-element.54.yi_ref, ...), custom_call_target="tpu_custom_call" | custom-call | tf_op jit(solution)/shard_map/y_out/pallas_call | solution.py:520
  67.3 3.0 %collective-permute-done.2.halo_ref = f32[8,1280]{1,0:T(8,128)S(1)} collective-permute-done((f32[8,1280]{1,0:T(8,128)S(1)}, f32[8,1280]{1,0:T(8,128)S(1)}, u32[]{:S(2)}, u32[]{:S(2)}) %collective-permute-start.2) | collective-permute-done | bytes 40992 | tf_op jit(solution)/shard_map/ppermute | solution.py:534
  70.4 0.0 collective-permute-done.1.got_ref
  70.4 2.8 %collective-permute-start.5 = (bf16[136,256]{1,0:T(8,128)(2,1)S(1)}, bf16[136,256]{1,0:T(8,128)(2,1)S(1)}, u32[]{:S(2)}, u32[]{:S(2)}) collective-permute-start(bf16[136,256]{1,0:T(8,128)(2,1)S(1)} %join.1.refs_0_), channel_id=1, source_target_pairs={{0,6},{1,7},{2,0},{3,1},{4,2},{5,3},{6,4},{7,5},{8,14},{9,15},{10,... | collective-permute-start | bytes 208904 | tf_op jit(solution)/shard_map/ppermute | solution.py:544
  73.2 0.3 collective-permute-start.4
  73.6 0.7 collective-permute-start.3
  74.3 4.4 %grad_x.1 = (bf16[256,1024]{1,0:T(8,128)(2,1)}, f32[16,256]{1,0:T(8,128)}) custom-call(f32[256,1024]{1,0:T(8,128)} %get-tuple-element.56.gs_hbm, f32[256,1024]{1,0:T(8,128)} %get-tuple-element.57.ls_hbm, bf16[32,64,128]{2,1,0:T(8,128)(2,1)S(1)} %all-to-all-done.1.st_ref, bf16[256,256]{1,0:T(8,128)(2,1)S(1)} %get-tuple-element.47.b_ref.bcc_ref, ...), custom_call_target="tpu_custom_call" | custom-call | tf_op jit(solution)/shard_map/grad_x/pallas_call | solution.py:520
  78.6 0.0 collective-permute-done.5.refs_3_
  78.7 0.0 collective-permute-done.4.refs_2_
  78.7 0.0 collective-permute-done.3.refs_1_
  78.7 2.6 %collective-permute-start.6 = (bf16[136,256]{1,0:T(8,128)(2,1)S(1)}, bf16[136,256]{1,0:T(8,128)(2,1)S(1)}, u32[]{:S(2)}, u32[]{:S(2)}) collective-permute-start(bf16[136,256]{1,0:T(8,128)(2,1)S(1)} %sum.1.mine_ref), channel_id=1, source_target_pairs={{0,1},{1,0},{2,3},{3,2},{4,5},{5,4},{6,7},{7,6},{8,9},{9,8},{10,11... | collective-permute-start | bytes 208904 | tf_op jit(solution)/shard_map/ppermute | solution.py:539
  81.4 0.9 %collective-permute-done.6.got_ref = bf16[136,256]{1,0:T(8,128)(2,1)S(1)} collective-permute-done((bf16[136,256]{1,0:T(8,128)(2,1)S(1)}, bf16[136,256]{1,0:T(8,128)(2,1)S(1)}, u32[]{:S(2)}, u32[]{:S(2)}) %collective-permute-start.6) | collective-permute-done | bytes 69664 | tf_op jit(solution)/shard_map/ppermute | solution.py:539
  82.3 0.7 last.1
  (3 shorter events, 0.1 us)
Async XLA Ops:
  0.6 0.7 slice-start
  0.6 0.7 slice-start.1
  1.4 4.3 %copy-start = (bf16[4,1024]{1,0:T(4,128)(2,1)S(1)}, bf16[4,1024]{1,0:T(4,128)(2,1)}, u32[]{:S(2)}) copy-start(bf16[4,1024]{1,0:T(4,128)(2,1)} %wx_ref.7) | copy-start | bytes 24580
  1.4 4.3 %copy-start.1 = (f32[16,256]{1,0:T(8,128)S(1)}, f32[16,256]{1,0:T(8,128)}, u32[]{:S(2)}) copy-start(f32[16,256]{1,0:T(8,128)} %dt_ref.2) | copy-start | bytes 49156
  1.4 4.3 %copy-start.2 = (bf16[4,256]{1,0:T(4,128)(2,1)S(1)}, bf16[4,256]{1,0:T(4,128)(2,1)}, u32[]{:S(2)}) copy-start(bf16[4,256]{1,0:T(4,128)(2,1)} %wbc_ref.9) | copy-start | bytes 6148
  1.4 4.3 %copy-start.3 = (f32[16]{0:T(128)S(1)}, f32[16]{0:T(128)}, u32[]{:S(2)}) copy-start(f32[16]{0:T(128)} %a_log_ref.3) | copy-start | bytes 196
  1.4 8.6 %collective-permute-start = (bf16[8,1280]{1,0:T(8,128)(2,1)S(1)}, bf16[8,1280]{1,0:T(8,128)(2,1)S(1)}, u32[]{:S(2)}, u32[]{:S(2)}) collective-permute-start(bf16[8,1280]{1,0:T(8,128)(2,1)S(1)} %pad_maximum_fusion), channel_id=1, source_target_pairs={{0,8},{8,16},{16,24},{24,32},{32,40},{40,48},{48,56},{56,64},{64,7... | collective-permute-start | bytes 61448 | tf_op jit(solution)/shard_map/ppermute | solution.py:534
  38.7 20.8 %all-to-all-start.1 = ((bf16[32,64,128]{2,1,0:T(8,128)(2,1)}), bf16[32,64,128]{2,1,0:T(8,128)(2,1)S(1)}, u32[]{:S(2)}, u32[]{:S(2)}) async-start(bf16[32,64,128]{2,1,0:T(8,128)(2,1)} %scan.1), calls=%async_computation.1 | async-start | bytes 1048576 | tf_op jit(solution)/shard_map/all_to_all | solution.py:635
  44.7 0.7 copy-start.4
  60.0 10.4 %collective-permute-start.1 = (bf16[128,256]{1,0:T(8,128)(2,1)S(1)}, bf16[128,256]{1,0:T(8,128)(2,1)S(1)}, u32[]{:S(2)}, u32[]{:S(2)}) collective-permute-start(bf16[128,256]{1,0:T(8,128)(2,1)S(1)} %get-tuple-element.58), channel_id=1, source_target_pairs={{0,1},{1,0},{2,3},{3,2},{4,5},{5,4},{6,7},{7,6},{8,9},{9,8},{10,11... | collective-permute-start | bytes 196616 | tf_op jit(solution)/shard_map/ppermute | solution.py:539
  63.5 6.8 %collective-permute-start.2 = (f32[8,1280]{1,0:T(8,128)S(1)}, f32[8,1280]{1,0:T(8,128)S(1)}, u32[]{:S(2)}, u32[]{:S(2)}) collective-permute-start(f32[8,1280]{1,0:T(8,128)S(1)} %get-tuple-element.59), channel_id=1, source_target_pairs={{8,0},{16,8},{24,16},{32,24},{40,32},{48,40},{56,48},{64,56},{72,6... | collective-permute-start | bytes 122888 | tf_op jit(solution)/shard_map/ppermute | solution.py:534
  70.4 8.2 %collective-permute-start.5 = (bf16[136,256]{1,0:T(8,128)(2,1)S(1)}, bf16[136,256]{1,0:T(8,128)(2,1)S(1)}, u32[]{:S(2)}, u32[]{:S(2)}) collective-permute-start(bf16[136,256]{1,0:T(8,128)(2,1)S(1)} %join.1.refs_0_), channel_id=1, source_target_pairs={{0,6},{1,7},{2,0},{3,1},{4,2},{5,3},{6,4},{7,5},{8,14},{9,15},{10,... | collective-permute-start | bytes 208904 | tf_op jit(solution)/shard_map/ppermute | solution.py:544
  73.2 5.4 %collective-permute-start.4 = (bf16[136,256]{1,0:T(8,128)(2,1)S(1)}, bf16[136,256]{1,0:T(8,128)(2,1)S(1)}, u32[]{:S(2)}, u32[]{:S(2)}) collective-permute-start(bf16[136,256]{1,0:T(8,128)(2,1)S(1)} %join.1.refs_0_), channel_id=1, source_target_pairs={{0,4},{1,5},{2,6},{3,7},{4,0},{5,1},{6,2},{7,3},{8,12},{9,13},{10,... | collective-permute-start | bytes 208904 | tf_op jit(solution)/shard_map/ppermute | solution.py:544
  73.6 5.1 %collective-permute-start.3 = (bf16[136,256]{1,0:T(8,128)(2,1)S(1)}, bf16[136,256]{1,0:T(8,128)(2,1)S(1)}, u32[]{:S(2)}, u32[]{:S(2)}) collective-permute-start(bf16[136,256]{1,0:T(8,128)(2,1)S(1)} %join.1.refs_0_), channel_id=1, source_target_pairs={{0,2},{1,3},{2,4},{3,5},{4,6},{5,7},{6,0},{7,1},{8,10},{9,11},{10,... | collective-permute-start | bytes 208904 | tf_op jit(solution)/shard_map/ppermute | solution.py:544
  78.7 3.5 %collective-permute-start.6 = (bf16[136,256]{1,0:T(8,128)(2,1)S(1)}, bf16[136,256]{1,0:T(8,128)(2,1)S(1)}, u32[]{:S(2)}, u32[]{:S(2)}) collective-permute-start(bf16[136,256]{1,0:T(8,128)(2,1)S(1)} %sum.1.mine_ref), channel_id=1, source_target_pairs={{0,1},{1,0},{2,3},{3,2},{4,5},{5,4},{6,7},{7,6},{8,9},{9,8},{10,11... | collective-permute-start | bytes 208904 | tf_op jit(solution)/shard_map/ppermute | solution.py:539

commit v5 on v4

--- a/solution.py
+++ b/solution.py
@@ -41,20 +41,23 @@
     return dot(diagonal(values.shape[1]), both, ((1,), (1,))).astype(BF16)
 
 
-def spread(pairs, slab, head_dim):
+def spread(pairs, slab, head_dim, width=LANES):
     heads = pairs.shape[1] // 2
-    row = iota((2 * heads, LANES), 0)
-    head = iota((2 * heads, LANES), 1) // head_dim + slab * (LANES // head_dim)
+    row = iota((2 * heads, width), 0)
+    head = iota((2 * heads, width), 1) // head_dim + slab * (width // head_dim)
     chosen = jnp.where((row == head) | (row == head + heads), 1.0, 0.0).astype(BF16)
     return dot(pairs, chosen, ((1,), (0,)))
 
 
 def head_sum(values, slab, head_dim, heads):
-    high, low = halves(values)
-    both = jnp.concatenate([high, low], axis=1)
-    head = (iota((heads, 2 * LANES), 1) % LANES) // head_dim + slab * (LANES // head_dim)
-    chosen = jnp.where(iota((heads, 2 * LANES), 0) == head, 1.0, 0.0).astype(BF16)
-    return dot(chosen, both, ((1,), (1,)))
+    width = values.shape[1]
+    head = (iota((heads, width), 1) % LANES) // head_dim + slab * (LANES // head_dim)
+    chosen = jnp.where(iota((heads, width), 0) == head, 1.0, 0.0).astype(BF16)
+    return dot(chosen, values.astype(BF16), ((1,), (1,)))
+
+
+def head_sum_exact(values, slab, head_dim, heads):
+    return head_sum(jnp.concatenate(halves(values), axis=1), slab, head_dim, heads)
 
 
 def per_head(ref, heads, rows):
@@ -114,16 +117,16 @@
 
 def load_ext(ext, halo_ref, values, at, lanes):
     if halo_ref is None:
-        ext[0:RIM, at] = jnp.zeros((RIM, LANES), F32)
+        ext[0:RIM, at] = jnp.zeros((RIM, at.stop - at.start), F32)
     else:
         ext[0:RIM, at] = halo_ref[:, at].astype(F32)
     ext[RIM : RIM + values.shape[0], at] = values[:, lanes].astype(F32)
 
 
-def filtered(ext, w_ref, at, w_at, rows):
+def filtered(ext, w_ref, at, w_at, rows, width=LANES):
     taps = w_ref.shape[0]
-    lanes = pl.ds(at, LANES)
-    w = w_ref[:, w_at : w_at + LANES].astype(F32)
+    lanes = pl.ds(at, width)
+    w = w_ref[:, w_at : w_at + width].astype(F32)
     total = w[0:1] * ext[pl.ds(RIM - taps + 1, rows), lanes]
     for tap in range(1, taps):
         total = total + w[tap : tap + 1] * ext[pl.ds(RIM - taps + 1 + tap, rows), lanes]
@@ -148,24 +151,25 @@
     high, low = [half.astype(F32) for half in halves(carry)]
     at = iota((RIM, LANES), 0)
     tail_ref[...] = jnp.where(at == 0, high, jnp.where(at == 1, low, 0.0)).astype(BF16)
-    below = iota((rows, LANES), 0) >= RIM
     bc = []
     for half in range(2):
         arrived(bc_in, half)
         load_ext(ext, None, bc_ref, lanes_of(channels // LANES + half), lanes_of(half))
         pre = filtered(ext, wbc_ref, channels + half * LANES, half * LANES, rows)
         bc.append((pre * sigmoid(pre)).T.astype(BF16))
-    for slab in range(channels // LANES):
-        lanes = lanes_of(slab)
+    width = LANES
+    below = iota((rows, width), 0) >= RIM
+    for slab in range(channels // width):
+        lanes = slice(slab * width, (slab + 1) * width)
         arrived(x_in, slab)
         load_ext(ext, None, x_ref, lanes, lanes)
-        pre = filtered(ext, wx_ref, slab * LANES, slab * LANES, rows)
+        pre = filtered(ext, wx_ref, slab * width, slab * width, rows, width)
         x_conv = (pre * sigmoid(pre)).astype(BF16).astype(F32)
-        leave = spread(leave_step, slab, head_dim)
+        leave = spread(leave_step, slab, head_dim, width)
         leaving_x = jnp.where(below, x_conv * leave, 0.0).astype(BF16)
+        sum_ref[0, :, lanes] = dot(bc[0], leaving_x, ((1,), (0,)))
         arrived(dy_in, slab)
-        enter_dy = dy_ref[:, lanes].astype(F32) * spread(entering, slab, head_dim)
-        sum_ref[0, :, lanes] = dot(bc[0], leaving_x, ((1,), (0,)))
+        enter_dy = dy_ref[:, lanes].astype(F32) * spread(entering, slab, head_dim, width)
         masked = jnp.where(below, enter_dy, 0.0).astype(BF16)
         sum_ref[1, :, lanes] = dot(bc[1], masked, ((1,), (0,)))
         ls_ref[:, lanes] = leave[0:RIM]
@@ -325,8 +329,8 @@
             at = (slice(None), slice((slab + 1 - group) * LANES, (slab + 1) * LANES))
             sent.append(put(gs_ref, gs_hbm, out_sems.at[slab // group * 2], at))
             sent.append(put(ls_ref, ls_hbm, out_sems.at[slab // group * 2 + 1], at))
-        along_dt = along_dt + head_sum(x_conv * d_scaled, slab, head_dim, heads)
-        z_diff = z_diff + head_sum(
+        along_dt = along_dt + head_sum_exact(x_conv * d_scaled, slab, head_dim, heads)
+        z_diff = z_diff + head_sum_exact(
             dy * intra - scaled.astype(F32) * d_scaled, slab, head_dim, heads
         )
     d_gram = dgram[...]
@@ -448,19 +452,16 @@
         copy.wait()
 
 
-def x_kernel(
-    head_dim, gs_hbm, ls_hbm, st_ref, bcc_ref, hv_ref, lx_ref, enter_ref, halo_ref, wx_ref,
-    gx_hbm, gdt_ref, gs_ref, ls_ref, gx_ref, ext, gs_sems, ls_sems, sems,
+def xc_kernel(
+    head_dim, gs_hbm, ls_hbm, st_ref, bcc_ref, lx_ref,
+    g_ref, leave_ref, overlap_ref, gs_ref, ls_ref, gs_sems, ls_sems,
 ):
     rows, channels = lx_ref.shape
-    heads = hv_ref.shape[1]
-    taps = wx_ref.shape[0]
+    heads = leave_ref.shape[0]
     slabs = channels // LANES
-    group = slabs // sems.shape[0]
     gs_in = fetch(gs_hbm, gs_ref, gs_sems)
     ls_in = fetch(ls_hbm, ls_ref, ls_sems)
     b_matrix = bcc_ref[:, 0:LANES]
-    step, _, along_dt, z_diff, carry, decay, dt_gate = [hv_ref[at] for at in range(7)]
     leave_term = jnp.zeros((heads, rows), F32)
     overlap = jnp.zeros((heads, LANES), F32)
     for slab in range(slabs):
@@ -471,33 +472,55 @@
         own = iota((heads, LANES), 0) == head
         overlap = overlap + jnp.where(own, jnp.sum(product, axis=0, keepdims=True), 0.0)
         d_leaving = dot(b_matrix, dstate, ((1,), (0,)))
-        ext[0:rows, lanes] = d_leaving
+        g_ref[:, lanes] = d_leaving
         leave_term = leave_term + head_sum(
             lx_ref[:, lanes].astype(F32) * d_leaving, slab, head_dim, heads
         )
+    leave_ref[...] = leave_term
+    overlap_ref[...] = overlap
+    for slab in range(slabs):
+        lanes = lanes_of(slab)
+        arrived(gs_in, slab)
+        arrived(ls_in, slab)
+        g_ref[:, lanes] = gs_ref[:, lanes] + ls_ref[:, lanes] * g_ref[:, lanes]
+
+
+def x_kernel(g_ref, halo_ref, wx_ref, gx_hbm, gx_ref, ext, sems):
+    rows, channels = g_ref.shape
+    taps = wx_ref.shape[0]
+    slabs = channels // LANES
+    group = slabs // sems.shape[0]
+    low = rows - RIM
+    ext[0:RIM, :] = g_ref[low:, :]
+    ext[RIM:, :] = halo_ref[:, 0:channels]
+    sent = []
+    for slab in range(slabs):
+        lanes = lanes_of(slab)
+        w = wx_ref[:, lanes].astype(F32)
+        body = w[taps - 1 : taps] * g_ref[0:low, lanes]
+        edge = w[taps - 1 : taps] * ext[0:RIM, lanes]
+        for tap in range(taps - 1):
+            ahead = taps - 1 - tap
+            body = body + w[tap : tap + 1] * g_ref[pl.ds(ahead, low), lanes]
+            edge = edge + w[tap : tap + 1] * ext[pl.ds(ahead, RIM), lanes]
+        gx_ref[:, lanes] = jnp.concatenate([body, edge], axis=0).astype(BF16)
+        if slab % group == group - 1:
+            at = (slice(None), slice((slab + 1 - group) * LANES, (slab + 1) * LANES))
+            sent.append(put(gx_ref, gx_hbm, sems.at[slab // group], at))
+    for copy in sent:
+        copy.wait()
+
+
+def dt_kernel(hv_ref, enter_ref, leave_ref, overlap_ref, gdt_ref):
+    heads, rows = leave_ref.shape
+    step, _, along_dt, z_diff, carry, decay, dt_gate = [hv_ref[at] for at in range(7)]
+    leave_term, overlap = leave_ref[...], overlap_ref[...]
     final = jnp.sum(leave_term, axis=1, keepdims=True) + carry * jnp.sum(overlap, axis=1, keepdims=True)
     d_cum = z_diff + enter_ref[...] - leave_term
     d_cum = d_cum + jnp.where(iota((heads, rows), 1) == rows - 1, final, 0.0)
     after = jnp.where(iota((rows, rows), 0) >= iota((rows, rows), 1), 1.0, 0.0)
     d_log = dot(d_cum, after, ((1,), (0,)), HIGHEST)
     gdt_ref[...] = (along_dt + leave_term / step - decay * d_log) * dt_gate
-    ext[rows:, :] = halo_ref[:, 0:channels]
-    sent = []
-    for slab in range(slabs):
-        lanes = lanes_of(slab)
-        arrived(gs_in, slab)
-        arrived(ls_in, slab)
-        ext[0:rows, lanes] = gs_ref[:, lanes] + ls_ref[:, lanes] * ext[0:rows, lanes]
-        w = wx_ref[:, lanes].astype(F32)
-        out = w[taps - 1 : taps] * ext[0:rows, lanes]
-        for tap in range(taps - 1):
-            out = out + w[tap : tap + 1] * ext[pl.ds(taps - 1 - tap, rows), lanes]
-        gx_ref[:, lanes] = out.astype(BF16)
-        if slab % group == group - 1:
-            at = (slice(None), slice((slab + 1 - group) * LANES, (slab + 1) * LANES))
-            sent.append(put(gx_ref, gx_hbm, sems.at[slab // group], at))
-    for copy in sent:
-        copy.wait()
 
 
 def smem():
@@ -661,7 +684,19 @@
         [((heads, rows), F32)],
         [pltpu.VMEM(*wide_bf), pltpu.VMEM(*wide_f), two],
     )
-    other, next_rim, enter_term = lax.optimization_barrier((other, next_rim, enter_term))
+    grad_xc, leave_term, overlap = call(
+        functools.partial(xc_kernel, head_dim),
+        "grad_xc",
+        [],
+        [gs, ls],
+        [st, bcc, lx],
+        [],
+        [wide_f, ((heads, rows), F32), ((heads, LANES), F32)],
+        [pltpu.VMEM(*wide_f), pltpu.VMEM(*wide_f), two, two],
+    )
+    other, next_rim, enter_term, leave_term = lax.optimization_barrier(
+        (other, next_rim, enter_term, leave_term)
+    )
     message = ((half + RIM, wide), BF16)
     joined = call(
         join_kernel,
@@ -675,27 +710,24 @@
     )
     ring = lax.axis_size("head") // 2
     pieces = [joined] + [around(joined, by) for by in range(1, ring)]
-    grad_x, grad_dt = call(
-        functools.partial(x_kernel, head_dim),
+    grad_x = call(
+        x_kernel,
         "grad_x",
         [],
-        [gs, ls],
-        [st, bcc, hv, lx, enter_term, next_rim, conv_x_w],
+        [],
+        [grad_xc, next_rim, conv_x_w],
         [wide_bf],
-        [((heads, rows), F32)],
-        [
-            pltpu.VMEM(*wide_f),
-            pltpu.VMEM(*wide_f),
-            pltpu.VMEM(*wide_bf),
-            pltpu.VMEM((rows + RIM, channels), F32),
-            two,
-            two,
-            two,
-        ],
-    )
-    pieces, grad_dt = lax.optimization_barrier((pieces, grad_dt))
+        [],
+        [pltpu.VMEM(*wide_bf), pltpu.VMEM((2 * RIM, channels), F32), sems((4,))],
+    )
+    pieces, grad_x = lax.optimization_barrier((pieces, grad_x))
     summed = call(sum_kernel, "sum", [], [], pieces, [], [message])
+    summed, leave_term = lax.optimization_barrier((summed, leave_term))
     swapped = swap_core(summed)
+    grad_dt = call(
+        dt_kernel, "grad_dt", [], [], [hv, enter_term, leave_term, overlap], [], [((heads, rows), F32)]
+    )
+    swapped, grad_dt = lax.optimization_barrier((swapped, grad_dt))
     grad_bc = call(
         last_kernel,
         "last",

time: 83.4 us -> 82.4 us (0.988)
  waiting for transfers between devices: 8.91 us -> 7.76 us
    ppermute x2, waiting for transfers between devices: 3.05 us -> 1.21 us  [shift_ctx(): return lax.ppermute(values, 'ctx', pairs)]
    ppermute x3, waiting for transfers between devices: 0.01 us -> 1.56 us  [around(): lax.ppermute(values, 'head', [(i, (i + 2 * by) % size) for i in range(siz...]
    ppermute x3, starting transfers between devices: 3.85 us -> 5.06 us  [around(): lax.ppermute(values, 'head', [(i, (i + 2 * by) % size) for i in range(siz...]
    ppermute x2, waiting for transfers between devices: 0.91 us -> 0.03 us  [swap_core(): return lax.ppermute(values, 'head', [(i, i ^ 1) for i in range(size)])]
    pallas_call x10 -> x12, Pallas kernels: 22.1 us -> 21.5 us  [call(): pl.pallas_call(kernel, name=name, out_shape=out if many else out[0], in_s...]
  transfers between devices with their start and end apart: 8 -> 8, of which waited for: 3 -> 4; matrix products, arithmetic and copies ran while one was open for 0% -> 0% of each run, Pallas kernels for 23% -> 23%
where the time goes in v5:
time: 82.4 us; the launch traced here: 81.9 us
  blocking collectives  27 us (33%)
  starting transfers between devices  22.8 us (28%)
  Pallas kernels  21.5 us (26%)
  waiting for transfers between devices  7.76 us (9%)
  between operations  1.48 us (2%)
  local copies, waits for them, and re-layouts  1.37 us (2%)
    all_to_all x1, blocking collectives, body(): got = lax.all_to_all(send, 'ctx', 0, 0)  27 us
    pallas_call x12, Pallas kernels, call(): pl.pallas_call(kernel, name=name, out_shape=out if many else out[0], in_s...  21.5 us
    ppermute x2, starting transfers between devices, shift_ctx(): return lax.ppermute(values, 'ctx', pairs)  6.06 us
    all_to_all x1, starting transfers between devices, body(): st = lax.all_to_all(scanned, 'ctx', 0, 0)  5.95 us
    ppermute x2, starting transfers between devices, swap_core(): return lax.ppermute(values, 'head', [(i, i ^ 1) for i in range(size)])  5.69 us
    ppermute x3, starting transfers between devices, around(): lax.ppermute(values, 'head', [(i, (i + 2 * by) % size) for i in range(siz...  5.06 us
    all_to_all x1, waiting for transfers between devices, body(): st = lax.all_to_all(scanned, 'ctx', 0, 0)  4.96 us
  transfers between devices with their start and end apart: 8, of which 4 were waited for; matrix products, arithmetic and copies ran while one was open for 0% of the time, Pallas kernels for 23%

profile of v5, /device:TPU:7, one launch (start us, length us, event | category | flops | bytes accessed | tf_op | source)
XLA Modules:
  0.0 81.9 jit_solution(5306378494499014853)
XLA Ops:
  0.6 0.0 slice-start
  0.6 0.0 slice-start.1
  0.7 0.7 slice-done
  1.4 0.0 slice-done.1
  1.4 0.0 copy-start
  1.4 0.0 copy-start.1
  1.4 0.0 copy-start.2
  1.4 0.0 copy-start.3
  1.4 3.6 %collective-permute-start = (bf16[8,1280]{1,0:T(8,128)(2,1)S(1)}, bf16[8,1280]{1,0:T(8,128)(2,1)S(1)}, u32[]{:S(2)}, u32[]{:S(2)}) collective-permute-start(bf16[8,1280]{1,0:T(8,128)(2,1)S(1)} %pad_maximum_fusion), channel_id=1, source_target_pairs={{0,8},{8,16},{16,24},{24,32},{32,40},{40,48},{48,56},{56,64},{64,7... | collective-permute-start | bytes 61448 | tf_op jit(solution)/shard_map/ppermute | solution.py:557
  5.6 0.0 copy-done
  5.6 0.0 copy-done.1
  5.7 0.0 copy-done.2
  5.7 0.0 copy-done.3
  5.7 4.0 %gather.1 = (f32[2,128,1024]{2,1,0:T(8,128)S(1)}, f32[8,1024]{1,0:T(8,128)S(1)}, f32[8,1024]{1,0:T(8,128)S(1)}, f32[8,1280]{1,0:T(8,128)S(1)}, bf16[8,128]{1,0:T(8,128)(2,1)S(1)}) custom-call(s32[1]{0:T(128)S(6)} %copy.13.doc_ref, f32[16]{0:T(128)S(1)} %copy-done.3, bf16[256,1024]{1,0:T(8,128)(2,1)} %x_hbm.3, bf16[256,1024]{1,0:T(8,128)(2,1)} %dy_hbm.3, ...), custom_call_target="tpu_custom_call" | custom-call | tf_op jit(solution)/shard_map/gather/pallas_call | solution.py:543
  9.7 0.0 collective-permute-done.halo_ref
  9.7 0.5 send.1
  10.2 27.0 %all_to_all.10.got_ref = bf16[32,72,128]{2,1,0:T(8,128)(2,1)S(1)} all-to-all(bf16[32,72,128]{2,1,0:T(8,128)(2,1)S(1)} %send.1), channel_id=1, replica_groups=mesh['ctx'=32,'head'=8] {'ctx'}, dimensions={0} | all-to-all | bytes 1179648 | tf_op jit(solution)/shard_map/all_to_all | solution.py:613
  37.2 1.2 %scan.1 = bf16[32,64,128]{2,1,0:T(8,128)(2,1)} custom-call(bf16[32,72,128]{2,1,0:T(8,128)(2,1)S(1)} %all_to_all.10.got_ref), custom_call_target="tpu_custom_call" | custom-call | tf_op jit(solution)/shard_map/scan/pallas_call | solution.py:543
  38.5 6.0 %all-to-all-start.1 = ((bf16[32,64,128]{2,1,0:T(8,128)(2,1)}), bf16[32,64,128]{2,1,0:T(8,128)(2,1)S(1)}, u32[]{:S(2)}, u32[]{:S(2)}) async-start(bf16[32,64,128]{2,1,0:T(8,128)(2,1)} %scan.1), calls=%async_computation.1 | async-start | bytes 1048576 | tf_op jit(solution)/shard_map/all_to_all | solution.py:658
  44.5 0.0 copy-start.4
  44.5 0.6 copy-done.4
  45.1 9.2 %intra.1 = (f32[256,1024]{1,0:T(8,128)}, f32[256,1024]{1,0:T(8,128)}, f32[256,1024]{1,0:T(8,128)S(1)}, bf16[256,1024]{1,0:T(8,128)(2,1)S(1)}, bf16[256,1024]{1,0...) custom-call(s32[1]{0:T(128)S(6)} %copy.13.doc_ref, ...), custom_call_target="tpu_custom_call" | custom-call | tf_op jit(solution)/shard_map/intra/pallas_call | solution.py:543
  54.3 5.0 %all-to-all-done.1.st_ref = bf16[32,64,128]{2,1,0:T(8,128)(2,1)S(1)} async-done(((bf16[32,64,128]{2,1,0:T(8,128)(2,1)}), bf16[32,64,128]{2,1,0:T(8,128)(2,1)S(1)}, u32[]{:S(2)}, u32[]{:S(2)}) %all-to-all-start.1) | async-done | bytes 524320 | tf_op jit(solution)/shard_map/all_to_all | solution.py:658
  59.2 0.5 grad_bc.1
  59.7 3.5 %collective-permute-start.1 = (bf16[128,256]{1,0:T(8,128)(2,1)S(1)}, bf16[128,256]{1,0:T(8,128)(2,1)S(1)}, u32[]{:S(2)}, u32[]{:S(2)}) collective-permute-start(bf16[128,256]{1,0:T(8,128)(2,1)S(1)} %get-tuple-element.63), channel_id=1, source_target_pairs={{0,1},{1,0},{2,3},{3,2},{4,5},{5,4},{6,7},{7,6},{8,9},{9,8},{10,11... | collective-permute-start | bytes 196616 | tf_op jit(solution)/shard_map/ppermute | solution.py:562
  63.3 2.5 %collective-permute-start.2 = (f32[8,1280]{1,0:T(8,128)S(1)}, f32[8,1280]{1,0:T(8,128)S(1)}, u32[]{:S(2)}, u32[]{:S(2)}) collective-permute-start(f32[8,1280]{1,0:T(8,128)S(1)} %get-tuple-element.64), channel_id=1, source_target_pairs={{8,0},{16,8},{24,16},{32,24},{40,32},{48,40},{56,48},{64,56},{72,6... | collective-permute-start | bytes 122888 | tf_op jit(solution)/shard_map/ppermute | solution.py:557
  65.7 1.3 %y_out.1 = (bf16[256,1024]{1,0:T(8,128)(2,1)}, f32[16,256]{1,0:T(8,128)S(1)}) custom-call(bf16[32,64,128]{2,1,0:T(8,128)(2,1)S(1)} %all-to-all-done.1.st_ref, bf16[256,256]{1,0:T(8,128)(2,1)S(1)} %get-tuple-element.53.b_ref.bcc_ref, f32[7,16,256]{2,1,0:T(8,128)S(1)} %get-tuple-element.59.hv_ref, f32[256,1024]{1,0:T(8,128)S(1)} %get-tuple-element.60.yi_ref, ...), custom_call_target="tpu_custom_call" | custom-call | tf_op jit(solution)/shard_map/y_out/pallas_call | solution.py:543
  67.1 1.8 %grad_xc.1 = (f32[256,1024]{1,0:T(8,128)S(1)}, f32[16,256]{1,0:T(8,128)S(1)}, f32[16,128]{1,0:T(8,128)S(1)}) custom-call(f32[256,1024]{1,0:T(8,128)} %get-tuple-element.66.gs_hbm, f32[256,1024]{1,0:T(8,128)} %get-tuple-element.67.ls_hbm, bf16[32,64,128]{2,1,0:T(8,128)(2,1)S(1)} %all-to-all-done.1.st_ref, ...), custom_call_target="tpu_custom_call" | custom-call | tf_op jit(solution)/shard_map/grad_xc/pallas_call | solution.py:543
  68.9 1.2 %collective-permute-done.2.halo_ref = f32[8,1280]{1,0:T(8,128)S(1)} collective-permute-done((f32[8,1280]{1,0:T(8,128)S(1)}, f32[8,1280]{1,0:T(8,128)S(1)}, u32[]{:S(2)}, u32[]{:S(2)}) %collective-permute-start.2) | collective-permute-done | bytes 40992 | tf_op jit(solution)/shard_map/ppermute | solution.py:557
  70.1 0.0 collective-permute-done.1.got_ref
  70.1 1.4 %collective-permute-start.3 = (bf16[136,256]{1,0:T(8,128)(2,1)S(1)}, bf16[136,256]{1,0:T(8,128)(2,1)S(1)}, u32[]{:S(2)}, u32[]{:S(2)}) collective-permute-start(bf16[136,256]{1,0:T(8,128)(2,1)S(1)} %join.1.refs_0_), channel_id=1, source_target_pairs={{0,2},{1,3},{2,4},{3,5},{4,6},{5,7},{6,0},{7,1},{8,10},{9,11},{10,... | collective-permute-start | bytes 208904 | tf_op jit(solution)/shard_map/ppermute | solution.py:567
  71.5 2.6 %collective-permute-start.4 = (bf16[136,256]{1,0:T(8,128)(2,1)S(1)}, bf16[136,256]{1,0:T(8,128)(2,1)S(1)}, u32[]{:S(2)}, u32[]{:S(2)}) collective-permute-start(bf16[136,256]{1,0:T(8,128)(2,1)S(1)} %join.1.refs_0_), channel_id=1, source_target_pairs={{0,4},{1,5},{2,6},{3,7},{4,0},{5,1},{6,2},{7,3},{8,12},{9,13},{10,... | collective-permute-start | bytes 208904 | tf_op jit(solution)/shard_map/ppermute | solution.py:567
  74.1 1.1 %collective-permute-start.5 = (bf16[136,256]{1,0:T(8,128)(2,1)S(1)}, bf16[136,256]{1,0:T(8,128)(2,1)S(1)}, u32[]{:S(2)}, u32[]{:S(2)}) collective-permute-start(bf16[136,256]{1,0:T(8,128)(2,1)S(1)} %join.1.refs_0_), channel_id=1, source_target_pairs={{0,6},{1,7},{2,0},{3,1},{4,2},{5,3},{6,4},{7,5},{8,14},{9,15},{10,... | collective-permute-start | bytes 208904 | tf_op jit(solution)/shard_map/ppermute | solution.py:567
  75.2 1.3 %grad_x.1 = bf16[256,1024]{1,0:T(8,128)(2,1)} custom-call(f32[256,1024]{1,0:T(8,128)S(1)} %get-tuple-element.71.g_ref, f32[8,1280]{1,0:T(8,128)S(1)} %collective-permute-done.2.halo_ref, bf16[4,1024]{1,0:T(4,128)(2,1)S(1)} %copy-done), custom_call_target="tpu_custom_call" | custom-call | tf_op jit(solution)/shard_map/grad_x/pallas_call | solution.py:543
  76.6 0.0 collective-permute-done.3.refs_1_
  76.6 0.1 collective-permute-done.4.refs_2_
  76.7 1.4 %collective-permute-done.5.refs_3_ = bf16[136,256]{1,0:T(8,128)(2,1)S(1)} collective-permute-done((bf16[136,256]{1,0:T(8,128)(2,1)S(1)}, bf16[136,256]{1,0:T(8,128)(2,1)S(1)}, u32[]{:S(2)}, u32[]{:S(2)}) %collective-permute-start.5) | collective-permute-done | bytes 69664 | tf_op jit(solution)/shard_map/ppermute | solution.py:567
  78.2 2.1 %collective-permute-start.6 = (bf16[136,256]{1,0:T(8,128)(2,1)S(1)}, bf16[136,256]{1,0:T(8,128)(2,1)S(1)}, u32[]{:S(2)}, u32[]{:S(2)}) collective-permute-start(bf16[136,256]{1,0:T(8,128)(2,1)S(1)} %sum.1.mine_ref), channel_id=1, source_target_pairs={{0,1},{1,0},{2,3},{3,2},{4,5},{5,4},{6,7},{7,6},{8,9},{9,8},{10,11... | collective-permute-start | bytes 208904 | tf_op jit(solution)/shard_map/ppermute | solution.py:562
  80.3 0.9 %grad_dt.1 = f32[16,256]{1,0:T(8,128)} custom-call(f32[7,16,256]{2,1,0:T(8,128)S(1)} %get-tuple-element.59.hv_ref, f32[16,256]{1,0:T(8,128)S(1)} %get-tuple-element.79.enter_ref, f32[16,256]{1,0:T(8,128)S(1)} %get-tuple-element.80.leave_ref, f32[16,128]{1,0:T(8,128)S(1)} %get-tuple-element.81.overlap_ref), custom_call_target="tpu_custom_call" | custom-call | tf_op jit(solution)/shard_map/grad_dt/pallas_call | solution.py:543
  81.2 0.0 collective-permute-done.6.got_ref
  81.2 0.7 last.1
  (3 shorter events, 0.1 us)
Async XLA Ops:
  0.6 0.7 slice-start
  0.6 0.7 slice-start.1
  1.4 4.3 %copy-start = (bf16[4,1024]{1,0:T(4,128)(2,1)S(1)}, bf16[4,1024]{1,0:T(4,128)(2,1)}, u32[]{:S(2)}) copy-start(bf16[4,1024]{1,0:T(4,128)(2,1)} %wx_ref.7) | copy-start | bytes 24580
  1.4 4.3 %copy-start.1 = (f32[16,256]{1,0:T(8,128)S(1)}, f32[16,256]{1,0:T(8,128)}, u32[]{:S(2)}) copy-start(f32[16,256]{1,0:T(8,128)} %dt_ref.2) | copy-start | bytes 49156
  1.4 4.3 %copy-start.2 = (bf16[4,256]{1,0:T(4,128)(2,1)S(1)}, bf16[4,256]{1,0:T(4,128)(2,1)}, u32[]{:S(2)}) copy-start(bf16[4,256]{1,0:T(4,128)(2,1)} %wbc_ref.9) | copy-start | bytes 6148
  1.4 4.3 %copy-start.3 = (f32[16]{0:T(128)S(1)}, f32[16]{0:T(128)}, u32[]{:S(2)}) copy-start(f32[16]{0:T(128)} %a_log_ref.3) | copy-start | bytes 196
  1.4 8.3 %collective-permute-start = (bf16[8,1280]{1,0:T(8,128)(2,1)S(1)}, bf16[8,1280]{1,0:T(8,128)(2,1)S(1)}, u32[]{:S(2)}, u32[]{:S(2)}) collective-permute-start(bf16[8,1280]{1,0:T(8,128)(2,1)S(1)} %pad_maximum_fusion), channel_id=1, source_target_pairs={{0,8},{8,16},{16,24},{24,32},{32,40},{40,48},{48,56},{56,64},{64,7... | collective-permute-start | bytes 61448 | tf_op jit(solution)/shard_map/ppermute | solution.py:557
  38.5 20.7 %all-to-all-start.1 = ((bf16[32,64,128]{2,1,0:T(8,128)(2,1)}), bf16[32,64,128]{2,1,0:T(8,128)(2,1)S(1)}, u32[]{:S(2)}, u32[]{:S(2)}) async-start(bf16[32,64,128]{2,1,0:T(8,128)(2,1)} %scan.1), calls=%async_computation.1 | async-start | bytes 1048576 | tf_op jit(solution)/shard_map/all_to_all | solution.py:658
  44.5 0.7 copy-start.4
  59.7 10.4 %collective-permute-start.1 = (bf16[128,256]{1,0:T(8,128)(2,1)S(1)}, bf16[128,256]{1,0:T(8,128)(2,1)S(1)}, u32[]{:S(2)}, u32[]{:S(2)}) collective-permute-start(bf16[128,256]{1,0:T(8,128)(2,1)S(1)} %get-tuple-element.63), channel_id=1, source_target_pairs={{0,1},{1,0},{2,3},{3,2},{4,5},{5,4},{6,7},{7,6},{8,9},{9,8},{10,11... | collective-permute-start | bytes 196616 | tf_op jit(solution)/shard_map/ppermute | solution.py:562
  63.3 6.8 %collective-permute-start.2 = (f32[8,1280]{1,0:T(8,128)S(1)}, f32[8,1280]{1,0:T(8,128)S(1)}, u32[]{:S(2)}, u32[]{:S(2)}) collective-permute-start(f32[8,1280]{1,0:T(8,128)S(1)} %get-tuple-element.64), channel_id=1, source_target_pairs={{8,0},{16,8},{24,16},{32,24},{40,32},{48,40},{56,48},{64,56},{72,6... | collective-permute-start | bytes 122888 | tf_op jit(solution)/shard_map/ppermute | solution.py:557
  70.1 6.4 %collective-permute-start.3 = (bf16[136,256]{1,0:T(8,128)(2,1)S(1)}, bf16[136,256]{1,0:T(8,128)(2,1)S(1)}, u32[]{:S(2)}, u32[]{:S(2)}) collective-permute-start(bf16[136,256]{1,0:T(8,128)(2,1)S(1)} %join.1.refs_0_), channel_id=1, source_target_pairs={{0,2},{1,3},{2,4},{3,5},{4,6},{5,7},{6,0},{7,1},{8,10},{9,11},{10,... | collective-permute-start | bytes 208904 | tf_op jit(solution)/shard_map/ppermute | solution.py:567
  71.5 5.2 %collective-permute-start.4 = (bf16[136,256]{1,0:T(8,128)(2,1)S(1)}, bf16[136,256]{1,0:T(8,128)(2,1)S(1)}, u32[]{:S(2)}, u32[]{:S(2)}) collective-permute-start(bf16[136,256]{1,0:T(8,128)(2,1)S(1)} %join.1.refs_0_), channel_id=1, source_target_pairs={{0,4},{1,5},{2,6},{3,7},{4,0},{5,1},{6,2},{7,3},{8,12},{9,13},{10,... | collective-permute-start | bytes 208904 | tf_op jit(solution)/shard_map/ppermute | solution.py:567
  74.1 4.0 %collective-permute-start.5 = (bf16[136,256]{1,0:T(8,128)(2,1)S(1)}, bf16[136,256]{1,0:T(8,128)(2,1)S(1)}, u32[]{:S(2)}, u32[]{:S(2)}) collective-permute-start(bf16[136,256]{1,0:T(8,128)(2,1)S(1)} %join.1.refs_0_), channel_id=1, source_target_pairs={{0,6},{1,7},{2,0},{3,1},{4,2},{5,3},{6,4},{7,5},{8,14},{9,15},{10,... | collective-permute-start | bytes 208904 | tf_op jit(solution)/shard_map/ppermute | solution.py:567
  78.2 3.1 %collective-permute-start.6 = (bf16[136,256]{1,0:T(8,128)(2,1)S(1)}, bf16[136,256]{1,0:T(8,128)(2,1)S(1)}, u32[]{:S(2)}, u32[]{:S(2)}) collective-permute-start(bf16[136,256]{1,0:T(8,128)(2,1)S(1)} %sum.1.mine_ref), channel_id=1, source_target_pairs={{0,1},{1,0},{2,3},{3,2},{4,5},{5,4},{6,7},{7,6},{8,9},{9,8},{10,11... | collective-permute-start | bytes 208904 | tf_op jit(solution)/shard_map/ppermute | solution.py:562

commit v6 on v5

--- a/solution.py
+++ b/solution.py
@@ -389,8 +389,8 @@
     give_ref[...] = total[pl.ds(pl.multiple_of((1 - core) * half, half), half), :].astype(BF16)
     d_leaving = dot(b_ref[0 : 2 * RIM, 0:LANES], dstate, ((1,), (0,)))[0:RIM]
     channels = rim_ref.shape[2]
-    halo_ref[:, 0:channels] = rim_ref[0] + rim_ref[1] * d_leaving
-    halo_ref[:, channels:] = ext[0:RIM, :]
+    halo_ref[:, 0:channels] = (rim_ref[0] + rim_ref[1] * d_leaving).astype(BF16)
+    halo_ref[:, channels:] = ext[0:RIM, :].astype(BF16)
 
 
 def join_kernel(keep_ref, got_ref, halo_ref, wbc_ref, out_ref, ext):
@@ -399,7 +399,7 @@
     wide = keep_ref.shape[1]
     out_ref[0:half, :] = (keep_ref[...] + got_ref[...].astype(F32)).astype(BF16)
     ext[0:RIM, :] = jnp.zeros((RIM, wide), F32)
-    ext[RIM:, :] = halo_ref[:, halo_ref.shape[1] - wide :]
+    ext[RIM:, :] = halo_ref[:, halo_ref.shape[1] - wide :].astype(F32)
     w = wbc_ref[...].astype(F32)
     rim = jnp.zeros((RIM, wide), F32)
     for tap in range(taps - 1):
@@ -492,7 +492,7 @@
     group = slabs // sems.shape[0]
     low = rows - RIM
     ext[0:RIM, :] = g_ref[low:, :]
-    ext[RIM:, :] = halo_ref[:, 0:channels]
+    ext[RIM:, :] = halo_ref[:, 0:channels].astype(F32)
     sent = []
     for slab in range(slabs):
         lanes = lanes_of(slab)
@@ -667,7 +667,7 @@
         [
             ((half, wide), F32),
             ((half, wide), BF16),
-            ((RIM, channels + wide), F32),
+            ((RIM, channels + wide), BF16),
         ],
         [pltpu.VMEM((rows + RIM, wide), F32), pltpu.VMEM((rows, wide), F32)],
     )

time: 82.4 us -> 82.2 us (level)
  no operation moved by 1% of the time
where the time goes in v6:
time: 82.2 us; the launch traced here: 81.7 us
  blocking collectives  27 us (33%)
  starting transfers between devices  22.8 us (28%)
  Pallas kernels  21.5 us (26%)
  waiting for transfers between devices  7.52 us (9%)
  between operations  1.48 us (2%)
  local copies, waits for them, and re-layouts  1.37 us (2%)
    all_to_all x1, blocking collectives, body(): got = lax.all_to_all(send, 'ctx', 0, 0)  27 us
    pallas_call x12, Pallas kernels, call(): pl.pallas_call(kernel, name=name, out_shape=out if many else out[0], in_s...  21.5 us
    ppermute x2, starting transfers between devices, shift_ctx(): return lax.ppermute(values, 'ctx', pairs)  6.06 us
    all_to_all x1, starting transfers between devices, body(): st = lax.all_to_all(scanned, 'ctx', 0, 0)  5.95 us
    ppermute x2, starting transfers between devices, swap_core(): return lax.ppermute(values, 'head', [(i, i ^ 1) for i in range(size)])  5.69 us
    ppermute x3, starting transfers between devices, around(): lax.ppermute(values, 'head', [(i, (i + 2 * by) % size) for i in range(siz...  5.06 us
    all_to_all x1, waiting for transfers between devices, body(): st = lax.all_to_all(scanned, 'ctx', 0, 0)  4.96 us
  transfers between devices with their start and end apart: 8, of which 4 were waited for; matrix products, arithmetic and copies ran while one was open for 0% of the time, Pallas kernels for 23%

profile of v6, /device:TPU:7, one launch (start us, length us, event | category | flops | bytes accessed | tf_op | source)
XLA Modules:
  0.0 81.7 jit_solution(17865734638879710870)
XLA Ops:
  0.6 0.0 slice-start
  0.6 0.0 slice-start.1
  0.7 0.7 slice-done
  1.4 0.0 slice-done.1
  1.4 0.0 copy-start
  1.4 0.0 copy-start.1
  1.4 0.0 copy-start.2
  1.4 0.0 copy-start.3
  1.4 3.6 %collective-permute-start = (bf16[8,1280]{1,0:T(8,128)(2,1)S(1)}, bf16[8,1280]{1,0:T(8,128)(2,1)S(1)}, u32[]{:S(2)}, u32[]{:S(2)}) collective-permute-start(bf16[8,1280]{1,0:T(8,128)(2,1)S(1)} %pad_maximum_fusion), channel_id=1, source_target_pairs={{0,8},{8,16},{16,24},{24,32},{32,40},{40,48},{48,56},{56,64},{64,7... | collective-permute-start | bytes 61448 | tf_op jit(solution)/shard_map/ppermute | solution.py:557
  5.6 0.0 copy-done
  5.6 0.0 copy-done.1
  5.7 0.0 copy-done.2
  5.7 0.0 copy-done.3
  5.7 4.0 %gather.1 = (f32[2,128,1024]{2,1,0:T(8,128)S(1)}, f32[8,1024]{1,0:T(8,128)S(1)}, f32[8,1024]{1,0:T(8,128)S(1)}, f32[8,1280]{1,0:T(8,128)S(1)}, bf16[8,128]{1,0:T(8,128)(2,1)S(1)}) custom-call(s32[1]{0:T(128)S(6)} %copy.13.doc_ref, f32[16]{0:T(128)S(1)} %copy-done.3, bf16[256,1024]{1,0:T(8,128)(2,1)} %x_hbm.3, bf16[256,1024]{1,0:T(8,128)(2,1)} %dy_hbm.3, ...), custom_call_target="tpu_custom_call" | custom-call | tf_op jit(solution)/shard_map/gather/pallas_call | solution.py:543
  9.7 0.0 collective-permute-done.halo_ref
  9.7 0.5 send.1
  10.2 27.0 %all_to_all.10.got_ref = bf16[32,72,128]{2,1,0:T(8,128)(2,1)S(1)} all-to-all(bf16[32,72,128]{2,1,0:T(8,128)(2,1)S(1)} %send.1), channel_id=1, replica_groups=mesh['ctx'=32,'head'=8] {'ctx'}, dimensions={0} | all-to-all | bytes 1179648 | tf_op jit(solution)/shard_map/all_to_all | solution.py:613
  37.2 1.2 %scan.1 = bf16[32,64,128]{2,1,0:T(8,128)(2,1)} custom-call(bf16[32,72,128]{2,1,0:T(8,128)(2,1)S(1)} %all_to_all.10.got_ref), custom_call_target="tpu_custom_call" | custom-call | tf_op jit(solution)/shard_map/scan/pallas_call | solution.py:543
  38.5 6.0 %all-to-all-start.1 = ((bf16[32,64,128]{2,1,0:T(8,128)(2,1)}), bf16[32,64,128]{2,1,0:T(8,128)(2,1)S(1)}, u32[]{:S(2)}, u32[]{:S(2)}) async-start(bf16[32,64,128]{2,1,0:T(8,128)(2,1)} %scan.1), calls=%async_computation.1 | async-start | bytes 1048576 | tf_op jit(solution)/shard_map/all_to_all | solution.py:658
  44.5 0.0 copy-start.4
  44.5 0.6 copy-done.4
  45.1 9.2 %intra.1 = (f32[256,1024]{1,0:T(8,128)}, f32[256,1024]{1,0:T(8,128)}, f32[256,1024]{1,0:T(8,128)S(1)}, bf16[256,1024]{1,0:T(8,128)(2,1)S(1)}, bf16[256,1024]{1,0...) custom-call(s32[1]{0:T(128)S(6)} %copy.13.doc_ref, ...), custom_call_target="tpu_custom_call" | custom-call | tf_op jit(solution)/shard_map/intra/pallas_call | solution.py:543
  54.3 5.0 %all-to-all-done.1.st_ref = bf16[32,64,128]{2,1,0:T(8,128)(2,1)S(1)} async-done(((bf16[32,64,128]{2,1,0:T(8,128)(2,1)}), bf16[32,64,128]{2,1,0:T(8,128)(2,1)S(1)}, u32[]{:S(2)}, u32[]{:S(2)}) %all-to-all-start.1) | async-done | bytes 524320 | tf_op jit(solution)/shard_map/all_to_all | solution.py:658
  59.2 0.5 grad_bc.1
  59.7 3.5 %collective-permute-start.1 = (bf16[128,256]{1,0:T(8,128)(2,1)S(1)}, bf16[128,256]{1,0:T(8,128)(2,1)S(1)}, u32[]{:S(2)}, u32[]{:S(2)}) collective-permute-start(bf16[128,256]{1,0:T(8,128)(2,1)S(1)} %get-tuple-element.63), channel_id=1, source_target_pairs={{0,1},{1,0},{2,3},{3,2},{4,5},{5,4},{6,7},{7,6},{8,9},{9,8},{10,11... | collective-permute-start | bytes 196616 | tf_op jit(solution)/shard_map/ppermute | solution.py:562
  63.3 2.5 %collective-permute-start.2 = (bf16[8,1280]{1,0:T(8,128)(2,1)S(1)}, bf16[8,1280]{1,0:T(8,128)(2,1)S(1)}, u32[]{:S(2)}, u32[]{:S(2)}) collective-permute-start(bf16[8,1280]{1,0:T(8,128)(2,1)S(1)} %get-tuple-element.64), channel_id=1, source_target_pairs={{8,0},{16,8},{24,16},{32,24},{40,32},{48,40},{56,48},{64,56},{72,6... | collective-permute-start | bytes 61448 | tf_op jit(solution)/shard_map/ppermute | solution.py:557
  65.7 1.3 %y_out.1 = (bf16[256,1024]{1,0:T(8,128)(2,1)}, f32[16,256]{1,0:T(8,128)S(1)}) custom-call(bf16[32,64,128]{2,1,0:T(8,128)(2,1)S(1)} %all-to-all-done.1.st_ref, bf16[256,256]{1,0:T(8,128)(2,1)S(1)} %get-tuple-element.53.b_ref.bcc_ref, f32[7,16,256]{2,1,0:T(8,128)S(1)} %get-tuple-element.59.hv_ref, f32[256,1024]{1,0:T(8,128)S(1)} %get-tuple-element.60.yi_ref, ...), custom_call_target="tpu_custom_call" | custom-call | tf_op jit(solution)/shard_map/y_out/pallas_call | solution.py:543
  67.1 1.8 %grad_xc.1 = (f32[256,1024]{1,0:T(8,128)S(1)}, f32[16,256]{1,0:T(8,128)S(1)}, f32[16,128]{1,0:T(8,128)S(1)}) custom-call(f32[256,1024]{1,0:T(8,128)} %get-tuple-element.66.gs_hbm, f32[256,1024]{1,0:T(8,128)} %get-tuple-element.67.ls_hbm, bf16[32,64,128]{2,1,0:T(8,128)(2,1)S(1)} %all-to-all-done.1.st_ref, ...), custom_call_target="tpu_custom_call" | custom-call | tf_op jit(solution)/shard_map/grad_xc/pallas_call | solution.py:543
  68.9 1.0 %collective-permute-done.2.halo_ref = bf16[8,1280]{1,0:T(8,128)(2,1)S(1)} collective-permute-done((bf16[8,1280]{1,0:T(8,128)(2,1)S(1)}, bf16[8,1280]{1,0:T(8,128)(2,1)S(1)}, u32[]{:S(2)}, u32[]{:S(2)}) %collective-permute-start.2) | collective-permute-done | bytes 20512 | tf_op jit(solution)/shard_map/ppermute | solution.py:557
  69.9 0.0 collective-permute-done.1.got_ref
  69.9 1.4 %collective-permute-start.3 = (bf16[136,256]{1,0:T(8,128)(2,1)S(1)}, bf16[136,256]{1,0:T(8,128)(2,1)S(1)}, u32[]{:S(2)}, u32[]{:S(2)}) collective-permute-start(bf16[136,256]{1,0:T(8,128)(2,1)S(1)} %join.1.refs_0_), channel_id=1, source_target_pairs={{0,2},{1,3},{2,4},{3,5},{4,6},{5,7},{6,0},{7,1},{8,10},{9,11},{10,... | collective-permute-start | bytes 208904 | tf_op jit(solution)/shard_map/ppermute | solution.py:567
  71.3 2.6 %collective-permute-start.4 = (bf16[136,256]{1,0:T(8,128)(2,1)S(1)}, bf16[136,256]{1,0:T(8,128)(2,1)S(1)}, u32[]{:S(2)}, u32[]{:S(2)}) collective-permute-start(bf16[136,256]{1,0:T(8,128)(2,1)S(1)} %join.1.refs_0_), channel_id=1, source_target_pairs={{0,4},{1,5},{2,6},{3,7},{4,0},{5,1},{6,2},{7,3},{8,12},{9,13},{10,... | collective-permute-start | bytes 208904 | tf_op jit(solution)/shard_map/ppermute | solution.py:567
  73.9 1.1 %collective-permute-start.5 = (bf16[136,256]{1,0:T(8,128)(2,1)S(1)}, bf16[136,256]{1,0:T(8,128)(2,1)S(1)}, u32[]{:S(2)}, u32[]{:S(2)}) collective-permute-start(bf16[136,256]{1,0:T(8,128)(2,1)S(1)} %join.1.refs_0_), channel_id=1, source_target_pairs={{0,6},{1,7},{2,0},{3,1},{4,2},{5,3},{6,4},{7,5},{8,14},{9,15},{10,... | collective-permute-start | bytes 208904 | tf_op jit(solution)/shard_map/ppermute | solution.py:567
  75.0 1.4 %grad_x.1 = bf16[256,1024]{1,0:T(8,128)(2,1)} custom-call(f32[256,1024]{1,0:T(8,128)S(1)} %get-tuple-element.71.g_ref, bf16[8,1280]{1,0:T(8,128)(2,1)S(1)} %collective-permute-done.2.halo_ref, bf16[4,1024]{1,0:T(4,128)(2,1)S(1)} %copy-done), custom_call_target="tpu_custom_call" | custom-call | tf_op jit(solution)/shard_map/grad_x/pallas_call | solution.py:543
  76.4 0.0 collective-permute-done.3.refs_1_
  76.4 0.1 collective-permute-done.4.refs_2_
  76.5 1.4 %collective-permute-done.5.refs_3_ = bf16[136,256]{1,0:T(8,128)(2,1)S(1)} collective-permute-done((bf16[136,256]{1,0:T(8,128)(2,1)S(1)}, bf16[136,256]{1,0:T(8,128)(2,1)S(1)}, u32[]{:S(2)}, u32[]{:S(2)}) %collective-permute-start.5) | collective-permute-done | bytes 69664 | tf_op jit(solution)/shard_map/ppermute | solution.py:567
  78.0 2.1 %collective-permute-start.6 = (bf16[136,256]{1,0:T(8,128)(2,1)S(1)}, bf16[136,256]{1,0:T(8,128)(2,1)S(1)}, u32[]{:S(2)}, u32[]{:S(2)}) collective-permute-start(bf16[136,256]{1,0:T(8,128)(2,1)S(1)} %sum.1.mine_ref), channel_id=1, source_target_pairs={{0,1},{1,0},{2,3},{3,2},{4,5},{5,4},{6,7},{7,6},{8,9},{9,8},{10,11... | collective-permute-start | bytes 208904 | tf_op jit(solution)/shard_map/ppermute | solution.py:562
  80.1 0.9 %grad_dt.1 = f32[16,256]{1,0:T(8,128)} custom-call(f32[7,16,256]{2,1,0:T(8,128)S(1)} %get-tuple-element.59.hv_ref, f32[16,256]{1,0:T(8,128)S(1)} %get-tuple-element.79.enter_ref, f32[16,256]{1,0:T(8,128)S(1)} %get-tuple-element.80.leave_ref, f32[16,128]{1,0:T(8,128)S(1)} %get-tuple-element.81.overlap_ref), custom_call_target="tpu_custom_call" | custom-call | tf_op jit(solution)/shard_map/grad_dt/pallas_call | solution.py:543
  81.0 0.0 collective-permute-done.6.got_ref
  81.0 0.7 last.1
  (3 shorter events, 0.1 us)
Async XLA Ops:
  0.6 0.7 slice-start
  0.6 0.7 slice-start.1
  1.4 4.3 %copy-start = (bf16[4,1024]{1,0:T(4,128)(2,1)S(1)}, bf16[4,1024]{1,0:T(4,128)(2,1)}, u32[]{:S(2)}) copy-start(bf16[4,1024]{1,0:T(4,128)(2,1)} %wx_ref.7) | copy-start | bytes 24580
  1.4 4.3 %copy-start.1 = (f32[16,256]{1,0:T(8,128)S(1)}, f32[16,256]{1,0:T(8,128)}, u32[]{:S(2)}) copy-start(f32[16,256]{1,0:T(8,128)} %dt_ref.2) | copy-start | bytes 49156
  1.4 4.3 %copy-start.2 = (bf16[4,256]{1,0:T(4,128)(2,1)S(1)}, bf16[4,256]{1,0:T(4,128)(2,1)}, u32[]{:S(2)}) copy-start(bf16[4,256]{1,0:T(4,128)(2,1)} %wbc_ref.9) | copy-start | bytes 6148
  1.4 4.3 %copy-start.3 = (f32[16]{0:T(128)S(1)}, f32[16]{0:T(128)}, u32[]{:S(2)}) copy-start(f32[16]{0:T(128)} %a_log_ref.3) | copy-start | bytes 196
  1.4 8.3 %collective-permute-start = (bf16[8,1280]{1,0:T(8,128)(2,1)S(1)}, bf16[8,1280]{1,0:T(8,128)(2,1)S(1)}, u32[]{:S(2)}, u32[]{:S(2)}) collective-permute-start(bf16[8,1280]{1,0:T(8,128)(2,1)S(1)} %pad_maximum_fusion), channel_id=1, source_target_pairs={{0,8},{8,16},{16,24},{24,32},{32,40},{40,48},{48,56},{56,64},{64,7... | collective-permute-start | bytes 61448 | tf_op jit(solution)/shard_map/ppermute | solution.py:557
  38.5 20.7 %all-to-all-start.1 = ((bf16[32,64,128]{2,1,0:T(8,128)(2,1)}), bf16[32,64,128]{2,1,0:T(8,128)(2,1)S(1)}, u32[]{:S(2)}, u32[]{:S(2)}) async-start(bf16[32,64,128]{2,1,0:T(8,128)(2,1)} %scan.1), calls=%async_computation.1 | async-start | bytes 1048576 | tf_op jit(solution)/shard_map/all_to_all | solution.py:658
  44.5 0.7 copy-start.4
  59.7 10.2 %collective-permute-start.1 = (bf16[128,256]{1,0:T(8,128)(2,1)S(1)}, bf16[128,256]{1,0:T(8,128)(2,1)S(1)}, u32[]{:S(2)}, u32[]{:S(2)}) collective-permute-start(bf16[128,256]{1,0:T(8,128)(2,1)S(1)} %get-tuple-element.63), channel_id=1, source_target_pairs={{0,1},{1,0},{2,3},{3,2},{4,5},{5,4},{6,7},{7,6},{8,9},{9,8},{10,11... | collective-permute-start | bytes 196616 | tf_op jit(solution)/shard_map/ppermute | solution.py:562
  63.3 6.6 %collective-permute-start.2 = (bf16[8,1280]{1,0:T(8,128)(2,1)S(1)}, bf16[8,1280]{1,0:T(8,128)(2,1)S(1)}, u32[]{:S(2)}, u32[]{:S(2)}) collective-permute-start(bf16[8,1280]{1,0:T(8,128)(2,1)S(1)} %get-tuple-element.64), channel_id=1, source_target_pairs={{8,0},{16,8},{24,16},{32,24},{40,32},{48,40},{56,48},{64,56},{72,6... | collective-permute-start | bytes 61448 | tf_op jit(solution)/shard_map/ppermute | solution.py:557
  69.9 6.4 %collective-permute-start.3 = (bf16[136,256]{1,0:T(8,128)(2,1)S(1)}, bf16[136,256]{1,0:T(8,128)(2,1)S(1)}, u32[]{:S(2)}, u32[]{:S(2)}) collective-permute-start(bf16[136,256]{1,0:T(8,128)(2,1)S(1)} %join.1.refs_0_), channel_id=1, source_target_pairs={{0,2},{1,3},{2,4},{3,5},{4,6},{5,7},{6,0},{7,1},{8,10},{9,11},{10,... | collective-permute-start | bytes 208904 | tf_op jit(solution)/shard_map/ppermute | solution.py:567
  71.3 5.2 %collective-permute-start.4 = (bf16[136,256]{1,0:T(8,128)(2,1)S(1)}, bf16[136,256]{1,0:T(8,128)(2,1)S(1)}, u32[]{:S(2)}, u32[]{:S(2)}) collective-permute-start(bf16[136,256]{1,0:T(8,128)(2,1)S(1)} %join.1.refs_0_), channel_id=1, source_target_pairs={{0,4},{1,5},{2,6},{3,7},{4,0},{5,1},{6,2},{7,3},{8,12},{9,13},{10,... | collective-permute-start | bytes 208904 | tf_op jit(solution)/shard_map/ppermute | solution.py:567
  73.9 4.0 %collective-permute-start.5 = (bf16[136,256]{1,0:T(8,128)(2,1)S(1)}, bf16[136,256]{1,0:T(8,128)(2,1)S(1)}, u32[]{:S(2)}, u32[]{:S(2)}) collective-permute-start(bf16[136,256]{1,0:T(8,128)(2,1)S(1)} %join.1.refs_0_), channel_id=1, source_target_pairs={{0,6},{1,7},{2,0},{3,1},{4,2},{5,3},{6,4},{7,5},{8,14},{9,15},{10,... | collective-permute-start | bytes 208904 | tf_op jit(solution)/shard_map/ppermute | solution.py:567
  78.0 3.1 %collective-permute-start.6 = (bf16[136,256]{1,0:T(8,128)(2,1)S(1)}, bf16[136,256]{1,0:T(8,128)(2,1)S(1)}, u32[]{:S(2)}, u32[]{:S(2)}) collective-permute-start(bf16[136,256]{1,0:T(8,128)(2,1)S(1)} %sum.1.mine_ref), channel_id=1, source_target_pairs={{0,1},{1,0},{2,3},{3,2},{4,5},{5,4},{6,7},{7,6},{8,9},{9,8},{10,11... | collective-permute-start | bytes 208904 | tf_op jit(solution)/shard_map/ppermute | solution.py:562

commit v7 on v6

--- a/solution.py
+++ b/solution.py
@@ -623,7 +623,7 @@
             pltpu.VMEM(*states),
             pltpu.VMEM((count * RIM, LANES), F32),
             pltpu.VMEM((count * RIM, channels // 2), F32),
-            sems((4,)),
+            sems((8,)),
         ],
     )
     scanned, dt_later = lax.optimization_barrier((scanned, dt_raw))
@@ -682,7 +682,7 @@
         [st, bcc, hv, yi, edy],
         [wide_bf],
         [((heads, rows), F32)],
-        [pltpu.VMEM(*wide_bf), pltpu.VMEM(*wide_f), two],
+        [pltpu.VMEM(*wide_bf), pltpu.VMEM(*wide_f), sems((4,))],
     )
     grad_xc, leave_term, overlap = call(
         functools.partial(xc_kernel, head_dim),

time: 82.2 us -> 82.1 us (level)
  no operation moved by 1% of the time
where the time goes in v7:
time: 82.1 us; the launch traced here: 81.7 us
  blocking collectives  27 us (33%)
  starting transfers between devices  22.8 us (28%)
  Pallas kernels  21.5 us (26%)
  waiting for transfers between devices  7.55 us (9%)
  between operations  1.48 us (2%)
  local copies, waits for them, and re-layouts  1.37 us (2%)
    all_to_all x1, blocking collectives, body(): got = lax.all_to_all(send, 'ctx', 0, 0)  27 us
    pallas_call x12, Pallas kernels, call(): pl.pallas_call(kernel, name=name, out_shape=out if many else out[0], in_s...  21.5 us
    ppermute x2, starting transfers between devices, shift_ctx(): return lax.ppermute(values, 'ctx', pairs)  6.06 us
    all_to_all x1, starting transfers between devices, body(): st = lax.all_to_all(scanned, 'ctx', 0, 0)  5.95 us
    ppermute x2, starting transfers between devices, swap_core(): return lax.ppermute(values, 'head', [(i, i ^ 1) for i in range(size)])  5.69 us
    ppermute x3, starting transfers between devices, around(): lax.ppermute(values, 'head', [(i, (i + 2 * by) % size) for i in range(siz...  5.06 us
    all_to_all x1, waiting for transfers between devices, body(): st = lax.all_to_all(scanned, 'ctx', 0, 0)  4.96 us
  transfers between devices with their start and end apart: 8, of which 4 were waited for; matrix products, arithmetic and copies ran while one was open for 0% of the time, Pallas kernels for 23%

profile of v7, /device:TPU:7, one launch (start us, length us, event | category | flops | bytes accessed | tf_op | source)
XLA Modules:
  0.0 81.7 jit_solution(3361347411736311019)
XLA Ops:
  0.6 0.0 slice-start
  0.6 0.0 slice-start.1
  0.7 0.7 slice-done
  1.4 0.0 slice-done.1
  1.4 0.0 copy-start
  1.4 0.0 copy-start.1
  1.4 0.0 copy-start.2
  1.4 0.0 copy-start.3
  1.4 3.6 %collective-permute-start = (bf16[8,1280]{1,0:T(8,128)(2,1)S(1)}, bf16[8,1280]{1,0:T(8,128)(2,1)S(1)}, u32[]{:S(2)}, u32[]{:S(2)}) collective-permute-start(bf16[8,1280]{1,0:T(8,128)(2,1)S(1)} %pad_maximum_fusion), channel_id=1, source_target_pairs={{0,8},{8,16},{16,24},{24,32},{32,40},{40,48},{48,56},{56,64},{64,7... | collective-permute-start | bytes 61448 | tf_op jit(solution)/shard_map/ppermute | solution.py:557
  5.6 0.0 copy-done
  5.6 0.0 copy-done.1
  5.7 0.0 copy-done.2
  5.7 0.0 copy-done.3
  5.7 4.0 %gather.1 = (f32[2,128,1024]{2,1,0:T(8,128)S(1)}, f32[8,1024]{1,0:T(8,128)S(1)}, f32[8,1024]{1,0:T(8,128)S(1)}, f32[8,1280]{1,0:T(8,128)S(1)}, bf16[8,128]{1,0:T(8,128)(2,1)S(1)}) custom-call(s32[1]{0:T(128)S(6)} %copy.13.doc_ref, f32[16]{0:T(128)S(1)} %copy-done.3, bf16[256,1024]{1,0:T(8,128)(2,1)} %x_hbm.3, bf16[256,1024]{1,0:T(8,128)(2,1)} %dy_hbm.3, ...), custom_call_target="tpu_custom_call" | custom-call | tf_op jit(solution)/shard_map/gather/pallas_call | solution.py:543
  9.7 0.0 collective-permute-done.halo_ref
  9.7 0.5 send.1
  10.2 27.0 %all_to_all.10.got_ref = bf16[32,72,128]{2,1,0:T(8,128)(2,1)S(1)} all-to-all(bf16[32,72,128]{2,1,0:T(8,128)(2,1)S(1)} %send.1), channel_id=1, replica_groups=mesh['ctx'=32,'head'=8] {'ctx'}, dimensions={0} | all-to-all | bytes 1179648 | tf_op jit(solution)/shard_map/all_to_all | solution.py:613
  37.2 1.2 %scan.1 = bf16[32,64,128]{2,1,0:T(8,128)(2,1)} custom-call(bf16[32,72,128]{2,1,0:T(8,128)(2,1)S(1)} %all_to_all.10.got_ref), custom_call_target="tpu_custom_call" | custom-call | tf_op jit(solution)/shard_map/scan/pallas_call | solution.py:543
  38.5 5.9 %all-to-all-start.1 = ((bf16[32,64,128]{2,1,0:T(8,128)(2,1)}), bf16[32,64,128]{2,1,0:T(8,128)(2,1)S(1)}, u32[]{:S(2)}, u32[]{:S(2)}) async-start(bf16[32,64,128]{2,1,0:T(8,128)(2,1)} %scan.1), calls=%async_computation.1 | async-start | bytes 1048576 | tf_op jit(solution)/shard_map/all_to_all | solution.py:658
  44.4 0.0 copy-start.4
  44.4 0.6 copy-done.4
  45.1 9.2 %intra.1 = (f32[256,1024]{1,0:T(8,128)}, f32[256,1024]{1,0:T(8,128)}, f32[256,1024]{1,0:T(8,128)S(1)}, bf16[256,1024]{1,0:T(8,128)(2,1)S(1)}, bf16[256,1024]{1,0...) custom-call(s32[1]{0:T(128)S(6)} %copy.13.doc_ref, ...), custom_call_target="tpu_custom_call" | custom-call | tf_op jit(solution)/shard_map/intra/pallas_call | solution.py:543
  54.2 5.0 %all-to-all-done.1.st_ref = bf16[32,64,128]{2,1,0:T(8,128)(2,1)S(1)} async-done(((bf16[32,64,128]{2,1,0:T(8,128)(2,1)}), bf16[32,64,128]{2,1,0:T(8,128)(2,1)S(1)}, u32[]{:S(2)}, u32[]{:S(2)}) %all-to-all-start.1) | async-done | bytes 524320 | tf_op jit(solution)/shard_map/all_to_all | solution.py:658
  59.2 0.5 grad_bc.1
  59.7 3.5 %collective-permute-start.1 = (bf16[128,256]{1,0:T(8,128)(2,1)S(1)}, bf16[128,256]{1,0:T(8,128)(2,1)S(1)}, u32[]{:S(2)}, u32[]{:S(2)}) collective-permute-start(bf16[128,256]{1,0:T(8,128)(2,1)S(1)} %get-tuple-element.63), channel_id=1, source_target_pairs={{0,1},{1,0},{2,3},{3,2},{4,5},{5,4},{6,7},{7,6},{8,9},{9,8},{10,11... | collective-permute-start | bytes 196616 | tf_op jit(solution)/shard_map/ppermute | solution.py:562
  63.2 2.5 %collective-permute-start.2 = (bf16[8,1280]{1,0:T(8,128)(2,1)S(1)}, bf16[8,1280]{1,0:T(8,128)(2,1)S(1)}, u32[]{:S(2)}, u32[]{:S(2)}) collective-permute-start(bf16[8,1280]{1,0:T(8,128)(2,1)S(1)} %get-tuple-element.64), channel_id=1, source_target_pairs={{8,0},{16,8},{24,16},{32,24},{40,32},{48,40},{56,48},{64,56},{72,6... | collective-permute-start | bytes 61448 | tf_op jit(solution)/shard_map/ppermute | solution.py:557
  65.7 1.3 %y_out.1 = (bf16[256,1024]{1,0:T(8,128)(2,1)}, f32[16,256]{1,0:T(8,128)S(1)}) custom-call(bf16[32,64,128]{2,1,0:T(8,128)(2,1)S(1)} %all-to-all-done.1.st_ref, bf16[256,256]{1,0:T(8,128)(2,1)S(1)} %get-tuple-element.53.b_ref.bcc_ref, f32[7,16,256]{2,1,0:T(8,128)S(1)} %get-tuple-element.59.hv_ref, f32[256,1024]{1,0:T(8,128)S(1)} %get-tuple-element.60.yi_ref, ...), custom_call_target="tpu_custom_call" | custom-call | tf_op jit(solution)/shard_map/y_out/pallas_call | solution.py:543
  67.0 1.8 %grad_xc.1 = (f32[256,1024]{1,0:T(8,128)S(1)}, f32[16,256]{1,0:T(8,128)S(1)}, f32[16,128]{1,0:T(8,128)S(1)}) custom-call(f32[256,1024]{1,0:T(8,128)} %get-tuple-element.66.gs_hbm, f32[256,1024]{1,0:T(8,128)} %get-tuple-element.67.ls_hbm, bf16[32,64,128]{2,1,0:T(8,128)(2,1)S(1)} %all-to-all-done.1.st_ref, ...), custom_call_target="tpu_custom_call" | custom-call | tf_op jit(solution)/shard_map/grad_xc/pallas_call | solution.py:543
  68.8 1.0 %collective-permute-done.2.halo_ref = bf16[8,1280]{1,0:T(8,128)(2,1)S(1)} collective-permute-done((bf16[8,1280]{1,0:T(8,128)(2,1)S(1)}, bf16[8,1280]{1,0:T(8,128)(2,1)S(1)}, u32[]{:S(2)}, u32[]{:S(2)}) %collective-permute-start.2) | collective-permute-done | bytes 20512 | tf_op jit(solution)/shard_map/ppermute | solution.py:557
  69.9 0.0 collective-permute-done.1.got_ref
  69.9 1.4 %collective-permute-start.3 = (bf16[136,256]{1,0:T(8,128)(2,1)S(1)}, bf16[136,256]{1,0:T(8,128)(2,1)S(1)}, u32[]{:S(2)}, u32[]{:S(2)}) collective-permute-start(bf16[136,256]{1,0:T(8,128)(2,1)S(1)} %join.1.refs_0_), channel_id=1, source_target_pairs={{0,2},{1,3},{2,4},{3,5},{4,6},{5,7},{6,0},{7,1},{8,10},{9,11},{10,... | collective-permute-start | bytes 208904 | tf_op jit(solution)/shard_map/ppermute | solution.py:567
  71.3 2.6 %collective-permute-start.4 = (bf16[136,256]{1,0:T(8,128)(2,1)S(1)}, bf16[136,256]{1,0:T(8,128)(2,1)S(1)}, u32[]{:S(2)}, u32[]{:S(2)}) collective-permute-start(bf16[136,256]{1,0:T(8,128)(2,1)S(1)} %join.1.refs_0_), channel_id=1, source_target_pairs={{0,4},{1,5},{2,6},{3,7},{4,0},{5,1},{6,2},{7,3},{8,12},{9,13},{10,... | collective-permute-start | bytes 208904 | tf_op jit(solution)/shard_map/ppermute | solution.py:567
  73.9 1.1 %collective-permute-start.5 = (bf16[136,256]{1,0:T(8,128)(2,1)S(1)}, bf16[136,256]{1,0:T(8,128)(2,1)S(1)}, u32[]{:S(2)}, u32[]{:S(2)}) collective-permute-start(bf16[136,256]{1,0:T(8,128)(2,1)S(1)} %join.1.refs_0_), channel_id=1, source_target_pairs={{0,6},{1,7},{2,0},{3,1},{4,2},{5,3},{6,4},{7,5},{8,14},{9,15},{10,... | collective-permute-start | bytes 208904 | tf_op jit(solution)/shard_map/ppermute | solution.py:567
  75.0 1.4 %grad_x.1 = bf16[256,1024]{1,0:T(8,128)(2,1)} custom-call(f32[256,1024]{1,0:T(8,128)S(1)} %get-tuple-element.71.g_ref, bf16[8,1280]{1,0:T(8,128)(2,1)S(1)} %collective-permute-done.2.halo_ref, bf16[4,1024]{1,0:T(4,128)(2,1)S(1)} %copy-done), custom_call_target="tpu_custom_call" | custom-call | tf_op jit(solution)/shard_map/grad_x/pallas_call | solution.py:543
  76.3 0.0 collective-permute-done.3.refs_1_
  76.3 0.1 collective-permute-done.4.refs_2_
  76.4 1.4 %collective-permute-done.5.refs_3_ = bf16[136,256]{1,0:T(8,128)(2,1)S(1)} collective-permute-done((bf16[136,256]{1,0:T(8,128)(2,1)S(1)}, bf16[136,256]{1,0:T(8,128)(2,1)S(1)}, u32[]{:S(2)}, u32[]{:S(2)}) %collective-permute-start.5) | collective-permute-done | bytes 69664 | tf_op jit(solution)/shard_map/ppermute | solution.py:567
  77.9 2.1 %collective-permute-start.6 = (bf16[136,256]{1,0:T(8,128)(2,1)S(1)}, bf16[136,256]{1,0:T(8,128)(2,1)S(1)}, u32[]{:S(2)}, u32[]{:S(2)}) collective-permute-start(bf16[136,256]{1,0:T(8,128)(2,1)S(1)} %sum.1.mine_ref), channel_id=1, source_target_pairs={{0,1},{1,0},{2,3},{3,2},{4,5},{5,4},{6,7},{7,6},{8,9},{9,8},{10,11... | collective-permute-start | bytes 208904 | tf_op jit(solution)/shard_map/ppermute | solution.py:562
  80.1 0.9 %grad_dt.1 = f32[16,256]{1,0:T(8,128)} custom-call(f32[7,16,256]{2,1,0:T(8,128)S(1)} %get-tuple-element.59.hv_ref, f32[16,256]{1,0:T(8,128)S(1)} %get-tuple-element.79.enter_ref, f32[16,256]{1,0:T(8,128)S(1)} %get-tuple-element.80.leave_ref, f32[16,128]{1,0:T(8,128)S(1)} %get-tuple-element.81.overlap_ref), custom_call_target="tpu_custom_call" | custom-call | tf_op jit(solution)/shard_map/grad_dt/pallas_call | solution.py:543
  80.9 0.0 collective-permute-done.6.got_ref
  81.0 0.7 last.1
  (3 shorter events, 0.1 us)
Async XLA Ops:
  0.6 0.7 slice-start
  0.6 0.7 slice-start.1
  1.4 4.3 %copy-start = (bf16[4,1024]{1,0:T(4,128)(2,1)S(1)}, bf16[4,1024]{1,0:T(4,128)(2,1)}, u32[]{:S(2)}) copy-start(bf16[4,1024]{1,0:T(4,128)(2,1)} %wx_ref.7) | copy-start | bytes 24580
  1.4 4.3 %copy-start.1 = (f32[16,256]{1,0:T(8,128)S(1)}, f32[16,256]{1,0:T(8,128)}, u32[]{:S(2)}) copy-start(f32[16,256]{1,0:T(8,128)} %dt_ref.2) | copy-start | bytes 49156
  1.4 4.3 %copy-start.2 = (bf16[4,256]{1,0:T(4,128)(2,1)S(1)}, bf16[4,256]{1,0:T(4,128)(2,1)}, u32[]{:S(2)}) copy-start(bf16[4,256]{1,0:T(4,128)(2,1)} %wbc_ref.9) | copy-start | bytes 6148
  1.4 4.3 %copy-start.3 = (f32[16]{0:T(128)S(1)}, f32[16]{0:T(128)}, u32[]{:S(2)}) copy-start(f32[16]{0:T(128)} %a_log_ref.3) | copy-start | bytes 196
  1.4 8.3 %collective-permute-start = (bf16[8,1280]{1,0:T(8,128)(2,1)S(1)}, bf16[8,1280]{1,0:T(8,128)(2,1)S(1)}, u32[]{:S(2)}, u32[]{:S(2)}) collective-permute-start(bf16[8,1280]{1,0:T(8,128)(2,1)S(1)} %pad_maximum_fusion), channel_id=1, source_target_pairs={{0,8},{8,16},{16,24},{24,32},{32,40},{40,48},{48,56},{56,64},{64,7... | collective-permute-start | bytes 61448 | tf_op jit(solution)/shard_map/ppermute | solution.py:557
  38.5 20.7 %all-to-all-start.1 = ((bf16[32,64,128]{2,1,0:T(8,128)(2,1)}), bf16[32,64,128]{2,1,0:T(8,128)(2,1)S(1)}, u32[]{:S(2)}, u32[]{:S(2)}) async-start(bf16[32,64,128]{2,1,0:T(8,128)(2,1)} %scan.1), calls=%async_computation.1 | async-start | bytes 1048576 | tf_op jit(solution)/shard_map/all_to_all | solution.py:658
  44.4 0.7 copy-start.4
  59.7 10.2 %collective-permute-start.1 = (bf16[128,256]{1,0:T(8,128)(2,1)S(1)}, bf16[128,256]{1,0:T(8,128)(2,1)S(1)}, u32[]{:S(2)}, u32[]{:S(2)}) collective-permute-start(bf16[128,256]{1,0:T(8,128)(2,1)S(1)} %get-tuple-element.63), channel_id=1, source_target_pairs={{0,1},{1,0},{2,3},{3,2},{4,5},{5,4},{6,7},{7,6},{8,9},{9,8},{10,11... | collective-permute-start | bytes 196616 | tf_op jit(solution)/shard_map/ppermute | solution.py:562
  63.2 6.6 %collective-permute-start.2 = (bf16[8,1280]{1,0:T(8,128)(2,1)S(1)}, bf16[8,1280]{1,0:T(8,128)(2,1)S(1)}, u32[]{:S(2)}, u32[]{:S(2)}) collective-permute-start(bf16[8,1280]{1,0:T(8,128)(2,1)S(1)} %get-tuple-element.64), channel_id=1, source_target_pairs={{8,0},{16,8},{24,16},{32,24},{40,32},{48,40},{56,48},{64,56},{72,6... | collective-permute-start | bytes 61448 | tf_op jit(solution)/shard_map/ppermute | solution.py:557
  69.9 6.4 %collective-permute-start.3 = (bf16[136,256]{1,0:T(8,128)(2,1)S(1)}, bf16[136,256]{1,0:T(8,128)(2,1)S(1)}, u32[]{:S(2)}, u32[]{:S(2)}) collective-permute-start(bf16[136,256]{1,0:T(8,128)(2,1)S(1)} %join.1.refs_0_), channel_id=1, source_target_pairs={{0,2},{1,3},{2,4},{3,5},{4,6},{5,7},{6,0},{7,1},{8,10},{9,11},{10,... | collective-permute-start | bytes 208904 | tf_op jit(solution)/shard_map/ppermute | solution.py:567
  71.3 5.2 %collective-permute-start.4 = (bf16[136,256]{1,0:T(8,128)(2,1)S(1)}, bf16[136,256]{1,0:T(8,128)(2,1)S(1)}, u32[]{:S(2)}, u32[]{:S(2)}) collective-permute-start(bf16[136,256]{1,0:T(8,128)(2,1)S(1)} %join.1.refs_0_), channel_id=1, source_target_pairs={{0,4},{1,5},{2,6},{3,7},{4,0},{5,1},{6,2},{7,3},{8,12},{9,13},{10,... | collective-permute-start | bytes 208904 | tf_op jit(solution)/shard_map/ppermute | solution.py:567
  73.9 4.0 %collective-permute-start.5 = (bf16[136,256]{1,0:T(8,128)(2,1)S(1)}, bf16[136,256]{1,0:T(8,128)(2,1)S(1)}, u32[]{:S(2)}, u32[]{:S(2)}) collective-permute-start(bf16[136,256]{1,0:T(8,128)(2,1)S(1)} %join.1.refs_0_), channel_id=1, source_target_pairs={{0,6},{1,7},{2,0},{3,1},{4,2},{5,3},{6,4},{7,5},{8,14},{9,15},{10,... | collective-permute-start | bytes 208904 | tf_op jit(solution)/shard_map/ppermute | solution.py:567
  77.9 3.1 %collective-permute-start.6 = (bf16[136,256]{1,0:T(8,128)(2,1)S(1)}, bf16[136,256]{1,0:T(8,128)(2,1)S(1)}, u32[]{:S(2)}, u32[]{:S(2)}) collective-permute-start(bf16[136,256]{1,0:T(8,128)(2,1)S(1)} %sum.1.mine_ref), channel_id=1, source_target_pairs={{0,1},{1,0},{2,3},{3,2},{4,5},{5,4},{6,7},{7,6},{8,9},{9,8},{10,11... | collective-permute-start | bytes 208904 | tf_op jit(solution)/shard_map/ppermute | solution.py:562
